TPU v7x, 32 devices: a whole 2x2x4 slice. The times are simulated.
32 devices in a mesh: leaf: 2 (over x), row: 4 (over z), col: 4 (over y, core).
Axes of the slice: x: 2, y: 2, z: 4, core: 2. Of those that a mesh axis runs over, the one named last changes fastest.
Arguments:
- tokens: bfloat16 [768, 20480], P('col', ('leaf', 'row')), may hold values from -6 to 6
- memory: bfloat16 [128, 768], P('leaf', 'col'), may hold values from -6 to 6
- parents: int32 [80], P('leaf'), may hold values from -1 to 39, as said below
- memory_slots: int32 [80, 20], P('leaf'), may hold values from 0 to 63, as said below
- query_weight: bfloat16 [768, 768], P('col', 'row'), may hold values from -0.21875 to 0.21875
- query_bias: bfloat16 [768], P('row'), may hold values from -3 to 3
- key_weight: bfloat16 [768, 768], P('col', 'row'), may hold values from -0.21875 to 0.21875
- value_weight: bfloat16 [768, 768], P('col', 'row'), may hold values from -0.21875 to 0.21875
- value_bias: bfloat16 [768], P('row'), may hold values from -3 to 3
- out_weight: bfloat16 [768, 768], P('row', 'col'), may hold values from -1.75 to 1.75
- out_bias: bfloat16 [768], P('col'), may hold values from -2 to 2
- norm_gain: bfloat16 [768], P('col'), may hold values from 0.5 to 1.5
- norm_shift: bfloat16 [768], P('col'), may hold values from -2 to 2
- up_weight: bfloat16 [768, 3072], P('col', 'row'), may hold values from -0.21875 to 0.21875
- up_bias: bfloat16 [3072], P('row'), may hold values from -2 to 2
- down_weight: bfloat16 [768, 3072], P('col', 'row'), may hold values from -0.109375 to 0.109375
- down_bias: bfloat16 [768], P('col'), may hold values from -2 to 2
- final_gain: bfloat16 [768], P('col'), may hold values from 0.5 to 1.5
- final_shift: bfloat16 [768], P('col'), may hold values from -2 to 2
- cotangent: bfloat16 [768, 20480], P('col', ('leaf', 'row')), may hold values from -6 to 6
Outputs:
- layer_output: bfloat16 [768, 20480], P('col', ('leaf', 'row'))
- tokens_grad: float32 [768, 20480], P('col', ('leaf', 'row'))
- memory_grad: float32 [128, 768], P('leaf', 'col')
- query_weight_grad: float32 [768, 768], P('col', 'row')
- query_bias_grad: float32 [768], P('row')
- key_weight_grad: float32 [768, 768], P('col', 'row')
- value_weight_grad: float32 [768, 768], P('col', 'row')
- value_bias_grad: float32 [768], P('row')
- out_weight_grad: float32 [768, 768], P('row', 'col')
- out_bias_grad: float32 [768], P('col')
- norm_gain_grad: float32 [768], P('col')
- norm_shift_grad: float32 [768], P('col')
- up_weight_grad: float32 [768, 3072], P('col', 'row')
- up_bias_grad: float32 [3072], P('row')
- down_weight_grad: float32 [768, 3072], P('col', 'row')
- down_bias_grad: float32 [768], P('col')
- final_gain_grad: float32 [768], P('col')
- final_shift_grad: float32 [768], P('col')
Inputs may be any that keep to these rules, and one draw needn't show every extreme that they name: `parents`: segment s of a group of 2 trees belongs to tree s mod 2; each tree has 8 trunk segments in a chain from a root, whose parent is -1, 4 branch segments whose parent is the trunk's last, and 2 leaf segments under each branch; a parent is numbered within the group. `memory_slots`: the memory rows of a segment of tree t lie in rows t * 32 to (t + 1) * 32 - 1 of its group's memory rows, numbered within the group; every memory row is named by some segment.
All inputs are finite; a program needn't handle non-finite values.
Results may differ from a plain program's by a relative error of at most 0.019.
Values may be sent and summed in bfloat16 or wider, within the bound.
No kernel may reach another device: no remote copies, remote signals or barrier semaphores. Data moves between devices by JAX's collectives and lax.ppermute only.
A program may use at most 192 MiB of HBM per device.

v0:
```python
import jax
import jax.numpy as jnp
from jax import lax
from jax.sharding import PartitionSpec as P

D = 768
HEAD = 64
SEG = 256
MEM_SEG = 20


NEGATIVE = -1e30
EPSILON = 1e-05
HIGHEST = lax.Precision.HIGHEST


def gather_rows(local):
    return lax.all_gather(local, "row", axis=0, tiled=True)


def gather_cols(local):
    return lax.all_gather(local, "col", axis=0, tiled=True)


def product_term(gathered, weight):
    return jnp.dot(gathered, weight, preferred_element_type=jnp.float32)


def sum_cols(gathered, weight):
    return lax.psum_scatter(product_term(gathered, weight), "col", scatter_dimension=0, tiled=True)


def sum_rows(gathered, weight):
    return lax.psum_scatter(product_term(gathered, weight), "row", scatter_dimension=0, tiled=True)


def outer(left, right):
    return lax.dot_general(
        left, right, (((0,), (0,)), ((), ())), preferred_element_type=jnp.float32
    )


def column_sums(array):
    return jnp.sum(array, axis=0, dtype=jnp.float32)


def feature_sums(first, second):
    return lax.psum((first, second), "col")


def norm_forward(values, gain, shift):
    totals = feature_sums(jnp.sum(values, axis=1), jnp.sum(values * values, axis=1))
    center = totals[0] / D
    spread = totals[1] / D - center * center
    scale = lax.rsqrt(spread + EPSILON)
    normed = (values - center[:, None]) * scale[:, None]
    return (normed * gain + shift, normed, scale)


def norm_backward(grad_out, normed, scale, gain):
    scaled = grad_out * gain
    totals = feature_sums(jnp.sum(scaled, axis=1), jnp.sum(scaled * normed, axis=1))
    inner = scaled - totals[0][:, None] / D - normed * (totals[1][:, None] / D)
    return (inner * scale[:, None], jnp.sum(grad_out * normed, axis=0), jnp.sum(grad_out, axis=0))


def by_heads(array):
    return array.reshape(array.shape[0], array.shape[1], -1, HEAD).transpose(2, 0, 1, 3)


def from_heads(array):
    return array.transpose(1, 2, 0, 3).reshape(array.shape[1], array.shape[2], -1)


def scores_of(queries, keys, valid):
    raw = jnp.einsum("sqd,skd->sqk", queries, keys, preferred_element_type=jnp.float32)
    return jnp.where(valid[:, None, :], raw * HEAD ** (-0.5), NEGATIVE)


def head_forward(queries, keys, values, valid):
    scores = scores_of(queries, keys, valid)
    top = jnp.max(scores, axis=2, keepdims=True)
    weights = jnp.exp(scores - top)
    total = jnp.sum(weights, axis=2, keepdims=True)
    probs = (weights / total).astype(jnp.bfloat16)
    mixed = jnp.einsum("sqk,skd->sqd", probs, values, preferred_element_type=jnp.float32)
    return (mixed, (top + jnp.log(total))[..., 0])


def head_backward(queries, keys, values, grad_mixed, logsum, valid):
    scores = scores_of(queries, keys, valid)
    probs = jnp.exp(scores - logsum[..., None])
    grad_probs = jnp.einsum("sqd,skd->sqk", grad_mixed, values, preferred_element_type=jnp.float32)
    inner = jnp.sum(probs * grad_probs, axis=2, keepdims=True)
    grad_raw = jnp.where(
        valid[:, None, :], probs * (grad_probs - inner) * HEAD ** (-0.5), 0.0
    ).astype(jnp.bfloat16)
    grad_queries = jnp.einsum("sqk,skd->sqd", grad_raw, keys, preferred_element_type=jnp.float32)
    grad_keys = jnp.einsum("sqk,sqd->skd", grad_raw, queries, preferred_element_type=jnp.float32)
    grad_values = jnp.einsum(
        "sqk,sqd->skd", probs.astype(jnp.bfloat16), grad_mixed, preferred_element_type=jnp.float32
    )
    return (grad_queries, grad_keys, grad_values)


def on_device(
    tokens,
    memory,
    parents,
    memory_slots,
    query_weight,
    query_bias,
    key_weight,
    value_weight,
    value_bias,
    out_weight,
    out_bias,
    norm_gain,
    norm_shift,
    up_weight,
    up_bias,
    down_weight,
    down_bias,
    final_gain,
    final_shift,
    cotangent,
):
    width = query_weight.shape[1]
    row_count = lax.axis_size("row")
    col_count = lax.axis_size("col")
    token_major = tokens.T
    seg_local = parents.shape[0] // col_count
    first_seg = lax.axis_index("col") * seg_local
    own_parents = lax.dynamic_slice_in_dim(parents, first_seg, seg_local, 0)
    own_slots = lax.dynamic_slice_in_dim(memory_slots, first_seg, seg_local, 0)
    safe_parent = jnp.maximum(own_parents, 0)
    valid = jnp.concatenate(
        [
            jnp.ones((seg_local, MEM_SEG), bool),
            jnp.broadcast_to((own_parents >= 0)[:, None], (seg_local, SEG)),
            jnp.ones((seg_local, SEG), bool),
        ],
        axis=1,
    )
    group_tokens = token_major.shape[0] * row_count
    own_tokens = group_tokens // col_count
    bank_rows = memory.shape[0]
    bank_local = bank_rows // col_count
    ext_rows = own_tokens + bank_local

    def extend(group_part, bank_part):
        return jnp.concatenate(
            [
                group_part.reshape(col_count, own_tokens, -1),
                bank_part.reshape(col_count, bank_local, -1),
            ],
            axis=1,
        ).reshape(-1, group_part.shape[1])

    def split_bank(gathered):
        shaped = gathered.reshape(col_count, ext_rows, -1)
        return (
            shaped[:, :own_tokens].reshape(group_tokens, -1),
            shaped[:, own_tokens:].reshape(bank_rows, -1),
        )

    joint_weight = jnp.concatenate([query_weight, key_weight, value_weight], axis=1)
    token_rows = gather_rows(token_major)
    extended = extend(token_rows, memory)
    projected = sum_cols(extended, joint_weight)
    queries = (projected[:own_tokens, :width] + query_bias.astype(jnp.float32)).astype(jnp.bfloat16)
    keys_ext = projected[:, width : 2 * width].astype(jnp.bfloat16)
    values_ext = (projected[:, 2 * width :] + value_bias.astype(jnp.float32)).astype(jnp.bfloat16)
    key_gathered, value_gathered = (
        lax.all_gather(keys_ext, "col", axis=0, tiled=True),
        lax.all_gather(values_ext, "col", axis=0, tiled=True),
    )
    key_all, memory_keys = split_bank(key_gathered)
    value_all, memory_values = split_bank(value_gathered)
    keys = keys_ext[:own_tokens]
    values = values_ext[:own_tokens]

    def assemble(own, gathered, memory_rows):
        own_seg = own.reshape(seg_local, SEG, width)
        group_seg = gathered.reshape(-1, SEG, width)
        return by_heads(
            jnp.concatenate([memory_rows[own_slots], group_seg[safe_parent], own_seg], axis=1)
        )

    key_heads = assemble(keys, key_all, memory_keys)
    value_heads = assemble(values, value_all, memory_values)
    query_heads = by_heads(queries.reshape(seg_local, SEG, width))
    mixed, logsum = lax.map(
        lambda group: head_forward(group[0], group[1], group[2], valid),
        (query_heads, key_heads, value_heads),
    )
    context = from_heads(mixed).reshape(-1, width).astype(jnp.bfloat16)
    context_rows = gather_cols(context)
    attended = (
        sum_rows(context_rows, out_weight)
        + out_bias.astype(jnp.float32)
        + token_major.astype(jnp.float32)
    )
    grad_rows = cotangent.T.astype(jnp.float32)
    gain_first = norm_gain.astype(jnp.float32)
    gain_last = final_gain.astype(jnp.float32)
    hidden, first_normed, first_scale = norm_forward(
        attended, gain_first, norm_shift.astype(jnp.float32)
    )
    hidden_low = hidden.astype(jnp.bfloat16)
    hidden_rows = gather_rows(hidden_low)
    upper = sum_cols(hidden_rows, up_weight) + up_bias.astype(jnp.float32)
    active = jax.nn.gelu(upper, approximate=False).astype(jnp.bfloat16)
    active_rows = gather_cols(active)
    second = sum_rows(active_rows, down_weight.T) + down_bias.astype(jnp.float32) + hidden
    result, second_normed, second_scale = norm_forward(
        second, gain_last, final_shift.astype(jnp.float32)
    )
    second_grad, final_gain_grad, final_shift_grad = norm_backward(
        grad_rows, second_normed, second_scale, gain_last
    )
    second_rows = gather_rows(second_grad.astype(jnp.bfloat16))
    active_grad = sum_cols(second_rows, down_weight)
    down_weight_grad = outer(second_rows, active_rows)
    down_bias_grad = column_sums(second_rows)
    unused_value, gelu_pull = jax.vjp(lambda value: jax.nn.gelu(value, approximate=False), upper)
    upper_low = gelu_pull(active_grad)[0].astype(jnp.bfloat16)
    upper_rows = gather_cols(upper_low)
    hidden_grad = sum_rows(upper_rows, up_weight.T) + second_grad
    up_weight_grad = outer(hidden_rows, upper_rows)
    up_bias_grad = column_sums(upper_rows)
    first_grad, norm_gain_grad, norm_shift_grad = norm_backward(
        hidden_grad, first_normed, first_scale, gain_first
    )
    first_rows = gather_rows(first_grad.astype(jnp.bfloat16))
    context_grad = sum_cols(first_rows, out_weight.T).astype(jnp.bfloat16)
    out_weight_grad = outer(context_rows, first_rows)
    out_bias_grad = column_sums(first_rows)
    grad_heads = by_heads(context_grad.reshape(seg_local, SEG, width))
    query_parts, key_parts, value_parts = lax.map(
        lambda group: head_backward(group[0], group[1], group[2], group[3], group[4], valid),
        (query_heads, key_heads, value_heads, grad_heads, logsum),
    )
    query_grad = from_heads(query_parts).reshape(-1, width).astype(jnp.bfloat16)
    segment_ids = jnp.arange(parents.shape[0], dtype=jnp.int32)[:, None]
    parent_table = (segment_ids == own_parents[None, :]).astype(jnp.float32)
    own_table = (
        segment_ids == (first_seg + jnp.arange(seg_local, dtype=jnp.int32))[None, :]
    ).astype(jnp.float32)
    slot_table = (
        jnp.arange(bank_rows, dtype=jnp.int32)[:, None] == own_slots.reshape(-1)[None, :]
    ).astype(jnp.float32)

    def spread(parts):
        memory_piece = parts[:, :MEM_SEG].reshape(-1, width)
        parent_piece = parts[:, MEM_SEG : MEM_SEG + SEG].reshape(seg_local, -1)
        own_piece = parts[:, MEM_SEG + SEG :].reshape(seg_local, -1)
        group_piece = jnp.dot(
            parent_table, parent_piece, precision=HIGHEST, preferred_element_type=jnp.float32
        ) + jnp.dot(own_table, own_piece, precision=HIGHEST, preferred_element_type=jnp.float32)
        memory_sum = jnp.dot(
            slot_table, memory_piece, precision=HIGHEST, preferred_element_type=jnp.float32
        )
        return extend(group_piece.reshape(-1, width), memory_sum)

    key_grad_ext, value_grad_ext = (
        lax.psum_scatter(
            spread(from_heads(key_parts)).astype(jnp.bfloat16),
            "col",
            scatter_dimension=0,
            tiled=True,
        ).astype(jnp.float32),
        lax.psum_scatter(
            spread(from_heads(value_parts)).astype(jnp.bfloat16),
            "col",
            scatter_dimension=0,
            tiled=True,
        ).astype(jnp.float32),
    )
    query_ext = jnp.concatenate([query_grad, jnp.zeros((bank_local, width), jnp.bfloat16)], axis=0)
    joint_grad = jnp.concatenate(
        [query_ext, key_grad_ext.astype(jnp.bfloat16), value_grad_ext.astype(jnp.bfloat16)], axis=1
    )
    joint_rows = gather_cols(joint_grad)
    token_joint, bank_joint = split_bank(joint_rows)
    tokens_grad = sum_rows(token_joint, joint_weight.T) + first_grad
    joint_weight_grad = outer(extended, joint_rows)
    bias_sums = column_sums(joint_rows)
    query_weight_grad = joint_weight_grad[:, :width]
    key_weight_grad = joint_weight_grad[:, width : 2 * width]
    value_weight_grad = joint_weight_grad[:, 2 * width :]
    query_bias_grad = bias_sums[:width]
    value_bias_grad = bias_sums[2 * width :]
    memory_grad = lax.psum(
        jnp.dot(
            bank_joint[:, width:], joint_weight[:, width:].T, preferred_element_type=jnp.float32
        ).astype(jnp.bfloat16),
        "row",
    ).astype(jnp.float32)
    summed = (
        lax.psum(query_weight_grad.astype(jnp.bfloat16), "leaf").astype(jnp.float32),
        lax.psum(query_bias_grad.astype(jnp.bfloat16), "leaf").astype(jnp.float32),
        lax.psum(key_weight_grad.astype(jnp.bfloat16), "leaf").astype(jnp.float32),
        lax.psum(value_weight_grad.astype(jnp.bfloat16), "leaf").astype(jnp.float32),
        lax.psum(value_bias_grad.astype(jnp.bfloat16), "leaf").astype(jnp.float32),
        lax.psum(out_weight_grad.astype(jnp.bfloat16), "leaf").astype(jnp.float32),
        lax.psum(out_bias_grad.astype(jnp.bfloat16), "leaf").astype(jnp.float32),
        lax.psum(up_weight_grad.astype(jnp.bfloat16), "leaf").astype(jnp.float32),
        lax.psum(up_bias_grad.astype(jnp.bfloat16), "leaf").astype(jnp.float32),
        lax.psum(down_weight_grad.astype(jnp.bfloat16), "leaf").astype(jnp.float32),
        lax.psum(down_bias_grad.astype(jnp.bfloat16), "leaf").astype(jnp.float32),
    )
    gains = lax.psum(
        (norm_gain_grad, norm_shift_grad, final_gain_grad, final_shift_grad), ("leaf", "row")
    )
    return (
        result.astype(jnp.bfloat16).T,
        tokens_grad.T,
        memory_grad,
        summed[0],
        summed[1],
        summed[2],
        summed[3],
        summed[4],
        summed[5],
        summed[6],
        gains[0],
        gains[1],
        summed[7],
        summed[8],
        summed[9],
        summed[10],
        gains[2],
        gains[3],
    )


def solution(mesh):
    return jax.shard_map(
        on_device,
        mesh=mesh,
        in_specs=(
            P("col", ("leaf", "row")),
            P("leaf", "col"),
            P("leaf"),
            P("leaf", None),
            P("col", "row"),
            P("row"),
            P("col", "row"),
            P("col", "row"),
            P("row"),
            P("row", "col"),
            P("col"),
            P("col"),
            P("col"),
            P("col", "row"),
            P("row"),
            P("col", "row"),
            P("col"),
            P("col"),
            P("col"),
            P("col", ("leaf", "row")),
        ),
        out_specs=(
            P("col", ("leaf", "row")),
            P("col", ("leaf", "row")),
            P("leaf", "col"),
            P("col", "row"),
            P("row"),
            P("col", "row"),
            P("col", "row"),
            P("row"),
            P("row", "col"),
            P("col"),
            P("col"),
            P("col"),
            P("col", "row"),
            P("row"),
            P("col", "row"),
            P("col"),
            P("col"),
            P("col"),
        ),
        check_vma=False,
    )
```

profile of v0, /device:TPU:0, one launch (start us, length us, event | category | flops | bytes accessed | tf_op | source)
XLA Modules:
  0.0 2610.1 jit_solution(2856966699295913915)
XLA Ops:
  8.9 79.9 %all-gather.14.cloned.1.call-done = bf16[10240,192]{0,1:T(8,128)(2,1)} async-done(((bf16[2560,192]{0,1:T(8,128)(2,1)}), bf16[10240,192]{0,1:T(8,128)(2,1)}) %all-gather.14.cloned.1.call-update) | async-done | bytes 3932176 | tf_op jit(solution)/shard_map/all_gather | solution.py:18
  108.6 15.3 fusion.129
  124.5 192.8 %reduce-scatter.31.cloned.1.call-done = f32[2576,576]{1,0:T(8,128)} async-done(((f32[10304,576]{1,0:T(8,128)}), f32[2576,576]{1,0:T(8,128)}) %reduce-scatter.31.cloned.1.call-update) | async-done | bytes 5935120
  346.7 15.8 all-gather.30.cloned.1.call-done
  426.2 29.4 %while.26 = (s32[]{:T(128)}, bf16[3,10,256,64]{2,3,1,0:T(8,128)(2,1)}, f32[3,10,256]{2,1,0:T(8,128)S(1)}, pred[10,532]{1,0:T(8,128)(4,1)S(1)}, bf16[3,10,256,64]...) while((s32[]{:T(128)}, ...), condition=%wide.region_4.5_spmd, body=%wide.region_1.4_spmd.sunk | while | flops 364992000 | bytes 27010400 | solution.py:193
  459.6 33.1 %all-gather.16.cloned.1.call-done = bf16[10240,192]{0,1:T(8,128)(2,1)} async-done(((bf16[2560,192]{0,1:T(8,128)(2,1)}), bf16[10240,192]{0,1:T(8,128)(2,1)}) %all-gather.16.cloned.1.call-update) | async-done | bytes 3932176 | tf_op jit(solution)/shard_map/all_gather | solution.py:22
  499.8 135.8 %reduce-scatter.17.cloned.1.call-done = f32[2560,192]{0,1:T(8,128)} async-done(((f32[10240,192]{0,1:T(8,128)}), f32[2560,192]{0,1:T(8,128)}) %reduce-scatter.17.cloned.1.call-update) | async-done | bytes 1966096 | tf_op jit(solution)/shard_map/reduce_scatter | solution.py:34
  650.3 76.1 %all-gather.18.cloned.1.call-done = bf16[10240,192]{0,1:T(8,128)(2,1)} async-done(((bf16[2560,192]{0,1:T(8,128)(2,1)}), bf16[10240,192]{0,1:T(8,128)(2,1)}) %all-gather.18.cloned.1.call-update) | async-done | bytes 3932176 | tf_op jit(solution)/shard_map/all_gather | solution.py:18
  726.5 16.9 fusion.154
  744.0 219.6 %reduce-scatter.19.cloned.1.call-done = f32[2560,768]{1,0:T(8,128)} async-done(((f32[10240,768]{1,0:T(8,128)}), f32[2560,768]{1,0:T(8,128)}) %reduce-scatter.19.cloned.1.call-update) | async-done | bytes 7864336 | tf_op jit(solution)/shard_map/reduce_scatter | solution.py:30
  963.7 19.5 multiply_convert_fusion
  983.4 99.9 %all-gather.20.cloned.1.call-done = bf16[10240,768]{1,0:T(8,128)(2,1)} async-done(((bf16[2560,768]{1,0:T(8,128)(2,1)}), bf16[10240,768]{1,0:T(8,128)(2,1)}) %all-gather.20.cloned.1.call-update) | async-done | bytes 15728656 | tf_op jit(solution)/shard_map/all_gather | solution.py:22
  1083.3 13.7 fusion.155
  1097.8 135.7 %reduce-scatter.21.cloned.1.call-done = f32[2560,192]{0,1:T(8,128)} async-done(((f32[10240,192]{0,1:T(8,128)}), f32[2560,192]{0,1:T(8,128)}) %reduce-scatter.21.cloned.1.call-update) | async-done | bytes 1966096 | tf_op jit(solution)/shard_map/reduce_scatter | solution.py:34
  1265.6 76.2 %all-gather.22.cloned.1.call-done = bf16[10240,192]{0,1:T(8,128)(2,1)} async-done(((bf16[2560,192]{0,1:T(8,128)(2,1)}), bf16[10240,192]{0,1:T(8,128)(2,1)}) %all-gather.22.cloned.1.call-update) | async-done | bytes 3932176 | tf_op jit(solution)/shard_map/all_gather | solution.py:18
  1341.7 14.0 fusion.156
  1355.8 220.2 %reduce-scatter.23.cloned.1.call-done = f32[2560,768]{1,0:T(8,128)} async-done(((f32[10240,768]{1,0:T(8,128)}), f32[2560,768]{1,0:T(8,128)}) %reduce-scatter.23.cloned.1.call-update) | async-done | bytes 7864336 | tf_op jit(solution)/shard_map/reduce_scatter | solution.py:30
  1588.0 99.9 %all-gather.24.cloned.1.call-done = bf16[10240,768]{1,0:T(8,128)(2,1)} async-done(((bf16[2560,768]{1,0:T(8,128)(2,1)}), bf16[10240,768]{1,0:T(8,128)(2,1)}) %all-gather.24.cloned.1.call-update) | async-done | bytes 15728656 | tf_op jit(solution)/shard_map/all_gather | solution.py:22
  1687.9 13.8 fusion.157
  1702.3 135.8 %reduce-scatter.25.cloned.1.call-done = f32[2560,192]{0,1:T(8,128)} async-done(((f32[10240,192]{0,1:T(8,128)}), f32[2560,192]{0,1:T(8,128)}) %reduce-scatter.25.cloned.1.call-update) | async-done | bytes 1966096 | tf_op jit(solution)/shard_map/reduce_scatter | solution.py:34
  1858.7 76.1 %all-gather.26.cloned.1.call-done = bf16[10240,192]{0,1:T(8,128)(2,1)} async-done(((bf16[2560,192]{0,1:T(8,128)(2,1)}), bf16[10240,192]{0,1:T(8,128)(2,1)}) %all-gather.26.cloned.1.call-update) | async-done | bytes 3932176 | tf_op jit(solution)/shard_map/all_gather | solution.py:18
  1942.1 66.8 %reduce-scatter.27.cloned.1.call-done = f32[2560,192]{0,1:T(8,128)} async-done(((f32[10240,192]{0,1:T(8,128)}), f32[2560,192]{0,1:T(8,128)}) %reduce-scatter.27.cloned.1.call-update) | async-done | bytes 1966096 | tf_op jit(solution)/shard_map/reduce_scatter | solution.py:30
  2018.4 106.3 %while.27 = (s32[]{:T(128)}, bf16[3,10,256,64]{2,3,1,0:T(8,128)(2,1)}, f32[3,10,532,64]{2,3,0,1:T(8,128)}, f32[3,10,532,64]{2,3,0,1:T(8,128)}, pred[10,532]{1,0:...) while((s32[]{:T(128)}, ...), condition=%wide.region_29.30_spmd, body=%wide.region_27.29_spmd.sunk | while | flops 909768704 | bytes 93875376 | solution.py:240
  2042.1 11.7 bitcast_dynamic-update-slice_fusion.7
  2113.0 11.7 bitcast_dynamic-update-slice_fusion.7
  2224.5 52.2 %reduce-scatter.33.cloned.1.call-done = bf16[2576,192]{1,0:T(8,128)(2,1)} async-done(((bf16[10304,192]{1,0:T(8,128)(2,1)}), bf16[2576,192]{1,0:T(8,128)(2,1)}) %reduce-scatter.33.cloned.1.call-update) | async-done | bytes 989200
  2306.9 58.1 %all-gather.32.cloned.1.call-done = bf16[4,2576,576]{1,2,0:T(8,128)(2,1)} async-done(((bf16[1,2576,576]{1,2,0:T(8,128)(2,1)}), bf16[4,2576,576]{1,2,0:T(8,128)(2,1)}) %all-gather.32.cloned.1.call-update) | async-done | bytes 11870224 | tf_op jit(solution)/shard_map/all_gather | solution.py:22
  2365.0 24.9 copy.152
  2389.9 18.8 reshape.258
  2445.6 22.3 all-reduce.1
  2486.2 16.9 psum.176
  2513.8 85.2 %reduce-scatter.29.cloned.1.call-done = f32[2560,192]{0,1:T(8,128)} async-done(((f32[10240,192]{0,1:T(8,128)}), f32[2560,192]{0,1:T(8,128)}) %reduce-scatter.29.cloned.1.call-update) | async-done | bytes 1966096 | tf_op jit(solution)/shard_map/reduce_scatter | solution.py:34
  (361 shorter events, 535.3 us)
Async XLA Ops:
  7.2 1076.2 %copy-start = (bf16[192,768]{1,0:T(8,128)(2,1)S(1)}, bf16[192,768]{1,0:T(8,128)(2,1)}, u32[]{:S(2)}) copy-start(bf16[192,768]{1,0:T(8,128)(2,1)} %param.39) | copy-start | bytes 884740
  7.2 81.6 %all-gather.14.cloned.1.call-start = ((), (), s32[]{:S(2)}) async-start(), calls=%async_computation.10 | async-start | bytes 4915200 | tf_op jit(solution)/shard_map/all_gather | solution.py:18
  7.9 309.4 %reduce-scatter.31.cloned.1.call-start = ((), (), s32[]{:S(2)}) async-start(), calls=%async_computation.27 | async-start | bytes 32972800
  123.9 238.6 %all-gather.30.cloned.1.call-start = ((), (), s32[]{:S(2)}) async-start(), calls=%async_computation.25 | async-start | bytes 5160960 | tf_op jit(solution)/shard_map/all_gather | solution.py:176
  328.3 70.5 %all-gather.28.cloned.1.call-start = ((), (), s32[]{:S(2)}) async-start(), calls=%async_computation.24 | async-start | bytes 5160960 | tf_op jit(solution)/shard_map/all_gather | solution.py:175
  332.5 160.2 %all-gather.16.cloned.1.call-start = ((), (), s32[]{:S(2)}) async-start(), calls=%async_computation.11 | async-start | bytes 4915200 | tf_op jit(solution)/shard_map/all_gather | solution.py:22
  459.5 176.0 %reduce-scatter.17.cloned.1.call-start = ((), (), s32[]{:S(2)}) async-start(), calls=%async_computation.12 | async-start | bytes 9830400 | tf_op jit(solution)/shard_map/reduce_scatter | solution.py:34
  499.1 136.4 %copy-start.13 = (bf16[192,2560]{1,0:T(8,128)(2,1)S(1)}, bf16[192,2560]{1,0:T(8,128)(2,1)}, u32[]{:S(2)}) copy-start(bf16[192,2560]{1,0:T(8,128)(2,1)} %param.24) | copy-start | bytes 2949124
  499.1 227.3 %all-gather.18.cloned.1.call-start = ((), (), s32[]{:S(2)}) async-start(), calls=%async_computation.13 | async-start | bytes 4915200 | tf_op jit(solution)/shard_map/all_gather | solution.py:18
  499.8 1355.8 %copy-start.37 = (f32[192]{0:T(256)}, f32[192]{0:T(256)S(1)}, u32[]{:S(2)}) copy-start(f32[192]{0:T(256)S(1)} %convert_element_type.177) | copy-start | bytes 2308
  637.6 1218.0 %copy-start.3 = (f32[2560,192]{0,1:T(8,128)}, f32[2560,192]{0,1:T(8,128)S(1)}, u32[]{:S(2)}) copy-start(f32[2560,192]{0,1:T(8,128)S(1)} %get-tuple-element.238) | copy-start | bytes 5898244
  648.9 1206.6 %copy-start.22 = (f32[2560]{0:T(1024)}, f32[2560]{0:T(1024)S(1)}, u32[]{:S(2)}) copy-start(f32[2560]{0:T(1024)S(1)} %get-tuple-element.255) | copy-start | bytes 30724
  648.9 1206.7 %copy-start.24 = (f32[2560]{0:T(1024)}, f32[2560]{0:T(1024)S(1)}, u32[]{:S(2)}) copy-start(f32[2560]{0:T(1024)S(1)} %get-tuple-element.256) | copy-start | bytes 30724
  650.3 313.4 %reduce-scatter.19.cloned.1.call-start = ((), (), s32[]{:S(2)}) async-start(), calls=%async_computation.14 | async-start | bytes 39321600 | tf_op jit(solution)/shard_map/reduce_scatter | solution.py:30
  743.4 340.0 %all-gather.20.cloned.1.call-start = ((), (), s32[]{:S(2)}) async-start(), calls=%async_computation.15 | async-start | bytes 19660800 | tf_op jit(solution)/shard_map/all_gather | solution.py:22
  983.2 250.3 %reduce-scatter.21.cloned.1.call-start = ((), (), s32[]{:S(2)}) async-start(), calls=%async_computation.16 | async-start | bytes 9830400 | tf_op jit(solution)/shard_map/reduce_scatter | solution.py:34
  1097.1 151.4 %copy-start.8 = (bf16[192,2560]{1,0:T(8,128)(2,1)S(1)}, bf16[192,2560]{1,0:T(8,128)(2,1)}, u32[]{:S(2)}) copy-start(bf16[192,2560]{1,0:T(8,128)(2,1)} %param.43) | copy-start | bytes 2949124
  1097.1 244.6 %all-gather.22.cloned.1.call-start = ((), (), s32[]{:S(2)}) async-start(), calls=%async_computation.17 | async-start | bytes 4915200 | tf_op jit(solution)/shard_map/all_gather | solution.py:18
  1265.5 310.5 %reduce-scatter.23.cloned.1.call-start = ((), (), s32[]{:S(2)}) async-start(), calls=%async_computation.18 | async-start | bytes 39321600 | tf_op jit(solution)/shard_map/reduce_scatter | solution.py:30
  1355.8 332.1 %all-gather.24.cloned.1.call-start = ((), (), s32[]{:S(2)}) async-start(), calls=%async_computation.19 | async-start | bytes 19660800 | tf_op jit(solution)/shard_map/all_gather | solution.py:22
  1587.7 250.3 %reduce-scatter.25.cloned.1.call-start = ((), (), s32[]{:S(2)}) async-start(), calls=%async_computation.20 | async-start | bytes 9830400 | tf_op jit(solution)/shard_map/reduce_scatter | solution.py:34
  1701.7 233.1 %all-gather.26.cloned.1.call-start = ((), (), s32[]{:S(2)}) async-start(), calls=%async_computation.21 | async-start | bytes 4915200 | tf_op jit(solution)/shard_map/all_gather | solution.py:18
  1858.6 150.3 %reduce-scatter.27.cloned.1.call-start = ((), (), s32[]{:S(2)}) async-start(), calls=%async_computation.22 | async-start | bytes 9830400 | tf_op jit(solution)/shard_map/reduce_scatter | solution.py:30
  1941.3 281.2 %reduce-scatter.35.cloned.1.call-start = ((), (), s32[]{:S(2)}) async-start(), calls=%async_computation.29 | async-start | bytes 6594560
  2170.7 106.0 %reduce-scatter.33.cloned.1.call-start = ((), (), s32[]{:S(2)}) async-start(), calls=%async_computation.28 | async-start | bytes 6594560
  2217.0 148.0 %all-gather.32.cloned.1.call-start = ((), (), s32[]{:S(2)}) async-start(), calls=%async_computation.26 | async-start | bytes 15482880 | tf_op jit(solution)/shard_map/all_gather | solution.py:22
  2283.8 219.9 %all-reduce.10.cloned.1.call-start = ((), (), s32[]{:S(2)}) async-start(), calls=%async_computation.30 | async-start | bytes 1966080 | tf_op jit(solution)/shard_map/psum | solution.py:301
  2419.3 179.6 %reduce-scatter.29.cloned.1.call-start = ((), (), s32[]{:S(2)}) async-start(), calls=%async_computation.23 | async-start | bytes 9830400 | tf_op jit(solution)/shard_map/reduce_scatter | solution.py:34
  2477.7 121.2 %copy-start.4 = (f32[2560,192]{0,1:T(8,128)S(1)}, f32[2560,192]{0,1:T(8,128)}, u32[]{:S(2)}) copy-start(f32[2560,192]{0,1:T(8,128)} %copy-done.3) | copy-start | bytes 5898244
  2477.7 121.2 %copy-start.23 = (f32[2560]{0:T(1024)S(1)}, f32[2560]{0:T(1024)}, u32[]{:S(2)}) copy-start(f32[2560]{0:T(1024)} %copy-done.22) | copy-start | bytes 30724
  2477.7 121.2 %copy-start.25 = (f32[2560]{0:T(1024)S(1)}, f32[2560]{0:T(1024)}, u32[]{:S(2)}) copy-start(f32[2560]{0:T(1024)} %copy-done.24) | copy-start | bytes 30724
  2477.7 121.2 %copy-start.33 = (f32[2560]{0:T(1024)S(1)}, f32[2560]{0:T(1024)}, u32[]{:S(2)}) copy-start(f32[2560]{0:T(1024)} %copy-done.32) | copy-start | bytes 30724
  (55 other events, 976.7 us)
Sparse Core Ops, SparseCore 0:
  9.6 79.1 all-gather.13
  124.0 193.2 reduce-scatter.30
  328.4 34.1 all-gather.29
  364.6 34.1 all-gather.27
  459.7 32.9 all-gather.15
  499.3 136.2 reduce-scatter.16
  650.4 76.0 all-gather.17
  743.5 220.1 reduce-scatter.18
  983.3 99.9 all-gather.19
  1097.2 136.2 reduce-scatter.20
  1265.6 76.0 all-gather.21
  1355.9 220.1 reduce-scatter.22
  1587.8 99.9 all-gather.23
  1701.8 136.2 reduce-scatter.24
  1858.7 76.0 all-gather.25
  1941.4 67.5 reduce-scatter.26
  2170.8 51.6 reduce-scatter.34
  2225.0 51.5 reduce-scatter.32
  2283.9 80.9 all-gather.31
  2419.5 39.5 all-reduce.9
  2461.5 137.3 reduce-scatter.28
where the time goes:
time: 2620 us; the launch traced here: 2610 us
  waiting for transfers between devices  1870 us (71%)
  matrix products  265 us (10%)
  local copies, waits for them, and re-layouts  230 us (9%)
  other arithmetic  139 us (5%)
  blocking collectives  88.5 us (3%)
    reduce_scatter x3, waiting for transfers between devices, sum_cols(): lax.psum_scatter(product_term(gathered, weight), 'col', scatter_dimension...  507 us
    reduce_scatter x4, waiting for transfers between devices, sum_rows(): lax.psum_scatter(product_term(gathered, weight), 'row', scatter_dimension...  492 us
    all_gather x4, waiting for transfers between devices, gather_rows(): return lax.all_gather(local, 'row', axis=0, tiled=True)  308 us
    all_gather x4, waiting for transfers between devices, gather_cols(): return lax.all_gather(local, 'col', axis=0, tiled=True)  291 us
    unnamed x24, waiting for transfers between devices  249 us
    dot_general x7, matrix products, product_term(): return jnp.dot(gathered, weight, preferred_element_type=jnp.float32)  76.7 us
  transfers between devices with their start and end apart: 21, of which 20 were waited for; matrix products, arithmetic and copies ran while one was open for 6% of the time, Pallas kernels for 0%

commit v1 on v0

v1 whole, which is shorter than its diff:
```python
import functools

import jax
import jax.numpy as jnp
import numpy as np
from jax import lax
from jax.experimental import pallas as pl
from jax.experimental.pallas import tpu as pltpu
from jax.sharding import PartitionSpec as P

HEAD = 64
SEG = 256
NEGATIVE = -1e30
EPSILON = 1e-05
GROUP = ("row", "col")
EVERY = ("leaf", "row", "col")
BF16 = jnp.bfloat16
F32 = jnp.float32


def tn(left, right):
    return lax.dot_general(left, right, (((0,), (0,)), ((), ())), preferred_element_type=F32)


def nt(left, right):
    return lax.dot_general(left, right, (((1,), (1,)), ((), ())), preferred_element_type=F32)


def nn(left, right):
    return lax.dot_general(left, right, (((1,), (0,)), ((), ())), preferred_element_type=F32)


def plan_windows(own, count):
    segments, ranges = [], []
    for index in range(count):
        first, last = index * own, (index + 1) * own
        whole = [s for s in range(first // SEG, -(-last // SEG)) if s * SEG >= first and (s + 1) * SEG <= last]
        cut = [s for s in range(first // SEG, -(-last // SEG)) if s not in whole]
        pieces = [(s * SEG, SEG) for s in whole]
        for s in cut:
            low, high = max(first, s * SEG), min(last, (s + 1) * SEG)
            pieces.append((low, high - low))
            if low > s * SEG:
                pieces.append((s * SEG, low - s * SEG))
            if high < (s + 1) * SEG:
                pieces.append((high, (s + 1) * SEG - high))
        segments.append(whole + cut)
        ranges.append(pieces)
    return segments, ranges


def attention_forward(head_count, lengths, bank, bias_ref, win_ref, par_ref, slot_ref, ctx_ref, lse_ref):
    width = head_count * HEAD
    window = len(lengths) * SEG
    for head in range(head_count):
        low = head * HEAD
        key_mem = win_ref[0, width + low : width + low + HEAD, window : window + bank]
        value_mem = win_ref[0, 2 * width + low : 2 * width + low + HEAD, window : window + bank]
        for j, count in enumerate(lengths):
            cols = slice(j * SEG, (j + 1) * SEG)
            query = win_ref[0, low : low + HEAD, j * SEG : j * SEG + count]
            own = tn(win_ref[0, width + low : width + low + HEAD, cols], query)
            par = tn(par_ref[0, low : low + HEAD, cols], query) + bias_ref[j]
            mem = tn(key_mem, query) + slot_ref[:, j : j + 1]
            top = jnp.maximum(
                jnp.maximum(jnp.max(own, axis=0, keepdims=True), jnp.max(par, axis=0, keepdims=True)),
                jnp.max(mem, axis=0, keepdims=True),
            )
            own, par, mem = jnp.exp(own - top), jnp.exp(par - top), jnp.exp(mem - top)
            total = (
                jnp.sum(own, axis=0, keepdims=True)
                + jnp.sum(par, axis=0, keepdims=True)
                + jnp.sum(mem, axis=0, keepdims=True)
            )
            mixed = (
                nn(win_ref[0, 2 * width + low : 2 * width + low + HEAD, cols], own.astype(BF16))
                + nn(par_ref[0, width + low : width + low + HEAD, cols], par.astype(BF16))
                + nn(value_mem, mem.astype(BF16))
            )
            ctx_ref[0, low : low + HEAD, j * SEG : j * SEG + count] = (mixed / total).astype(BF16)
            lse_ref[0, head : head + 1, j * SEG : j * SEG + count] = top + jnp.log(total)


def attention_backward(
    head_count, lengths, bank, bias_ref, win_ref, par_ref, slot_ref, dctx_ref, lse_ref, dwin_ref, dpar_ref
):
    width = head_count * HEAD
    window = len(lengths) * SEG
    tail = win_ref.shape[2] - window
    for head in range(head_count):
        low = head * HEAD
        qs, ks, vs = (slice(part * width + low, part * width + low + HEAD) for part in range(3))
        key_mem = win_ref[0, ks, window : window + bank]
        value_mem = win_ref[0, vs, window : window + bank]
        dkey_mem = jnp.zeros((HEAD, bank), F32)
        dvalue_mem = jnp.zeros((HEAD, bank), F32)
        for j, count in enumerate(lengths):
            cols = slice(j * SEG, (j + 1) * SEG)
            tok = slice(j * SEG, j * SEG + count)
            query = win_ref[0, qs, tok]
            dctx = dctx_ref[0, low : low + HEAD, tok]
            lse = lse_ref[0, head : head + 1, tok]
            key_own, value_own = win_ref[0, ks, cols], win_ref[0, vs, cols]
            key_par, value_par = par_ref[0, low : low + HEAD, cols], par_ref[0, width + low : width + low + HEAD, cols]
            own = jnp.exp(tn(key_own, query) - lse)
            par = jnp.exp(tn(key_par, query) + bias_ref[j] - lse)
            mem = jnp.exp(tn(key_mem, query) + slot_ref[:, j : j + 1] - lse)
            gown, gpar, gmem = tn(value_own, dctx), tn(value_par, dctx), tn(value_mem, dctx)
            inner = (
                jnp.sum(own * gown, axis=0, keepdims=True)
                + jnp.sum(par * gpar, axis=0, keepdims=True)
                + jnp.sum(mem * gmem, axis=0, keepdims=True)
            )
            gown = (own * (gown - inner)).astype(BF16)
            gpar = (par * (gpar - inner)).astype(BF16)
            gmem = (mem * (gmem - inner)).astype(BF16)
            dquery = nn(key_own, gown) + nn(key_par, gpar) + nn(key_mem, gmem)
            dwin_ref[0, qs, tok] = (dquery * HEAD ** (-0.5)).astype(BF16)
            if count < SEG:
                dwin_ref[0, qs, j * SEG + count : (j + 1) * SEG] = jnp.zeros((HEAD, SEG - count), BF16)
            dwin_ref[0, ks, cols] = nt(query, gown).astype(BF16)
            dwin_ref[0, vs, cols] = nt(dctx, own.astype(BF16)).astype(BF16)
            dpar_ref[0, low : low + HEAD, cols] = nt(query, gpar).astype(BF16)
            dpar_ref[0, width + low : width + low + HEAD, cols] = nt(dctx, par.astype(BF16)).astype(BF16)
            dkey_mem += nt(query, gmem)
            dvalue_mem += nt(dctx, mem.astype(BF16))
        pad = jnp.zeros((HEAD, tail - bank), F32)
        dwin_ref[0, qs, window:] = jnp.zeros((HEAD, tail), BF16)
        dwin_ref[0, ks, window:] = jnp.concatenate([dkey_mem, pad], axis=1).astype(BF16)
        dwin_ref[0, vs, window:] = jnp.concatenate([dvalue_mem, pad], axis=1).astype(BF16)


def step_block(array):
    return pl.BlockSpec((1,) + array.shape[1:], lambda step, *_: (step, 0, 0))


def whole_block(array):
    return pl.BlockSpec(array.shape, lambda step, *_: (0,) * len(array.shape))


def attend(lengths, bank, parent_bias, window, parent, slots):
    groups, rows, columns = window.shape
    width = rows // 3
    own = sum(lengths)
    heads = width // HEAD
    outs = (
        jax.ShapeDtypeStruct((groups, width, own), BF16),
        jax.ShapeDtypeStruct((groups, heads, own), F32),
    )
    return pl.pallas_call(
        functools.partial(attention_forward, heads, lengths, bank),
        grid=(groups,),
        in_specs=[
            pl.BlockSpec(memory_space=pltpu.SMEM),
            step_block(window),
            step_block(parent),
            whole_block(slots),
        ],
        out_specs=[step_block(out) for out in outs],
        out_shape=outs,
        compiler_params=pltpu.CompilerParams(vmem_limit_bytes=40 << 20),
        name="attention_forward",
    )(parent_bias, window, parent, slots)


def attend_back(lengths, bank, parent_bias, window, parent, slots, dctx, lse):
    groups, rows, columns = window.shape
    heads = rows // 3 // HEAD
    outs = (jax.ShapeDtypeStruct(window.shape, BF16), jax.ShapeDtypeStruct(parent.shape, BF16))
    return pl.pallas_call(
        functools.partial(attention_backward, heads, lengths, bank),
        grid=(groups,),
        in_specs=[
            pl.BlockSpec(memory_space=pltpu.SMEM),
            step_block(window),
            step_block(parent),
            whole_block(slots),
            step_block(dctx),
            step_block(lse),
        ],
        out_specs=[step_block(out) for out in outs],
        out_shape=outs,
        compiler_params=pltpu.CompilerParams(vmem_limit_bytes=40 << 20),
        name="attention_backward",
    )(parent_bias, window, parent, slots, dctx, lse)


def copy_block(index_ref, source_ref, out_ref):
    out_ref[...] = source_ref[...]


def pick_parents(parents, gathered, seg_row, per_device):
    count = parents.shape[0]
    feat = gathered.shape[1]
    return pl.pallas_call(
        copy_block,
        grid_spec=pltpu.PrefetchScalarGridSpec(
            num_scalar_prefetch=1,
            grid=(count,),
            in_specs=[
                pl.BlockSpec((1, feat, SEG), lambda n, index: (index[n] // seg_row, 0, index[n] % seg_row)),
            ],
            out_specs=pl.BlockSpec((1, feat, SEG), lambda n, index: (n // per_device, 0, n % per_device)),
        ),
        out_shape=jax.ShapeDtypeStruct((count // per_device, feat, per_device * SEG), gathered.dtype),
        name="pick_parents",
    )(parents, gathered)


def add_parents_kernel(count, seg_row, per_device, bank, index_ref, mem_ref, par_ref, out_ref, sum_ref):
    feat = par_ref.shape[1]
    sum_ref[...] = jnp.zeros(sum_ref.shape, F32)
    for n in range(count):
        seg = index_ref[n]

        @pl.when(seg >= 0)
        def add(n=n, seg=seg):
            block = par_ref[n // per_device, :, (n % per_device) * SEG : (n % per_device + 1) * SEG]
            sum_ref[seg] += block.astype(F32)

    rows = out_ref.shape[0]
    for r in range(rows):
        for s in range(seg_row):
            out_ref[r, :, s * SEG : (s + 1) * SEG] = sum_ref[r * seg_row + s].astype(BF16)
        out_ref[r, :, seg_row * SEG :] = mem_ref[...].astype(BF16)


def add_parents(parents, mem, contributions, rows, seg_row, per_device):
    count = parents.shape[0]
    feat, bank = mem.shape
    out = jax.ShapeDtypeStruct((rows, feat, seg_row * SEG + bank), BF16)
    return pl.pallas_call(
        functools.partial(add_parents_kernel, count, seg_row, per_device, bank),
        in_specs=[
            pl.BlockSpec(memory_space=pltpu.SMEM),
            pl.BlockSpec(memory_space=pltpu.VMEM),
            pl.BlockSpec(memory_space=pltpu.VMEM),
        ],
        out_specs=pl.BlockSpec(memory_space=pltpu.VMEM),
        out_shape=out,
        scratch_shapes=[pltpu.VMEM((rows * seg_row, feat, SEG), F32)],
        compiler_params=pltpu.CompilerParams(vmem_limit_bytes=40 << 20),
        name="add_parents",
    )(parents, mem, contributions)


def exchange(blocks):
    return lax.all_to_all(blocks, "col", 0, 0, tiled=True)


def norm_stats(values):
    center = jnp.mean(values, axis=0, keepdims=True)
    spread = jnp.mean(values * values, axis=0, keepdims=True) - center * center
    return center, lax.rsqrt(spread + EPSILON)


def norm_back(grad, normed, scale, gain):
    scaled = grad * gain
    return scale * (
        scaled
        - jnp.mean(scaled, axis=0, keepdims=True)
        - normed * jnp.mean(scaled * normed, axis=0, keepdims=True)
    )


def lane_sum(array):
    return jnp.sum(array, axis=-1, dtype=F32)


def on_device(
    tokens,
    memory,
    parents,
    memory_slots,
    query_weight,
    query_bias,
    key_weight,
    value_weight,
    value_bias,
    out_weight,
    out_bias,
    norm_gain,
    norm_shift,
    up_weight,
    up_bias,
    down_weight,
    down_bias,
    final_gain,
    final_shift,
    cotangent,
):
    rows, cols = lax.axis_size("row"), lax.axis_size("col")
    row, col = lax.axis_index("row"), lax.axis_index("col")
    feat, row_tokens = tokens.shape
    own = row_tokens // cols
    seg_row = row_tokens // SEG
    model = feat * cols
    width = query_weight.shape[1]
    hidden_width = up_weight.shape[1]
    bank = memory.shape[0]
    segments, ranges = plan_windows(own, cols)
    per_device = len(segments[0])
    window = per_device * SEG
    lengths = tuple(min(SEG, own - j * SEG) for j in range(per_device))

    first_shard = jnp.concatenate([query_weight, key_weight, value_weight, out_weight.T], axis=1)
    first = lax.all_gather(first_shard, GROUP, axis=0, tiled=True).reshape(rows, model, -1)
    up = lax.all_gather(up_weight, GROUP, axis=0, tiled=True).reshape(rows, model, -1)
    down = lax.all_gather(down_weight, GROUP, axis=0, tiled=True).reshape(rows, model, -1)

    def window_of(array, index):
        return jnp.concatenate([array[:, a : a + n] for a, n in ranges[index]], axis=1)

    vectors = jnp.stack([out_bias, norm_gain, norm_shift, down_bias, final_gain, final_shift], axis=1)
    tail = -(-(bank + vectors.shape[1]) // 128) * 128
    side = jnp.concatenate(
        [memory.T, vectors, jnp.zeros((feat, tail - bank - vectors.shape[1]), BF16)], axis=1
    )
    sent = jnp.stack([jnp.concatenate([window_of(tokens, i), side], axis=1) for i in range(cols)])
    tok_window = exchange(sent).reshape(model, window + tail)
    grad_out = exchange(jnp.stack([window_of(cotangent, i)[:, :own] for i in range(cols)]))
    grad_out = grad_out.reshape(model, own).astype(F32)
    column = lambda i: tok_window[:, window + bank + i : window + bank + i + 1].astype(F32)
    out_b, gain_1, shift_1, down_b, gain_2, shift_2 = (column(i) for i in range(6))

    row_vectors = jnp.concatenate(
        [query_bias[:, None], value_bias[:, None], up_bias.reshape(-1, feat).T], axis=1
    )
    row_side = jnp.concatenate([row_vectors, jnp.zeros((feat, 128 - row_vectors.shape[1]), BF16)], axis=1)
    everything = lax.all_gather(jnp.concatenate([tokens, row_side], axis=1), "row", axis=0)
    row_cols = everything[:, :, row_tokens : row_tokens + row_vectors.shape[1]].astype(F32)
    query_b, value_b = row_cols[:, :, 0:1], row_cols[:, :, 1:2]
    up_b = row_cols[:, :, 2:].transpose(0, 2, 1).reshape(rows, hidden_width, 1)

    row_parents = lax.dynamic_slice_in_dim(parents, row * seg_row, seg_row, 0)
    row_slots = lax.dynamic_slice_in_dim(memory_slots, row * seg_row, seg_row, 0)
    chosen = np.array(segments, np.int32)
    pick = (chosen.reshape(-1)[:, None] == np.arange(seg_row)[None, :]).astype(np.int32)
    all_parents = jnp.sum(pick * row_parents[None, :], axis=1)
    own_pick = lax.dynamic_index_in_dim(
        jnp.asarray(pick.reshape(cols, per_device, seg_row)), col, 0, keepdims=False
    )
    own_parents = jnp.sum(own_pick * row_parents[None, :], axis=1)
    parent_bias = jnp.where(own_parents >= 0, 0.0, NEGATIVE).astype(F32)
    counts = jnp.sum((row_slots[:, :, None] == jnp.arange(bank)[None, None, :]).astype(F32), axis=1)
    own_counts = jnp.sum(own_pick[:, :, None].astype(F32) * counts[None], axis=1)
    slots = jnp.where(own_counts > 0, jnp.log(jnp.maximum(own_counts, 1.0)), NEGATIVE).T

    par_sent = pick_parents(jnp.maximum(all_parents, 0), everything, seg_row, per_device)
    tok_parent = exchange(par_sent).reshape(model, window)

    def project(block, toks):
        return jnp.einsum("rdf,dt->rft", block, toks, preferred_element_type=F32)

    scale = HEAD ** (-0.5)
    joint = project(first[:, :, : 3 * width], tok_window)
    win = jnp.concatenate(
        [
            (joint[:, :width] + query_b).astype(BF16) * jnp.asarray(scale, BF16),
            joint[:, width : 2 * width].astype(BF16),
            (joint[:, 2 * width :] + value_b).astype(BF16),
        ],
        axis=1,
    )
    joint_par = project(first[:, :, width : 3 * width], tok_parent)
    par = jnp.concatenate(
        [joint_par[:, :width].astype(BF16), (joint_par[:, width:] + value_b).astype(BF16)], axis=1
    )
    ctx, lse = attend(lengths, bank, parent_bias, win, par, slots)
    out_t = first[:, :, 3 * width :].transpose(1, 0, 2).reshape(model, rows * width)
    ctx = ctx.reshape(rows * width, own)
    tok_own = tok_window[:, :own].astype(F32)
    attended = nn(out_t, ctx) + out_b + tok_own
    center_1, scale_1 = norm_stats(attended)
    normed_1 = (attended - center_1) * scale_1
    hidden = normed_1 * gain_1 + shift_1
    hidden_low = hidden.astype(BF16)
    upper = project(up, hidden_low) + up_b
    phi = 0.5 * (1.0 + lax.erf(upper * np.float32(0.5**0.5)))
    active = (upper * phi).astype(BF16)
    slope = phi + upper * jnp.exp(-0.5 * upper * upper) * np.float32(1.0 / np.sqrt(2.0 * np.pi))
    second = jnp.einsum("rdj,rjt->dt", down, active, preferred_element_type=F32) + down_b + hidden
    center_2, scale_2 = norm_stats(second)
    normed_2 = (second - center_2) * scale_2
    result = (normed_2 * gain_2 + shift_2).astype(BF16)

    second_grad = norm_back(grad_out, normed_2, scale_2, gain_2)
    final_gain_grad = lane_sum(grad_out * normed_2)
    final_shift_grad = lane_sum(grad_out)
    down_low = second_grad.astype(BF16)
    down_grad = jnp.einsum("dt,rjt->rdj", down_low, active, preferred_element_type=F32)
    down_bias_grad = lane_sum(down_low)
    upper_low = (project(down, down_low) * slope).astype(BF16)
    up_grad = jnp.einsum("dt,rjt->rdj", hidden_low, upper_low, preferred_element_type=F32)
    up_bias_grad = lane_sum(upper_low).reshape(-1)
    hidden_grad = jnp.einsum("rdj,rjt->dt", up, upper_low, preferred_element_type=F32) + second_grad
    first_grad = norm_back(hidden_grad, normed_1, scale_1, gain_1)
    norm_gain_grad = lane_sum(hidden_grad * normed_1)
    norm_shift_grad = lane_sum(hidden_grad)
    first_low = first_grad.astype(BF16)
    out_bias_grad = lane_sum(first_low)
    out_grad = nt(first_low, ctx).reshape(model, rows, width).transpose(1, 0, 2)
    dctx = tn(out_t, first_low).astype(BF16).reshape(rows, width, own)
    dwin, dpar = attend_back(lengths, bank, parent_bias, win, par, slots, dctx, lse)

    joint_grad = jnp.einsum("dt,rft->rdf", tok_window, dwin, preferred_element_type=F32)
    par_grad = jnp.einsum("dt,rft->rdf", tok_parent, dpar, preferred_element_type=F32)
    first_grads = jnp.concatenate(
        [joint_grad[:, :, :width], joint_grad[:, :, width:] + par_grad, out_grad], axis=2
    ).astype(BF16)
    query_bias_grad = lane_sum(dwin[:, :width]).reshape(-1)
    value_bias_grad = (lane_sum(dwin[:, 2 * width :]) + lane_sum(dpar[:, width:])).reshape(-1)

    dtok = jnp.einsum("rdf,rft->dt", first[:, :, : 3 * width], dwin, preferred_element_type=F32)
    dtok = dtok.at[:, :own].add(first_grad).astype(BF16)
    dtok_par = jnp.einsum("rdf,rft->dt", first[:, :, width : 3 * width], dpar, preferred_element_type=F32)
    back = exchange(jnp.concatenate([dtok, dtok_par.astype(BF16)], axis=1).reshape(cols, feat, -1))
    mem_part = jnp.sum(back[:, :, window : window + 128].astype(F32), axis=0)
    placed = add_parents(all_parents, mem_part, back[:, :, window + tail :], rows, seg_row, per_device)
    placed = lax.psum_scatter(placed, "row", scatter_dimension=0, tiled=False).astype(F32)
    memory_grad = placed[:, row_tokens : row_tokens + bank].T
    pieces = []
    step = np.gcd(own, SEG)
    for start in range(0, row_tokens, step):
        total = placed[:, start : start + step]
        for i in range(cols):
            at = 0
            for a, n in ranges[i]:
                if a <= start < a + n:
                    total = total + back[i, :, at + start - a : at + start - a + step].astype(F32)
                at += n
        pieces.append(total)
    tokens_grad = jnp.concatenate(pieces, axis=1)

    returned = exchange(result.reshape(cols, feat, own))
    order = {}
    for i in range(cols):
        at = 0
        for a, n in ranges[i]:
            if at < own:
                order[a] = (i, at, n)
            at += n
    layer_output = jnp.concatenate(
        [returned[i, :, at : at + n] for a, (i, at, n) in sorted(order.items())], axis=1
    )

    def reduce_weights(grads):
        mine = lax.psum_scatter(grads.reshape(-1, grads.shape[-1]), GROUP, scatter_dimension=0, tiled=True)
        return lax.psum(mine, "leaf").astype(F32)

    down_total = reduce_weights(down_grad.astype(BF16))
    up_total = reduce_weights(up_grad.astype(BF16))
    first_total = reduce_weights(first_grads)
    sums = lax.psum(
        jnp.concatenate(
            [
                query_bias_grad,
                value_bias_grad,
                out_bias_grad,
                norm_gain_grad,
                norm_shift_grad,
                up_bias_grad,
                down_bias_grad,
                final_gain_grad,
                final_shift_grad,
            ]
        ),
        EVERY,
    )

    def part(offset, length, index):
        return lax.dynamic_slice_in_dim(sums, offset + index * length, length, 0)

    return (
        layer_output,
        tokens_grad,
        memory_grad,
        first_total[:, :width],
        part(0, width, row),
        first_total[:, width : 2 * width],
        first_total[:, 2 * width : 3 * width],
        part(model, width, row),
        first_total[:, 3 * width :].T,
        part(2 * model, feat, col),
        part(3 * model, feat, col),
        part(4 * model, feat, col),
        up_total,
        part(5 * model, hidden_width, row),
        down_total,
        part(5 * model + rows * hidden_width, feat, col),
        part(6 * model + rows * hidden_width, feat, col),
        part(7 * model + rows * hidden_width, feat, col),
    )


def solution(mesh):
    return jax.shard_map(
        on_device,
        mesh=mesh,
        in_specs=(
            P("col", ("leaf", "row")),
            P("leaf", "col"),
            P("leaf"),
            P("leaf", None),
            P("col", "row"),
            P("row"),
            P("col", "row"),
            P("col", "row"),
            P("row"),
            P("row", "col"),
            P("col"),
            P("col"),
            P("col"),
            P("col", "row"),
            P("row"),
            P("col", "row"),
            P("col"),
            P("col"),
            P("col"),
            P("col", ("leaf", "row")),
        ),
        out_specs=(
            P("col", ("leaf", "row")),
            P("col", ("leaf", "row")),
            P("leaf", "col"),
            P("col", "row"),
            P("row"),
            P("col", "row"),
            P("col", "row"),
            P("row"),
            P("row", "col"),
            P("col"),
            P("col"),
            P("col"),
            P("col", "row"),
            P("row"),
            P("col", "row"),
            P("col"),
            P("col"),
            P("col"),
        ),
        check_vma=False,
    )
```

time: 2620 us -> 684 us (0.26)
  waiting for transfers between devices: 1870 us -> 375 us
  local copies, waits for them, and re-layouts: 230 us -> 41 us
  matrix products: 265 us -> 83.2 us
  other arithmetic: 139 us -> 50.1 us
  Pallas kernels: 0 us -> 43 us
  blocking collectives: 88.5 us -> 46.3 us
    reduce_scatter x7 -> x4, waiting for transfers between devices: 999 us -> 204 us  [the longest x3 153 us: reduce_weights(): lax.psum_scatter(grads.reshape(-1, grads.shape[-1]), GROUP, scatter_dimen...]
    all_gather x10 -> x4, waiting for transfers between devices: 622 us -> 154 us  [the longest x1 49.5 us: on_device(): lax.all_gather(jnp.concatenate([tokens, row_side], axis=1), 'row', axis=0)]
    unnamed x24 -> x9, waiting for transfers between devices: 249 us -> 1.32 us
    dot_general x39 -> x15, matrix products: 250 us -> 83.2 us  [the longest x4 25.6 us: project(): return jnp.einsum('rdf,dt->rft', block, toks, preferred_element_type=F32)]
    convert_element_type x29 -> x10, other arithmetic: 58.4 us -> 9.43 us  [the longest x3 3.97 us: reduce_weights(): return lax.psum(mine, 'leaf').astype(F32)]
    another operation x10 -> x8, local copies, waits for them, and re-layouts: 49.2 us -> 3.59 us  [the longest x4 25.6 us: assemble(): group_seg = gathered.reshape(-1, SEG, width)]
    pallas_call x0 -> x4, Pallas kernels: none -> 43 us  [the longest x1 20 us: attend_back(): pl.pallas_call(functools.partial(attention_backward, heads, lengths, bank...]
    psum x7 -> x1, blocking collectives: 88.5 us -> 46.3 us  [on_device(): lax.psum(jnp.concatenate([query_bias_grad, value_bias_grad, out_bias_grad...]
  transfers between devices with their start and end apart: 21 -> 14, of which waited for: 20 -> 8; matrix products, arithmetic and copies ran while one was open for 6% -> 17% of each run, Pallas kernels for 0% -> 6%
where the time goes in v1:
time: 684 us; the launch traced here: 675 us
  waiting for transfers between devices  375 us (55%)
  matrix products  83.2 us (12%)
  other arithmetic  50.1 us (7%)
  blocking collectives  46.3 us (7%)
  Pallas kernels  43 us (6%)
  local copies, waits for them, and re-layouts  41 us (6%)
  starting transfers between devices  20.1 us (3%)
  between operations  15.5 us (2%)
    reduce_scatter x3, waiting for transfers between devices, reduce_weights(): lax.psum_scatter(grads.reshape(-1, grads.shape[-1]), GROUP, scatter_dimen...  153 us
    reduce_scatter x1, waiting for transfers between devices, on_device(): lax.psum_scatter(placed, 'row', scatter_dimension=0, tiled=False)  50.7 us
    all_gather x1, waiting for transfers between devices, on_device(): lax.all_gather(jnp.concatenate([tokens, row_side], axis=1), 'row', axis=0)  49.5 us
    psum x1, blocking collectives, on_device(): lax.psum(jnp.concatenate([query_bias_grad, value_bias_grad, out_bias_grad...  46.3 us
    all_gather x1, waiting for transfers between devices, on_device(): lax.all_gather(down_weight, GROUP, axis=0, tiled=True)  44.4 us
    all_gather x1, waiting for transfers between devices, on_device(): lax.all_gather(first_shard, GROUP, axis=0, tiled=True)  43.5 us
    dot_general x4, matrix products, project(): return jnp.einsum('rdf,dt->rft', block, toks, preferred_element_type=F32)  25.6 us
    pallas_call x1, Pallas kernels, attend_back(): pl.pallas_call(functools.partial(attention_backward, heads, lengths, bank...  20 us
  transfers between devices with their start and end apart: 14, of which 8 were waited for; matrix products, arithmetic and copies ran while one was open for 17% of the time, Pallas kernels for 6%

profile of v1, /device:TPU:0, one launch (start us, length us, event | category | flops | bytes accessed | tf_op | source)
XLA Modules:
  0.0 674.6 jit_solution(18173489705896112480)
XLA Ops:
  9.9 3.1 concatenate.75
  18.5 4.4 all-to-all-start
  24.9 16.0 %all-to-all-done = bf16[4,192,896]{2,1,0:T(8,128)(2,1)S(1)} async-done(((bf16[4,192,896]{2,1,0:T(8,128)(2,1)}), bf16[4,192,896]{2,1,0:T(8,128)(2,1)S(1)}, u32[]{:S(2)}, u32[]{:S(2)}) %all-to-all-start) | async-done | bytes 1376288 | tf_op jit(solution)/shard_map/all_to_all | solution.py:248
  40.8 3.5 all-to-all-start.3
  46.1 49.5 %all-gather.12.cloned.1.call-done = bf16[768,2688]{1,0:T(8,128)(2,1)} async-done(((bf16[192,2688]{1,0:T(8,128)(2,1)}), bf16[768,2688]{1,0:T(8,128)(2,1)}) %all-gather.12.cloned.1.call-update) | async-done | bytes 4128784 | tf_op jit(solution)/shard_map/all_gather | solution.py:330
  95.6 7.9 %pick_parents.1 = bf16[4,192,768]{2,1,0:T(8,128)(2,1)} custom-call(s32[12]{0:T(128)} %broadcast_maximum_fusion.index_ref, bf16[4,192,2688]{2,1,0:T(8,128)(2,1)} %bitcast.335), custom_call_target="tpu_custom_call" | custom-call | tf_op jit(solution)/shard_map/pick_parents/pallas_call | solution.py:195
  103.5 3.6 all-to-all-start.1
  109.5 43.5 %all-gather.6.cloned.1.call-done = bf16[3072,768]{1,0:T(8,128)(2,1)} async-done(((bf16[192,768]{1,0:T(8,128)(2,1)}), bf16[3072,768]{1,0:T(8,128)(2,1)}) %all-gather.6.cloned.1.call-update) | async-done | bytes 4718608 | tf_op jit(solution)/shard_map/all_gather | solution.py:307
  155.1 5.0 fusion.18
  169.3 3.9 fusion.11
  174.4 13.4 %attention_forward.1 = (bf16[4,192,640]{2,1,0:T(8,128)(2,1)S(1)}, f32[4,3,640]{2,1,0:T(4,128)S(1)}) custom-call(f32[3]{0:T(128)S(1)} %compare_select_fusion.1.bias_ref, bf16[4,576,896]{2,1,0:T(8,128)(2,1)S(1)} %pad_maximum_fusion.1.win_ref, bf16[4,384,768]{2,1,0:T(8,128)(2,1)S(1)} %pad_maximum_fusion.3.par_ref, f32[64,3]{1,0:T(8,128)S(1)} %bitcast.323), custom_call_target="tpu_custom_call" | custom-call | tf_op jit(solution)/shard_map/attention_forward/pallas_call | solution.py:150
  190.3 17.0 %all-gather.8.cloned.1.call-done = bf16[3072,768]{1,0:T(8,128)(2,1)} async-done(((bf16[192,768]{1,0:T(8,128)(2,1)}), bf16[3072,768]{1,0:T(8,128)(2,1)}) %all-gather.8.cloned.1.call-update) | async-done | bytes 4718608 | tf_op jit(solution)/shard_map/all_gather | solution.py:308
  207.3 9.8 %fusion.9 = (bf16[4,768,640]{1,2,0:T(8,128)(2,1)}, f32[640,4,768]{2,0,1:T(8,128)}) fusion(f32[4,768]{1,0:T(4,128)S(1)} %add.309, bf16[4,768,768]{2,1,0:T(8,128)(2,1)} %bitcast.352, f32[768,640]{1,0:T(8,128)} %get-tuple-element.171, f32[768]{0:T(1024)S(1)} %get-tuple-element.124, f32[768]{0:T(1024)S(1)} %get-tuple-element.125, ...), kind=kOutput, calls=%fused_computation.12 | convolution fusion | flops 3034152960 | bytes 18504704 | tf_op jit(solution)/shard_map/rdf,dt->rft/dot_general | solution.py:353
  217.1 44.4 %all-gather.10.cloned.1.call-done = bf16[3072,768]{1,0:T(8,128)(2,1)} async-done(((bf16[192,768]{1,0:T(8,128)(2,1)}), bf16[3072,768]{1,0:T(8,128)(2,1)}) %all-gather.10.cloned.1.call-update) | async-done | bytes 4718608 | tf_op jit(solution)/shard_map/all_gather | solution.py:309
  261.5 8.3 %fusion.84 = (f32[640]{0:T(1024)S(1)}, f32[640]{0:T(1024)S(1)}, f32[768,640]{1,0:T(8,128)S(1)}) fusion(f32[768]{0:T(1024)S(1)} %get-tuple-element.124, f32[768]{0:T(1024)S(1)} %get-tuple-element.125, f32[640]{0:T(1024)S(1)} %get-tuple-element.170, f32[768,640]{1,0:T(8,128)} %get-tuple-element.171, f32[640]{0:T(1024)S(1)} %get-tuple-element.169, ...), kind=kOutput, calls=%fused_computation.233 | convolution fusion | flops 3024321536 | bytes 12602368 | tf_op jit(solution)/shard_map/rdj,rjt->dt/dot_general | solution.py:382
  274.0 6.9 %convert_reduce_fusion = (f32[4,768]{1,0:T(4,128)}, bf16[4,768,640]{1,2,0:T(8,128)(2,1)S(1)}) fusion(f32[640,4,768]{2,0,1:T(8,128)S(1)} %copy-done.55, f32[4,768]{1,0:T(4,128)S(1)} %add.309, bf16[4,768,768]{2,1,0:T(8,128)(2,1)S(1)} %bitcast.355, f32[768,640]{1,0:T(8,128)S(1)} %get-tuple-element.136), kind=kOutput, calls=%fused_computation.13 | convolution fusion | flops 3045946368 | bytes 18505728 | tf_op jit(solution)/shard_map/rdf,dt->rft/dot_general | solution.py:353
  280.9 5.8 convolution_convert_fusion.1
  286.7 9.9 %multiply_reduce_fusion = (f32[768]{0:T(1024)}, f32[640]{0:T(1024)S(1)}, f32[640]{0:T(1024)S(1)}, f32[768]{0:T(1024)}, f32[768,640]{1,0:T(8,128)S(1)}) fusion(f32[768,640]{1,0:T(8,128)} %get-tuple-element.171, f32[640]{0:T(1024)S(1)} %get-tuple-element.170, f32[640]{0:T(1024)S(1)} %get-tuple-element.169, f32[768]{0:T(1024)S(1)} %get-tuple-element.125, ...), kind=kOutput, calls=%fused_computation.63 | convolution fusion | flops 3024811264 | bytes 14568448 | tf_op jit(solution)/shard_map/rdj,rjt->dt/dot_general | solution.py:396
  301.2 20.0 %attention_backward.1 = (bf16[4,576,896]{2,1,0:T(8,128)(2,1)S(1)}, bf16[4,384,768]{2,1,0:T(8,128)(2,1)S(1)}) custom-call(f32[3]{0:T(128)S(1)} %compare_select_fusion.1.bias_ref, bf16[4,576,896]{2,1,0:T(8,128)(2,1)S(1)} %copy-done.3, bf16[4,384,768]{2,1,0:T(8,128)(2,1)S(1)} %pad_maximum_fusion.3.par_ref, f32[64,3]{1,0:T(8,128)S(1)} %bitcast.324, ...), custom_call_target="tpu_custom_call" | custom-call | tf_op jit(solution)/shard_map/attention_backward/pallas_call | solution.py:170
  321.2 3.9 convolution_bitcast_fusion
  326.9 3.5 fusion.10
  333.4 3.7 fusion.37
  341.3 5.9 pad_maximum_fusion
  348.8 7.6 %convolution_convert_fusion = bf16[4,768,768]{1,2,0:T(8,128)(2,1)} fusion(bf16[4,768,640]{1,2,0:T(8,128)(2,1)} %get-tuple-element.172, f32[768,640]{1,0:T(8,128)S(1)} %copy-done.21), kind=kOutput, calls=%fused_computation.23 | convolution fusion | flops 3022749696 | bytes 10616832 | tf_op jit(solution)/shard_map/dt,rjt->rdj/dot_general | solution.py:391
  357.0 7.3 %fusion.31 = f32[768,896]{1,0:T(8,128)S(1)} fusion(bf16[4,576,896]{2,1,0:T(8,128)(2,1)} %copy-done.5, bf16[4,768,768]{2,1,0:T(8,128)(2,1)} %bitcast.346), kind=kOutput, calls=%fused_computation.73 | convolution fusion | flops 3170893824 | bytes 10813440 | tf_op jit(solution)/shard_map/rdf,rft->dt/dot_general | solution.py:414
  367.3 4.0 bitcast_convert_fusion
  373.1 4.6 all-to-all-start.4
  377.7 74.4 %reduce-scatter.7.cloned.1.call-done = bf16[192,768]{1,0:T(8,128)(2,1)} async-done(((bf16[3072,768]{1,0:T(8,128)(2,1)}), bf16[192,768]{1,0:T(8,128)(2,1)}) %reduce-scatter.7.cloned.1.call-update) | async-done | bytes 294928 | tf_op jit(solution)/shard_map/reduce_scatter | solution.py:448
  452.2 78.5 %reduce-scatter.11.cloned.1.call-done = bf16[192,768]{1,0:T(8,128)(2,1)} async-done(((bf16[3072,768]{1,0:T(8,128)(2,1)}), bf16[192,768]{1,0:T(8,128)(2,1)}) %reduce-scatter.11.cloned.1.call-update) | async-done | bytes 294928 | tf_op jit(solution)/shard_map/reduce_scatter | solution.py:448
  539.7 3.5 all-to-all-start.2
  543.5 46.3 %psum.29 = f32[9216]{0:T(1024)S(1)} all-reduce(f32[9216]{0:T(1024)S(1)} %constant_dynamic-update-slice_fusion.8), channel_id=1, replica_groups=mesh['leaf'=2,'row'=4,'col'=4] {'leaf','row','col'}, use_global_device_ids=true, to_apply=%region_27.28 | all-reduce | flops 9216 | bytes 73728 | tf_op jit(solution)/shard_map/psum | solution.py:454
  597.2 50.7 %reduce-scatter.5.cloned.1.call-done = bf16[1,192,2688]{2,1,0:T(8,128)(2,1)} async-done(((bf16[4,192,2688]{2,1,0:T(8,128)(2,1)}), bf16[1,192,2688]{2,1,0:T(8,128)(2,1)}) %reduce-scatter.5.cloned.1.call-update) | async-done | bytes 1032208 | tf_op jit(solution)/shard_map/reduce_scatter | solution.py:420
  (278 shorter events, 89.3 us)
Async XLA Ops:
  7.2 15.7 %copy-start = (s32[40,20]{0,1:T(8,128)S(1)}, s32[40,20]{0,1:T(8,128)}, u32[]{:S(2)}) copy-start(s32[40,20]{0,1:T(8,128)} %param.27) | copy-start | bytes 9604
  7.2 88.3 %all-gather.12.cloned.1.call-start = ((), (), s32[]{:S(2)}) async-start(), calls=%async_computation.16 | async-start | bytes 5160960 | tf_op jit(solution)/shard_map/all_gather | solution.py:330
  13.0 139.9 %all-gather.6.cloned.1.call-start = ((), (), s32[]{:S(2)}) async-start(), calls=%async_computation.9 | async-start | bytes 5013504 | tf_op jit(solution)/shard_map/all_gather | solution.py:307
  14.1 193.2 %all-gather.8.cloned.1.call-start = ((), (), s32[]{:S(2)}) async-start(), calls=%async_computation.10 | async-start | bytes 5013504 | tf_op jit(solution)/shard_map/all_gather | solution.py:308
  14.8 246.7 %all-gather.10.cloned.1.call-start = ((), (), s32[]{:S(2)}) async-start(), calls=%async_computation.11 | async-start | bytes 5013504 | tf_op jit(solution)/shard_map/all_gather | solution.py:309
  18.5 22.3 %all-to-all-start = ((bf16[4,192,896]{2,1,0:T(8,128)(2,1)}), bf16[4,192,896]{2,1,0:T(8,128)(2,1)S(1)}, u32[]{:S(2)}, u32[]{:S(2)}) async-start(bf16[4,192,896]{2,1,0:T(8,128)(2,1)} %pad_maximum_fusion.4), calls=%async_computation | async-start | bytes 2752512 | tf_op jit(solution)/shard_map/all_to_all | solution.py:248
  23.8 20.8 %copy-start.41 = (s32[12,10]{1,0:T(8,128)S(1)}, s32[12,10]{1,0:T(8,128)}, u32[]{:S(2)}) copy-start(s32[12,10]{1,0:T(8,128)} %constant.122.clone) | copy-start | bytes 1444
  40.8 62.6 %copy-start.13 = (bf16[4,192,896]{2,1,0:T(8,128)(2,1)}, bf16[4,192,896]{2,1,0:T(8,128)(2,1)S(1)}, u32[]{:S(2)}) copy-start(bf16[4,192,896]{2,1,0:T(8,128)(2,1)S(1)} %all-to-all-done) | copy-start | bytes 4128772
  40.8 62.6 %all-to-all-start.3 = ((bf16[4,192,640]{2,1,0:T(8,128)(2,1)}), bf16[4,192,640]{2,1,0:T(8,128)(2,1)S(1)}, u32[]{:S(2)}, u32[]{:S(2)}) async-start(bf16[4,192,640]{2,1,0:T(8,128)(2,1)} %pad_maximum_fusion.5), calls=%async_computation.3 | async-start | bytes 1966080 | tf_op jit(solution)/shard_map/all_to_all | solution.py:248
  103.5 51.6 %all-to-all-start.1 = ((bf16[4,192,768]{2,1,0:T(8,128)(2,1)}), bf16[4,192,768]{2,1,0:T(8,128)(2,1)S(1)}, u32[]{:S(2)}, u32[]{:S(2)}) async-start(bf16[4,192,768]{2,1,0:T(8,128)(2,1)} %pick_parents.1), calls=%async_computation.1 | async-start | bytes 2359296 | tf_op jit(solution)/shard_map/all_to_all | solution.py:248
  107.0 270.7 %reduce-scatter.9.cloned.1.call-start = ((), (), s32[]{:S(2)}) async-start(), calls=%async_computation.14 | async-start | bytes 5013504 | tf_op jit(solution)/shard_map/reduce_scatter | solution.py:448
  174.3 13.5 %copy-start.2 = (bf16[4,576,896]{2,1,0:T(8,128)(2,1)}, bf16[4,576,896]{2,1,0:T(8,128)(2,1)S(1)}, u32[]{:S(2)}) copy-start(bf16[4,576,896]{2,1,0:T(8,128)(2,1)S(1)} %pad_maximum_fusion.1.win_ref) | copy-start | bytes 12386308
  174.4 13.5 %copy-start.26 = (bf16[4,768,192]{1,2,0:T(8,128)(2,1)S(1)}, bf16[4,768,192]{1,2,0:T(8,128)(2,1)}, u32[]{:S(2)}) copy-start(bf16[4,768,192]{1,2,0:T(8,128)(2,1)} %copy.249) | copy-start | bytes 3538948
  261.5 8.3 %copy-start.9 = (bf16[4,192,640]{2,1,0:T(8,128)(2,1)S(1)}, bf16[4,192,640]{2,1,0:T(8,128)(2,1)}, u32[]{:S(2)}) copy-start(bf16[4,192,640]{2,1,0:T(8,128)(2,1)} %copy-done.8) | copy-start | bytes 2949124
  261.5 12.2 %copy-start.55 = (f32[640,4,768]{2,0,1:T(8,128)S(1)}, f32[640,4,768]{2,0,1:T(8,128)}, u32[]{:S(2)}) copy-start(f32[640,4,768]{2,0,1:T(8,128)} %get-tuple-element.173) | copy-start | bytes 23592964
  273.7 7.2 %copy-start.20 = (f32[768,640]{1,0:T(8,128)}, f32[768,640]{1,0:T(8,128)S(1)}, u32[]{:S(2)}) copy-start(f32[768,640]{1,0:T(8,128)S(1)} %get-tuple-element.136) | copy-start | bytes 5898244
  274.0 6.9 %copy-start.22 = (f32[768,640]{1,0:T(8,128)S(1)}, f32[768,640]{1,0:T(8,128)}, u32[]{:S(2)}) copy-start(f32[768,640]{1,0:T(8,128)} %get-tuple-element.171) | copy-start | bytes 5898244
  286.7 165.5 %reduce-scatter.7.cloned.1.call-start = ((), (), s32[]{:S(2)}) async-start(), calls=%async_computation.13 | async-start | bytes 5013504 | tf_op jit(solution)/shard_map/reduce_scatter | solution.py:448
  286.7 10.0 %copy-start.23 = (f32[768,640]{1,0:T(8,128)S(1)}, f32[768,640]{1,0:T(8,128)}, u32[]{:S(2)}) copy-start(f32[768,640]{1,0:T(8,128)} %get-tuple-element.171) | copy-start | bytes 5898244
  301.2 20.1 %copy-start.15 = (bf16[4,192,896]{2,1,0:T(8,128)(2,1)S(1)}, bf16[4,192,896]{2,1,0:T(8,128)(2,1)}, u32[]{:S(2)}) copy-start(bf16[4,192,896]{2,1,0:T(8,128)(2,1)} %copy-done.13) | copy-start | bytes 4128772
  347.2 183.4 %reduce-scatter.11.cloned.1.call-start = ((), (), s32[]{:S(2)}) async-start(), calls=%async_computation.15 | async-start | bytes 5013504 | tf_op jit(solution)/shard_map/reduce_scatter | solution.py:448
  357.0 7.4 %copy-start.11 = (f32[768,640]{1,0:T(8,128)S(1)}, f32[768,640]{1,0:T(8,128)}, u32[]{:S(2)}) copy-start(f32[768,640]{1,0:T(8,128)} %copy-done.10) | copy-start | bytes 5898244
  373.1 157.6 %all-to-all-start.4 = ((bf16[4,192,1664]{2,1,0:T(8,128)(2,1)}), bf16[4,192,1664]{2,1,0:T(8,128)(2,1)}, u32[]{:S(2)}, u32[]{:S(2)}) async-start(bf16[4,192,1664]{2,1,0:T(8,128)(2,1)} %bitcast.325), calls=%async_computation.4 | async-start | bytes 5111808 | tf_op jit(solution)/shard_map/all_to_all | solution.py:248
  377.7 213.7 %all-reduce.3.cloned.1.call-start = ((), (), s32[]{:S(2)}) async-start(), calls=%async_computation.17 | async-start | bytes 1769472 | tf_op jit(solution)/shard_map/psum | solution.py:449
  530.7 117.2 %reduce-scatter.5.cloned.1.call-start = ((), (), s32[]{:S(2)}) async-start(), calls=%async_computation.12 | async-start | bytes 5160960 | tf_op jit(solution)/shard_map/reduce_scatter | solution.py:420
  537.1 6.2 copy-start.44
  537.1 6.3 copy-start.39
  537.1 6.3 copy-start.43
  537.1 6.3 copy-start.37
  537.1 6.3 copy-start.36
  539.7 51.4 %all-to-all-start.2 = ((bf16[4,192,640]{2,1,0:T(8,128)(2,1)}), bf16[4,192,640]{2,1,0:T(8,128)(2,1)S(1)}, u32[]{:S(2)}, u32[]{:S(2)}) async-start(bf16[4,192,640]{2,1,0:T(8,128)(2,1)} %bitcast.24), calls=%async_computation.2 | async-start | bytes 1966080 | tf_op jit(solution)/shard_map/all_to_all | solution.py:248
  653.2 14.5 %copy-start.1 = (s32[40,20]{0,1:T(8,128)S(1)}, s32[40,20]{0,1:T(8,128)}, u32[]{:S(2)}) copy-start(s32[40,20]{0,1:T(8,128)} %param.27) | copy-start | bytes 9604
  (38 other events, 138.9 us)
Sparse Core Ops, SparseCore 0:
  13.2 82.3 all-gather.11
  98.4 54.5 all-gather.5
  155.3 52.0 all-gather.7
  209.5 52.0 all-gather.9
  286.8 74.0 reduce-scatter.8
  365.1 87.0 reduce-scatter.6
  456.0 74.5 reduce-scatter.10
  533.3 36.3 all-reduce.2
  572.1 75.7 reduce-scatter.4

commit v2 on v1

v2 whole, which is shorter than its diff:
```python
import functools

import jax
import jax.numpy as jnp
import numpy as np
from jax import lax
from jax.experimental import pallas as pl
from jax.experimental.pallas import tpu as pltpu
from jax.sharding import PartitionSpec as P

HEAD = 64
SEG = 256
NEGATIVE = -1e30
EPSILON = 1e-05
EVERY = ("leaf", "row", "col")
BF16 = jnp.bfloat16
F32 = jnp.float32


def after(value, *others):
    return lax.optimization_barrier((value, others))[0]


def tn(left, right):
    return lax.dot_general(left, right, (((0,), (0,)), ((), ())), preferred_element_type=F32)


def nt(left, right):
    return lax.dot_general(left, right, (((1,), (1,)), ((), ())), preferred_element_type=F32)


def nn(left, right):
    return lax.dot_general(left, right, (((1,), (0,)), ((), ())), preferred_element_type=F32)


def plan_windows(own, count):
    segments, ranges = [], []
    for index in range(count):
        first, last = index * own, (index + 1) * own
        whole = [s for s in range(first // SEG, -(-last // SEG)) if s * SEG >= first and (s + 1) * SEG <= last]
        cut = [s for s in range(first // SEG, -(-last // SEG)) if s not in whole]
        pieces = [(s * SEG, SEG) for s in whole]
        for s in cut:
            low, high = max(first, s * SEG), min(last, (s + 1) * SEG)
            pieces.append((low, high - low))
            if low > s * SEG:
                pieces.append((s * SEG, low - s * SEG))
            if high < (s + 1) * SEG:
                pieces.append((high, (s + 1) * SEG - high))
        segments.append(whole + cut)
        ranges.append(pieces)
    return segments, ranges


def static_of(index, values):
    out = jnp.int32(values[0])
    for i, value in enumerate(values[1:], 1):
        out = jnp.where(index == i, jnp.int32(value), out)
    return out


def own_segments(segments, here_ref):
    return [
        here_ref[0] * here_ref[3] + static_of(here_ref[1], [lists[j] for lists in segments])
        for j in range(len(segments[0]))
    ]


def window_biases(segments, bank, here_ref, parents_ref, slots_ref):
    rows = lax.broadcasted_iota(jnp.int32, (bank, 1), 0)
    out = []
    for seg in own_segments(segments, here_ref):
        count = jnp.zeros((bank, 1), F32)
        for m in range(slots_ref.shape[1]):
            count = count + jnp.where(rows == slots_ref[seg, m], 1.0, 0.0)
        slot = jnp.where(count > 0, jnp.log(jnp.maximum(count, 1.0)), NEGATIVE)
        out.append((jnp.where(parents_ref[seg] >= 0, 0.0, NEGATIVE).astype(F32), slot))
    return out


def attention_forward(
    head_count, lengths, segments, bank, here_ref, parents_ref, slots_ref, win_ref, par_ref, ctx_ref, lse_ref
):
    width = head_count * HEAD
    biases = window_biases(segments, bank, here_ref, parents_ref, slots_ref)
    window = len(lengths) * SEG
    for head in range(head_count):
        low = head * HEAD
        key_mem = win_ref[0, width + low : width + low + HEAD, window : window + bank]
        value_mem = win_ref[0, 2 * width + low : 2 * width + low + HEAD, window : window + bank]
        for j, count in enumerate(lengths):
            cols = slice(j * SEG, (j + 1) * SEG)
            query = win_ref[0, low : low + HEAD, j * SEG : j * SEG + count]
            own = tn(win_ref[0, width + low : width + low + HEAD, cols], query)
            par = tn(par_ref[0, low : low + HEAD, cols], query) + biases[j][0]
            mem = tn(key_mem, query) + biases[j][1]
            top = jnp.maximum(
                jnp.maximum(jnp.max(own, axis=0, keepdims=True), jnp.max(par, axis=0, keepdims=True)),
                jnp.max(mem, axis=0, keepdims=True),
            )
            own, par, mem = jnp.exp(own - top), jnp.exp(par - top), jnp.exp(mem - top)
            total = (
                jnp.sum(own, axis=0, keepdims=True)
                + jnp.sum(par, axis=0, keepdims=True)
                + jnp.sum(mem, axis=0, keepdims=True)
            )
            mixed = (
                nn(win_ref[0, 2 * width + low : 2 * width + low + HEAD, cols], own.astype(BF16))
                + nn(par_ref[0, width + low : width + low + HEAD, cols], par.astype(BF16))
                + nn(value_mem, mem.astype(BF16))
            )
            ctx_ref[0, low : low + HEAD, j * SEG : j * SEG + count] = (mixed / total).astype(BF16)
            lse_ref[0, head : head + 1, j * SEG : j * SEG + count] = top + jnp.log(total)


def attention_backward(
    head_count,
    lengths,
    segments,
    bank,
    here_ref,
    parents_ref,
    slots_ref,
    win_ref,
    par_ref,
    dctx_ref,
    lse_ref,
    dwin_ref,
    dpar_ref,
):
    width = head_count * HEAD
    biases = window_biases(segments, bank, here_ref, parents_ref, slots_ref)
    window = len(lengths) * SEG
    tail = win_ref.shape[2] - window
    for head in range(head_count):
        low = head * HEAD
        qs, ks, vs = (slice(part * width + low, part * width + low + HEAD) for part in range(3))
        key_mem = win_ref[0, ks, window : window + bank]
        value_mem = win_ref[0, vs, window : window + bank]
        dkey_mem = jnp.zeros((HEAD, bank), F32)
        dvalue_mem = jnp.zeros((HEAD, bank), F32)
        for j, count in enumerate(lengths):
            cols = slice(j * SEG, (j + 1) * SEG)
            tok = slice(j * SEG, j * SEG + count)
            query = win_ref[0, qs, tok]
            dctx = dctx_ref[0, low : low + HEAD, tok]
            lse = lse_ref[0, head : head + 1, tok]
            key_own, value_own = win_ref[0, ks, cols], win_ref[0, vs, cols]
            key_par, value_par = par_ref[0, low : low + HEAD, cols], par_ref[0, width + low : width + low + HEAD, cols]
            own = jnp.exp(tn(key_own, query) - lse)
            par = jnp.exp(tn(key_par, query) + biases[j][0] - lse)
            mem = jnp.exp(tn(key_mem, query) + biases[j][1] - lse)
            gown, gpar, gmem = tn(value_own, dctx), tn(value_par, dctx), tn(value_mem, dctx)
            inner = (
                jnp.sum(own * gown, axis=0, keepdims=True)
                + jnp.sum(par * gpar, axis=0, keepdims=True)
                + jnp.sum(mem * gmem, axis=0, keepdims=True)
            )
            gown = (own * (gown - inner)).astype(BF16)
            gpar = (par * (gpar - inner)).astype(BF16)
            gmem = (mem * (gmem - inner)).astype(BF16)
            dquery = nn(key_own, gown) + nn(key_par, gpar) + nn(key_mem, gmem)
            dwin_ref[0, qs, tok] = (dquery * HEAD ** (-0.5)).astype(BF16)
            if count < SEG:
                dwin_ref[0, qs, j * SEG + count : (j + 1) * SEG] = jnp.zeros((HEAD, SEG - count), BF16)
            dwin_ref[0, ks, cols] = nt(query, gown).astype(BF16)
            dwin_ref[0, vs, cols] = nt(dctx, own.astype(BF16)).astype(BF16)
            dpar_ref[0, low : low + HEAD, cols] = nt(query, gpar).astype(BF16)
            dpar_ref[0, width + low : width + low + HEAD, cols] = nt(dctx, par.astype(BF16)).astype(BF16)
            dkey_mem += nt(query, gmem)
            dvalue_mem += nt(dctx, mem.astype(BF16))
        pad = jnp.zeros((HEAD, tail - bank), F32)
        dwin_ref[0, qs, window:] = jnp.zeros((HEAD, tail), BF16)
        dwin_ref[0, ks, window:] = jnp.concatenate([dkey_mem, pad], axis=1).astype(BF16)
        dwin_ref[0, vs, window:] = jnp.concatenate([dvalue_mem, pad], axis=1).astype(BF16)


def step_block(array):
    return pl.BlockSpec((1,) + array.shape[1:], lambda step, *_: (step, 0, 0))


def whole_block(array):
    return pl.BlockSpec(array.shape, lambda step, *_: (0,) * len(array.shape))


def cost(microseconds):
    return pl.CostEstimate(flops=int(microseconds * 1.0e9), bytes_accessed=0, transcendentals=0)


def params(mib):
    return pltpu.CompilerParams(vmem_limit_bytes=mib << 20)


def across_lanes(rows, index, low, high, columns):
    chosen = (lax.broadcasted_iota(jnp.int32, (rows.shape[0], 128), 0) == index).astype(BF16)
    column = tn(rows[:, low:high] if high - low < rows.shape[1] else rows, chosen)
    return jnp.concatenate([column] * (columns // 128), axis=1)


def project_kernel(low, high, scaled, near_ref, far_ref, toks_ref, bias_ref, out_ref):
    depth = near_ref.shape[1]
    out = tn(near_ref[0, :, low:high], toks_ref[:depth]) + tn(far_ref[0, :, low:high], toks_ref[depth:])
    out = (out + across_lanes(bias_ref[0], 1, low, high, out.shape[1])).astype(BF16)
    if scaled:
        out_ref[0, :scaled] = out[:scaled] * jnp.asarray(HEAD ** (-0.5), BF16)
        out_ref[0, scaled:] = out[scaled:]
    else:
        out_ref[0] = out


def project(near, far, toks, bias, low, high, scaled):
    groups = near.shape[0]
    out = jax.ShapeDtypeStruct((groups, high - low, toks.shape[1]), BF16)
    return pl.pallas_call(
        functools.partial(project_kernel, low, high, scaled),
        grid=(groups,),
        in_specs=[step_block(near), step_block(far), whole_block(toks), step_block(bias)],
        out_specs=step_block(out),
        out_shape=out,
        compiler_params=params(40),
        cost_estimate=cost(0.1),
        name="project",
    )(near, far, toks, bias)


def chunks(columns):
    return columns // 128


def mlp_forward_kernel(
    at,
    ctx_ref,
    win_ref,
    cot_keep,
    cot_got,
    cot_last,
    out_ref,
    near_up,
    far_up,
    near_down,
    far_down,
    bias_ref,
    keep_ref,
    along_ref,
    close_ref,
    active_ref,
    slope_ref,
    grad_ref,
    low_ref,
    hidden_ref,
    normed_ref,
    scale_ref,
    sums_ref,
    total_ref,
    wide_ref,
    parts_ref,
):
    step, last = pl.program_id(0), pl.num_programs(0) - 1
    depth = near_up.shape[2]
    model, own = total_ref.shape
    feat = keep_ref.shape[1]

    def column(i):
        return win_ref[:, at + i : at + i + 1].astype(F32)

    @pl.when(step == 0)
    def start():
        total_ref[...] = nn(out_ref[...], ctx_ref[...])
        bias, gain, shift = column(0), column(1), column(2)

        def body(i, carry):
            cols = pl.ds(pl.multiple_of(i * 128, 128), 128)
            values = total_ref[:, cols] + bias + win_ref[:, cols].astype(F32)
            center, scale = norm_stats(values)
            normed = (values - center) * scale
            hidden = normed * gain + shift
            normed_ref[:, cols] = normed
            scale_ref[:, cols] = scale
            wide_ref[:, cols] = hidden
            hidden_ref[:, cols] = hidden.astype(BF16)
            return carry

        lax.fori_loop(0, chunks(own), body, 0)
        total_ref[...] = jnp.zeros(total_ref.shape, F32)

    width = near_up.shape[3]
    piece = width // 3
    for low in range(0, width, piece):
        rows = slice(low, low + piece)
        upper = tn(near_up[0, 0, :, rows], hidden_ref[:depth]) + tn(far_up[0, 0, :, rows], hidden_ref[depth:])
        upper = upper + across_lanes(bias_ref[0], 0, low, low + piece, own)
        phi = 0.5 * (1.0 + lax.erf(upper * np.float32(0.5**0.5)))
        active_ref[0, rows] = (upper * phi).astype(BF16)
        slope_ref[0, rows] = (
            phi + upper * jnp.exp(-0.5 * upper * upper) * np.float32(1.0 / np.sqrt(2.0 * np.pi))
        ).astype(BF16)
    total_ref[:depth] += nn(near_down[0, 0], active_ref[0])
    total_ref[depth:] += nn(far_down[0, 0], active_ref[0])

    @pl.when(step == last)
    def finish():
        bias, gain, shift = column(3), column(4), column(5)
        parts_ref[...] = jnp.zeros(parts_ref.shape, F32)

        def body(i, carry):
            cols = pl.ds(pl.multiple_of(i * 128, 128), 128)
            values = total_ref[:, cols] + bias + wide_ref[:, cols]
            center, scale = norm_stats(values)
            normed = (values - center) * scale
            result = (normed * gain + shift).astype(BF16)
            keep_ref[0, :, cols] = result[:feat]
            along_ref[0, :, cols] = result[feat : 2 * feat]
            close_ref[0, :, cols] = result[2 * feat : 3 * feat]
            along_ref[1, :, cols] = result[3 * feat :]
            pieces = (cot_keep, cot_got, cot_last)
            cot = jnp.concatenate([pieces[i][j, :, cols] for i, j in PIECES], axis=0).astype(F32)
            grad = norm_back(cot, normed, scale, gain)
            grad_ref[:, cols] = grad
            grad_low = grad.astype(BF16)
            low_ref[:, cols] = grad_low
            parts_ref[0] += grad_low.astype(F32)
            parts_ref[1] += cot * normed
            parts_ref[2] += cot
            return carry

        lax.fori_loop(0, chunks(own), body, 0)
        for i in range(3):
            sums_ref[:, i : i + 1] = jnp.sum(parts_ref[i], axis=1, keepdims=True)


def weight_block(array, which):
    return pl.BlockSpec((1, 1) + array.shape[2:], lambda step, *_: (which, step, 0, 0))


def mlp_forward(at, ctx, win, cot, out_t, near, far, bias):
    groups, depth, width = near.shape[1:]
    feat, own = cot[0].shape[1:]
    model = feat * 4
    outs = [
        jax.ShapeDtypeStruct((1, feat, own), BF16),
        jax.ShapeDtypeStruct((2, feat, own), BF16),
        jax.ShapeDtypeStruct((1, feat, own), BF16),
        jax.ShapeDtypeStruct((groups, width, own), BF16),
        jax.ShapeDtypeStruct((groups, width, own), BF16),
        jax.ShapeDtypeStruct((model, own), F32),
        jax.ShapeDtypeStruct((model, own), BF16),
        jax.ShapeDtypeStruct((model, own), BF16),
        jax.ShapeDtypeStruct((model, own), F32),
        jax.ShapeDtypeStruct((1, own), F32),
        jax.ShapeDtypeStruct((model, 3), F32),
    ]
    specs = [step_block(o) if i in (3, 4) else whole_block(o) for i, o in enumerate(outs)]
    return pl.pallas_call(
        functools.partial(mlp_forward_kernel, at),
        grid=(groups,),
        in_specs=[
            whole_block(ctx),
            whole_block(win),
            *[whole_block(piece) for piece in cot],
            whole_block(out_t),
            weight_block(near, 0),
            weight_block(far, 0),
            weight_block(near, 1),
            weight_block(far, 1),
            step_block(bias),
        ],
        out_specs=specs,
        out_shape=outs,
        scratch_shapes=[
            pltpu.VMEM((model, own), F32),
            pltpu.VMEM((model, own), F32),
            pltpu.VMEM((3, model, 128), F32),
        ],
        compiler_params=params(56),
        cost_estimate=cost(240),
        name="mlp_forward",
    )(ctx, win, *cot, out_t, near, far, near, far, bias)


def down_grad_kernel(low_ref, active_ref, keep_ref, send_ref):
    grads = nt(low_ref[...], active_ref[0]).astype(BF16)
    depth = keep_ref.shape[1]
    keep_ref[0] = grads[:depth]
    send_ref[0] = grads[depth:]


def down_grads(low, active):
    groups, width, own = active.shape
    out = jax.ShapeDtypeStruct((groups, low.shape[0] // 2, width), BF16)
    return pl.pallas_call(
        down_grad_kernel,
        grid=(groups,),
        in_specs=[whole_block(low), step_block(active)],
        out_specs=[step_block(out)] * 2,
        out_shape=[out] * 2,
        compiler_params=params(32),
        cost_estimate=cost(50),
        name="down_grads",
    )(low, active)


def mlp_backward_kernel(
    at,
    low_ref,
    slope_ref,
    hidden_ref,
    near_up,
    far_up,
    near_down,
    far_down,
    grad_ref,
    normed_ref,
    scale_ref,
    win_ref,
    out_ref,
    keep_ref,
    send_ref,
    first_ref,
    first_low_ref,
    dctx_ref,
    bias_ref,
    sums_ref,
    total_ref,
    parts_ref,
):
    step, last = pl.program_id(0), pl.num_programs(0) - 1
    depth = near_up.shape[2]
    model, own = low_ref.shape

    @pl.when(step == 0)
    def start():
        total_ref[...] = grad_ref[...]

    upper = tn(near_down[0, 0], low_ref[:depth]) + tn(far_down[0, 0], low_ref[depth:])
    upper = (upper * slope_ref[0].astype(F32)).astype(BF16)
    bias_ref[0] = jnp.sum(upper.astype(F32), axis=1, keepdims=True)
    total_ref[:depth] += nn(near_up[0, 0], upper)
    total_ref[depth:] += nn(far_up[0, 0], upper)
    keep_ref[0] = nt(hidden_ref[:depth], upper).astype(BF16)
    send_ref[0] = nt(hidden_ref[depth:], upper).astype(BF16)

    @pl.when(step == last)
    def finish():
        gain = win_ref[:, at + 1 : at + 2].astype(F32)
        parts_ref[...] = jnp.zeros(parts_ref.shape, F32)

        def body(i, carry):
            cols = pl.ds(pl.multiple_of(i * 128, 128), 128)
            hidden_grad = total_ref[:, cols]
            normed = normed_ref[:, cols]
            first = norm_back(hidden_grad, normed, scale_ref[:, cols], gain)
            first_ref[:, cols] = first
            first_low = first.astype(BF16)
            first_low_ref[:, cols] = first_low
            parts_ref[0] += first_low.astype(F32)
            parts_ref[1] += hidden_grad * normed
            parts_ref[2] += hidden_grad
            return carry

        lax.fori_loop(0, chunks(own), body, 0)
        for i in range(3):
            sums_ref[:, i : i + 1] = jnp.sum(parts_ref[i], axis=1, keepdims=True)
        dctx_ref[...] = tn(out_ref[...], first_low_ref[...]).astype(BF16)


def mlp_backward(at, low, slope, hidden, near, far, grad, normed, scale, win, out_t):
    groups, depth, width = near.shape[1:]
    model, own = low.shape
    outs = [
        jax.ShapeDtypeStruct((groups, depth, width), BF16),
        jax.ShapeDtypeStruct((groups, depth, width), BF16),
        jax.ShapeDtypeStruct((model, own), F32),
        jax.ShapeDtypeStruct((model, own), BF16),
        jax.ShapeDtypeStruct((out_t.shape[1], own), BF16),
        jax.ShapeDtypeStruct((groups, width, 1), F32),
        jax.ShapeDtypeStruct((model, 3), F32),
    ]
    specs = [step_block(o) if i in (0, 1, 5) else whole_block(o) for i, o in enumerate(outs)]
    return pl.pallas_call(
        functools.partial(mlp_backward_kernel, at),
        grid=(groups,),
        in_specs=[
            whole_block(low),
            step_block(slope),
            whole_block(hidden),
            weight_block(near, 0),
            weight_block(far, 0),
            weight_block(near, 1),
            weight_block(far, 1),
            whole_block(grad),
            whole_block(normed),
            whole_block(scale),
            whole_block(win),
            whole_block(out_t),
        ],
        out_specs=specs,
        out_shape=outs,
        scratch_shapes=[pltpu.VMEM((model, own), F32), pltpu.VMEM((3, model, 128), F32)],
        compiler_params=params(56),
        cost_estimate=cost(240),
        name="mlp_backward",
    )(low, slope, hidden, near, far, near, far, grad, normed, scale, win, out_t)


def first_grad_kernel(
    width, win_ref, par_ref, dwin_ref, dpar_ref, low_ref, ctx_ref, up_ref, first_ref, last_ref, keep_ref, send_ref
):
    depth = keep_ref.shape[1]
    half = depth // 4
    query = jnp.sum(dwin_ref[0, :width].astype(F32), axis=1, keepdims=True)
    value = jnp.sum(dwin_ref[0, 2 * width :].astype(F32), axis=1, keepdims=True)
    value = value + jnp.sum(dpar_ref[0, width:].astype(F32), axis=1, keepdims=True)
    by_row = [array[i : i + half] for array in (query, value, up_ref[0]) for i in range(0, array.shape[0], half)]
    by_row = jnp.concatenate(by_row, axis=1)
    by_row = jnp.concatenate([by_row] * 4, axis=0)
    used = by_row.shape[1] + 6
    pad = jnp.zeros((depth, keep_ref.shape[2] - 4 * width - used), F32)
    for part, out_ref in enumerate((keep_ref, send_ref)):
        rows = slice(part * depth, (part + 1) * depth)
        win, par = win_ref[rows], par_ref[rows]
        out_ref[0, :, :width] = nt(win, dwin_ref[0, :width]).astype(BF16)
        for i in range(1, 3):
            grads = nt(win, dwin_ref[0, i * width : (i + 1) * width])
            grads = grads + nt(par, dpar_ref[0, (i - 1) * width : i * width])
            out_ref[0, :, i * width : (i + 1) * width] = grads.astype(BF16)
        out_ref[0, :, 3 * width : 4 * width] = nt(low_ref[rows], ctx_ref[0]).astype(BF16)
        extra = jnp.concatenate([by_row, first_ref[rows], last_ref[rows], pad], axis=1)
        out_ref[0, :, 4 * width :] = extra.astype(BF16)


def first_grads(win, par, dwin, dpar, low, ctx, up_bias, first_sums, last_sums):
    groups, width, own = ctx.shape
    out = jax.ShapeDtypeStruct((groups, low.shape[0] // 2, 4 * width + 128), BF16)
    return pl.pallas_call(
        functools.partial(first_grad_kernel, width),
        grid=(groups,),
        in_specs=[
            whole_block(win),
            whole_block(par),
            step_block(dwin),
            step_block(dpar),
            whole_block(low),
            step_block(ctx),
            step_block(up_bias),
            whole_block(first_sums),
            whole_block(last_sums),
        ],
        out_specs=[step_block(out)] * 2,
        out_shape=[out] * 2,
        compiler_params=params(40),
        cost_estimate=cost(120),
        name="first_grads",
    )(win, par, dwin, dpar, low, ctx, up_bias, first_sums, last_sums)


def token_grad_kernel(low, high, parent, near_ref, far_ref, dwin_ref, more_ref, keep_ref, along_ref, close_ref, total_ref):
    step, last = pl.program_id(0), pl.num_programs(0) - 1
    depth = near_ref.shape[1]
    columns = total_ref.shape[1]
    own = more_ref.shape[1]

    @pl.when(step == 0)
    def start():
        total_ref[...] = jnp.zeros(total_ref.shape, F32)
        if not parent:
            total_ref[:, :own] = more_ref[...]

    if parent:
        grads = jnp.concatenate([more_ref[0], dwin_ref[0, low:high, more_ref.shape[2] :]], axis=1)
    else:
        grads = dwin_ref[0, low:high, :columns]
    total_ref[:depth] += nn(near_ref[0, :, low:high], grads)
    total_ref[depth:] += nn(far_ref[0, :, low:high], grads)

    @pl.when(step == last)
    def finish():
        feat = keep_ref.shape[1]
        for i, out in enumerate((keep_ref.at[0], along_ref.at[0], close_ref.at[0], along_ref.at[1])):
            out[...] = total_ref[i * feat : (i + 1) * feat].astype(BF16)


def token_grads(near, far, dwin, more, low, high, parent, columns):
    groups, depth = near.shape[:2]
    feat = depth // 2
    outs = [jax.ShapeDtypeStruct((n, feat, columns), BF16) for n in (1, 2, 1)]
    return pl.pallas_call(
        functools.partial(token_grad_kernel, low, high, parent),
        grid=(groups,),
        in_specs=[
            step_block(near),
            step_block(far),
            step_block(dwin),
            step_block(more) if parent else whole_block(more),
        ],
        out_specs=[whole_block(out) for out in outs],
        out_shape=outs,
        scratch_shapes=[pltpu.VMEM((2 * depth, columns), F32)],
        compiler_params=params(40),
        cost_estimate=cost(50),
        name="token_grads",
    )(near, far, dwin, more)


def attend(lengths, segments, bank, scalars, window, parent):
    groups, rows, columns = window.shape
    width = rows // 3
    heads = width // HEAD
    outs = (
        jax.ShapeDtypeStruct((groups, width, sum(lengths)), BF16),
        jax.ShapeDtypeStruct((groups, heads, sum(lengths)), F32),
    )
    return pl.pallas_call(
        functools.partial(attention_forward, heads, lengths, segments, bank),
        grid=(groups,),
        in_specs=[SMEM] * 3 + [step_block(window), step_block(parent)],
        out_specs=[step_block(out) for out in outs],
        out_shape=outs,
        compiler_params=params(40),
        cost_estimate=cost(130),
        name="attention_forward",
    )(*scalars, window, parent)


def attend_back(lengths, segments, bank, scalars, window, parent, dctx, lse):
    groups, rows, columns = window.shape
    outs = (jax.ShapeDtypeStruct(window.shape, BF16), jax.ShapeDtypeStruct(parent.shape, BF16))
    return pl.pallas_call(
        functools.partial(attention_backward, rows // 3 // HEAD, lengths, segments, bank),
        grid=(groups,),
        in_specs=[SMEM] * 3 + [step_block(window), step_block(parent), step_block(dctx), step_block(lse)],
        out_specs=[step_block(out) for out in outs],
        out_shape=outs,
        compiler_params=params(40),
        cost_estimate=cost(200),
        name="attention_backward",
    )(*scalars, window, parent, dctx, lse)


def swap(array, axis, mask):
    count = lax.axis_size(axis)
    return lax.ppermute(array, axis, [(i, i ^ mask) for i in range(count)])


SMEM = pl.BlockSpec(memory_space=pltpu.SMEM)
VMEM = pl.BlockSpec(memory_space=pltpu.VMEM)
ORDER = (0, 2, 1, 3)
SENDS = ((0, 0), (1, 0), (2, 0), (1, 1))


def at_distance(here_ref, lists, slot, j):
    distance = ORDER[slot]
    return static_of(here_ref[1], [lists[i ^ distance][j] for i in range(len(lists))])


def flipped(here_ref, part, half):
    return pl.multiple_of((part ^ here_ref[2]) * half, 32)


def spots(rows, columns, shift):
    return (
        lax.broadcasted_iota(jnp.int32, (rows, columns), 0) + shift
        == lax.broadcasted_iota(jnp.int32, (rows, columns), 1)
    ).astype(BF16)


def pack_weights_kernel(
    here_ref,
    query_ref,
    key_ref,
    value_ref,
    out_ref,
    up_ref,
    down_ref,
    up_b_ref,
    query_b_ref,
    value_b_ref,
    half_ref,
    turned_ref,
):
    feat, width = query_ref.shape
    half = feat // 2
    rows = pl.ds(flipped(here_ref, 0, half), half)
    turned_ref[...] = tn(out_ref[...], spots(width, width, 0)).astype(BF16)
    for i, ref in enumerate((query_ref, key_ref, value_ref, turned_ref)):
        half_ref[:half, i * width : (i + 1) * width] = ref[rows, :]
    half_ref[half : 2 * half] = up_ref[rows, :]
    half_ref[2 * half : 3 * half] = down_ref[rows, :]
    zero = jnp.zeros((1, width), F32)
    joint = [query_b_ref[...].astype(F32), zero, value_b_ref[...].astype(F32), zero]
    wide = (half_ref.shape[0] - 3 * half, half_ref.shape[1])
    index = lax.broadcasted_iota(jnp.int32, wide, 0)
    up_row = jnp.broadcast_to(up_b_ref[...].astype(F32), wide)
    joint_row = jnp.broadcast_to(jnp.concatenate(joint, axis=1), wide)
    half_ref[3 * half :] = jnp.where(index == 0, up_row, jnp.where(index == 1, joint_row, 0.0)).astype(BF16)


def pack_weights(here, query, key, value, out, up, down, *biases):
    feat, width = query.shape
    hidden = up.shape[1]
    return pl.pallas_call(
        pack_weights_kernel,
        in_specs=[SMEM] + [VMEM] * 9,
        out_specs=VMEM,
        out_shape=jax.ShapeDtypeStruct((3 * feat // 2 + 16, hidden), BF16),
        scratch_shapes=[pltpu.VMEM((feat, width), BF16)],
        compiler_params=params(24),
        cost_estimate=cost(0.1),
        name="pack_weights",
    )(here, query, key, value, out, up, down, *[bias.reshape(1, -1) for bias in biases])


def pack_kernel(blocks, sided, here_ref, source_ref, *refs):
    half = source_ref.shape[0] // 2
    count = len(blocks[0])
    outs = refs[2:5] if sided else refs
    if sided:
        mem_ref, vec_ref, side_ref = refs[0], refs[1], refs[5]
        bank = mem_ref.shape[0]
        side = tn(mem_ref[...], spots(bank, 128, 0)) + tn(vec_ref[...], spots(vec_ref.shape[0], 128, bank))
        side_ref[...] = side.astype(BF16)
    for slot, (out, place) in enumerate(SENDS):
        for part in range(2):
            low = flipped(here_ref, part, half)
            rows = slice(part * half, (part + 1) * half)
            for j in range(count):
                at = pl.multiple_of(at_distance(here_ref, blocks, slot, j) * 128, 128)
                outs[out][place, rows, j * 128 : (j + 1) * 128] = source_ref[pl.ds(low, half), pl.ds(at, 128)]
            if sided:
                outs[out][place, rows, count * 128 :] = side_ref[pl.ds(low, half), :]


def pack(blocks, here, source, *side):
    feat = source.shape[0]
    columns = len(blocks[0]) * 128 + (128 if side else 0)
    return pl.pallas_call(
        functools.partial(pack_kernel, blocks, bool(side)),
        in_specs=[SMEM] + [VMEM] * (1 + len(side)),
        out_specs=[VMEM] * 3,
        out_shape=[jax.ShapeDtypeStruct((n, feat, columns), source.dtype) for n in (1, 2, 1)],
        scratch_shapes=[pltpu.VMEM((feat, 128), BF16)] if side else [],
        compiler_params=params(24),
        cost_estimate=cost(0.1),
        name="pack",
    )(here, source, *side)


def exchange(keep, along, near):
    got = swap(along, "col", 2)
    return keep, got, swap(jnp.concatenate([near, got[1:]], axis=0), "col", 1)


def joined(pieces):
    keep, got, last = pieces
    return jnp.concatenate([keep, got[:1], last], axis=0)


PIECES = ((0, 0), (1, 0), (2, 0), (2, 1))


def parent_of(here_ref, parents_ref, segments, slot, j):
    return parents_ref[here_ref[0] * here_ref[3] + at_distance(here_ref, segments, slot, j)]


def pick_kernel(segments, here_ref, parents_ref, source_ref, *outs):
    half = source_ref.shape[1] // 2
    seg_row = here_ref[3]
    for slot, (out, place) in enumerate(SENDS):
        for j in range(len(segments[0])):
            seg = jnp.maximum(parent_of(here_ref, parents_ref, segments, slot, j), 0)
            row = lax.div(seg, seg_row)
            at = pl.multiple_of((seg - row * seg_row) * SEG, SEG)
            for part in range(2):
                rows = slice(part * half, (part + 1) * half)
                outs[out][place, rows, j * SEG : (j + 1) * SEG] = source_ref[
                    row, pl.ds(flipped(here_ref, part, half), half), pl.ds(at, SEG)
                ]


def pick_parents(segments, here, parents, gathered):
    feat = gathered.shape[1]
    columns = len(segments[0]) * SEG
    return pl.pallas_call(
        functools.partial(pick_kernel, segments),
        in_specs=[SMEM, SMEM, VMEM],
        out_specs=[VMEM] * 3,
        out_shape=[jax.ShapeDtypeStruct((n, feat, columns), gathered.dtype) for n in (1, 2, 1)],
        compiler_params=params(24),
        cost_estimate=cost(1),
        name="pick_parents",
    )(here, parents, gathered)


def add_parents_kernel(segments, seg_row, here_ref, parents_ref, *refs):
    pieces, out_ref, sum_ref = refs[:3], refs[3], refs[4]
    window = len(segments[0]) * SEG
    sum_ref[...] = jnp.zeros(sum_ref.shape, F32)
    for slot, (piece, place) in enumerate(PIECES):
        for j in range(len(segments[0])):
            seg = parent_of(here_ref, parents_ref, segments, slot, j)

            @pl.when(seg >= 0)
            def add(seg=seg, piece=piece, place=place, cols=slice(j * SEG, (j + 1) * SEG)):
                sum_ref[seg] += pieces[piece][place, :, cols].astype(F32)

    mem = sum(pieces[piece][place, :, window:].astype(F32) for piece, place in PIECES)
    for r in range(out_ref.shape[0]):
        for s in range(seg_row):
            out_ref[r, :, s * SEG : (s + 1) * SEG] = sum_ref[r * seg_row + s].astype(BF16)
        out_ref[r, :, seg_row * SEG :] = mem.astype(BF16)


def add_parents(segments, here, parents, pieces, rows, seg_row):
    feat, columns = pieces[0].shape[1:]
    bank = columns - len(segments[0]) * SEG
    return pl.pallas_call(
        functools.partial(add_parents_kernel, segments, seg_row),
        in_specs=[SMEM, SMEM, VMEM, VMEM, VMEM],
        out_specs=VMEM,
        out_shape=jax.ShapeDtypeStruct((rows, feat, seg_row * SEG + bank), BF16),
        scratch_shapes=[pltpu.VMEM((rows * seg_row, feat, SEG), F32)],
        compiler_params=params(40),
        cost_estimate=cost(20),
        name="add_parents",
    )(here, parents, *pieces)


def finish_kernel(blocks, here_ref, placed_ref, *refs):
    pieces, out_ref = refs[:3], refs[3]
    half = out_ref.shape[0] // 2
    for part in range(2):
        low = flipped(here_ref, part, half)
        rows = slice(part * half, (part + 1) * half)
        out_ref[pl.ds(low, half), :] = placed_ref[rows, : out_ref.shape[1]].astype(F32)
        for slot, (piece, place) in enumerate(PIECES):
            for j in range(len(blocks[0])):
                at = pl.multiple_of(at_distance(here_ref, blocks, slot, j) * 128, 128)
                out_ref[pl.ds(low, half), pl.ds(at, 128)] += pieces[piece][
                    place, rows, j * 128 : (j + 1) * 128
                ].astype(F32)


def finish_tokens(blocks, here, placed, pieces, columns):
    return pl.pallas_call(
        functools.partial(finish_kernel, blocks),
        in_specs=[SMEM, VMEM, VMEM, VMEM, VMEM],
        out_specs=VMEM,
        out_shape=jax.ShapeDtypeStruct((placed.shape[0], columns), F32),
        compiler_params=params(24),
        cost_estimate=cost(2.5),
        name="finish_tokens",
    )(here, placed, *pieces)


def place_kernel(blocks, here_ref, *refs):
    pieces, out_ref = refs[:3], refs[3]
    half = out_ref.shape[0] // 2
    for part in range(2):
        low = flipped(here_ref, part, half)
        rows = slice(part * half, (part + 1) * half)
        for slot, (piece, place) in enumerate(PIECES):
            for j in range(pieces[0].shape[2] // 128):
                at = pl.multiple_of(at_distance(here_ref, blocks, slot, j) * 128, 128)
                out_ref[pl.ds(low, half), pl.ds(at, 128)] = pieces[piece][place, rows, j * 128 : (j + 1) * 128]


def place(blocks, here, pieces, columns):
    return pl.pallas_call(
        functools.partial(place_kernel, blocks),
        in_specs=[SMEM, VMEM, VMEM, VMEM],
        out_specs=VMEM,
        out_shape=jax.ShapeDtypeStruct((pieces[0].shape[1], columns), pieces[0].dtype),
        compiler_params=params(24),
        cost_estimate=cost(1.7),
        name="place",
    )(here, *pieces)


def gather_weights(half):
    return [half] + [swap(half, "row", n) for n in range(1, lax.axis_size("row"))]


def spread_weights(along):
    along = jnp.stack(along, axis=1)
    opposite = swap(along, "leaf", 1)
    across = swap(along, "col", 2)
    return along, opposite, across, swap(across, "leaf", 1)


def whole_weights(parts):
    near = jnp.stack(parts, axis=2)
    arrays, rows, blocks, depth, columns = near.shape
    near = near.reshape(arrays, rows, blocks * depth, columns)
    return near, swap(near, "col", 1)


def add_up(*terms):
    total = terms[0].astype(F32)
    for term in terms[1:]:
        total = total + term.astype(F32)
    return total


def reduce_blocks(keep):
    rows, features, columns = keep.shape
    return rows, 2, 2, features // 4, columns


def reduce_across(keep, near):
    shape = reduce_blocks(keep)
    return add_up(keep.reshape(shape)[:, :, 1], near.reshape(shape)[:, :, 1]).astype(BF16)


def reduce_up(keep, near, across):
    shape = reduce_blocks(keep)
    return add_up(keep.reshape(shape)[:, 1, 0], near.reshape(shape)[:, 1, 0], across[:, 1]).astype(BF16)


def reduce_along(keep, near, across, up):
    shape = reduce_blocks(keep)
    mine = add_up(keep.reshape(shape)[:, 0, 0], near.reshape(shape)[:, 0, 0], across[:, 0], up)
    return [mine[n].astype(BF16) for n in range(shape[0])]


def reduce_rows(along, got):
    total = add_up(along[0], *got)
    mask = 2
    while mask < lax.axis_size("leaf"):
        total = add_up(total, swap(total.astype(BF16), "leaf", mask))
        mask *= 2
    return total.astype(BF16)


def reduce_corner(keep, near):
    shape = reduce_blocks(keep)
    middle = shape[0] // 2
    corner = add_up(keep.reshape(shape)[:, 1, 1], near.reshape(shape)[:, 1, 1]).astype(BF16)
    return corner[:middle], corner[middle:]


def reduce_edges(keep, near, by_leaf, by_col):
    shape = reduce_blocks(keep)
    middle = shape[0] // 2
    keep, near = keep.reshape(shape), near.reshape(shape)
    leaf = add_up(keep[:, 0, 1], near[:, 0, 1])
    leaf = jnp.concatenate([leaf[:middle], add_up(leaf[middle:], by_col)], axis=0).astype(BF16)
    along = add_up(keep[:, 1, 0], near[:, 1, 0])
    along = jnp.concatenate([add_up(along[:middle], by_leaf), along[middle:]], axis=0).astype(BF16)
    return leaf, along


def reduce_mine(keep, near, leaf, along):
    shape = reduce_blocks(keep)
    mine = add_up(keep.reshape(shape)[:, 0, 0], near.reshape(shape)[:, 0, 0], leaf, along)
    return [mine[n].astype(BF16) for n in range(shape[0])]


def send_rows(along):
    return [swap(block, "row", n) for n, block in enumerate(along) if n]


def norm_stats(values):
    center = jnp.mean(values, axis=0, keepdims=True)
    spread = jnp.mean(values * values, axis=0, keepdims=True) - center * center
    return center, lax.rsqrt(spread + EPSILON)


def norm_back(grad, normed, scale, gain):
    scaled = grad * gain
    return scale * (
        scaled
        - jnp.mean(scaled, axis=0, keepdims=True)
        - normed * jnp.mean(scaled * normed, axis=0, keepdims=True)
    )


def lane_sum(array):
    return jnp.sum(array, axis=-1, dtype=F32)


def on_device(
    tokens,
    memory,
    parents,
    memory_slots,
    query_weight,
    query_bias,
    key_weight,
    value_weight,
    value_bias,
    out_weight,
    out_bias,
    norm_gain,
    norm_shift,
    up_weight,
    up_bias,
    down_weight,
    down_bias,
    final_gain,
    final_shift,
    cotangent,
):
    rows, cols = lax.axis_size("row"), lax.axis_size("col")
    row, col = lax.axis_index("row"), lax.axis_index("col")
    feat, row_tokens = tokens.shape
    own = row_tokens // cols
    seg_row = row_tokens // SEG
    model = feat * cols
    width = query_weight.shape[1]
    hidden_width = up_weight.shape[1]
    bank = memory.shape[0]
    segments, ranges = plan_windows(own, cols)
    window = len(segments[0]) * SEG
    tail = 128
    lengths = tuple(min(SEG, own - j * SEG) for j in range(len(segments[0])))
    half = feat // 2
    parity = lax.axis_index("leaf") % 2
    here = jnp.stack([row, col, parity, jnp.int32(seg_row)]).astype(jnp.int32)
    blocks = [[b for a, n in ranges[i] for b in range(a // 128, (a + n) // 128)] for i in range(cols)]
    own_blocks = [each[: own // 128] for each in blocks]
    scalars = (here, parents, memory_slots)

    weight_half = pack_weights(
        here, query_weight, key_weight, value_weight, out_weight, up_weight, down_weight, up_bias, query_bias, value_bias
    )
    along = gather_weights(weight_half)

    zero = jnp.zeros((feat,), BF16)
    vectors = jnp.stack([out_bias, norm_gain, norm_shift, down_bias, final_gain, final_shift, zero, zero])
    token_sends = pack(blocks, here, after(tokens, weight_half), memory, vectors)
    cot_sends = pack(own_blocks, here, after(cotangent, token_sends))
    token_got = swap(token_sends[1], "col", 2)
    along = after(along, cot_sends, token_got)
    everything = lax.all_gather(after(tokens, along), "row", axis=0)
    row_vectors = jnp.stack([piece[3 * half :] for piece in along])
    near_first, far_first = (array[0] for array in whole_weights(spread_weights([piece[:half][None] for piece in along])))
    token_last = swap(jnp.concatenate([token_sends[2], token_got[1:]], axis=0), "col", 1)
    tok_window = joined((token_sends[0], token_got, token_last)).reshape(model, window + tail)
    second_parts = spread_weights([piece[half : 3 * half].reshape(2, half, -1) for piece in along])
    win = project(near_first, far_first, tok_window, row_vectors, 0, 3 * width, width)
    out_t = jnp.concatenate([near_first[:, :, 3 * width :], far_first[:, :, 3 * width :]], axis=1)
    out_t = out_t.transpose(1, 0, 2).reshape(model, rows * width)
    everything = after(everything, win, out_t, second_parts[2])
    par_keep, par_along, par_near = pick_parents(segments, here, parents, everything)
    par_got = swap(par_along, "col", 2)
    near, far = whole_weights(after(second_parts, par_along))
    par_got = after(par_got, near)
    par_near = jnp.concatenate([par_near, par_got[1:]], axis=0)
    tok_parent = joined((par_keep, par_got, swap(par_near, "col", 1))).reshape(model, window)
    par = project(near_first, far_first, tok_parent, row_vectors, width, 3 * width, 0)
    cot_keep, cot_along, cot_near = after(cot_sends, par_near)
    cot_got = swap(cot_along, "col", 2)
    ctx, lse = attend(lengths, segments, bank, scalars, win, par)
    cot_got = after(cot_got, ctx)
    cot_pieces = cot_keep, cot_got, swap(jnp.concatenate([cot_near, cot_got[1:]], axis=0), "col", 1)
    at = window + bank
    *result, active, slope, second_grad, down_low, hidden_low, normed, scale, last_sums = mlp_forward(
        at, ctx.reshape(rows * width, own), tok_window, cot_pieces, out_t, near, far, row_vectors
    )
    down_keep, down_send = down_grads(down_low, active)
    up_keep, up_send, first_grad, first_low, dctx, up_bias_grad, first_sums = mlp_backward(
        at, after(down_low, down_send), slope, hidden_low, near, far, second_grad, normed, scale, tok_window, out_t
    )
    down_near, up_near = swap(down_send, "col", 1), swap(up_send, "col", 1)
    down_across = reduce_across(after(down_keep, dctx), down_near)
    up_across = reduce_across(after(up_keep, down_across), up_near)
    dctx = after(dctx, down_across, up_across).reshape(rows, width, own)
    dwin, dpar = attend_back(lengths, segments, bank, scalars, win, par, dctx, lse)

    dtok_par = token_grads(near_first, far_first, dwin, dpar, width, 3 * width, True, window + tail)
    par_keep, par_along, par_near = dtok_par
    par_got = swap(par_along, "col", 2)
    first_low = after(first_low, par_along)
    first_keep, first_send = first_grads(
        tok_window, tok_parent, dwin, dpar, first_low, ctx, up_bias_grad, first_sums, last_sums
    )
    par_got = after(par_got, first_send)
    par_near = jnp.concatenate([par_near, par_got[1:]], axis=0)
    first_near = swap(first_send, "col", 1)
    down_across = swap(down_across, "leaf", 1)
    down_up = reduce_up(after(down_keep, par_near), down_near, down_across)
    par_last = after(swap(par_near, "col", 1), down_up)
    placed = add_parents(segments, here, parents, (par_keep, par_got, par_last), rows, seg_row)
    corner = reduce_corner(after(first_keep, placed), first_near)
    by_leaf, by_col = swap(corner[0], "leaf", 1), swap(corner[1], "col", 2)
    dtok = token_grads(near_first, far_first, dwin, after(first_grad, corner), 0, 3 * width, False, window)
    placed = lax.psum_scatter(placed, "row", scatter_dimension=0, tiled=False)
    edges = reduce_edges(after(first_keep, dtok), first_near, by_leaf, by_col)
    by_leaf, by_col = swap(edges[0], "leaf", 1), swap(edges[1], "col", 2)
    up_across = swap(up_across, "leaf", 1)
    up_up = reduce_up(after(up_keep, edges), up_near, up_across)
    down_up = swap(down_up, "col", 2)
    down_rows = reduce_along(after(down_keep, up_up), down_near, down_across, down_up)
    up_up = swap(up_up, "col", 2)
    up_rows = reduce_along(after(up_keep, down_rows), up_near, up_across, up_up)
    first_rows = reduce_mine(after(first_keep, up_rows), first_near, by_leaf, by_col)
    result_pieces = exchange(*after(result, first_rows))
    down_got, up_got, first_got = send_rows(down_rows), send_rows(up_rows), send_rows(first_rows)
    second_mine = jnp.concatenate([reduce_rows(down_rows, down_got), reduce_rows(up_rows, up_got)], axis=1)
    second_other = swap(second_mine, "leaf", 1)
    first_mine = reduce_rows(after(first_rows, second_mine), first_got)
    first_other = swap(first_mine, "leaf", 1)
    layer_output = place(own_blocks, here, result_pieces, row_tokens)

    def in_order(mine, other):
        return jnp.where(
            parity == 0, jnp.concatenate([mine, other], axis=0), jnp.concatenate([other, mine], axis=0)
        ).astype(F32)

    second_total, first_total = in_order(second_mine, second_other), in_order(first_mine, first_other)
    down_total, up_total = second_total[:, :hidden_width], second_total[:, hidden_width:]
    count = (2 * width + hidden_width) // half
    by_row = first_mine[:, 4 * width : 4 * width + count].astype(F32).T.reshape(-1)
    by_col = first_total[:, 4 * width + count : 4 * width + count + 6].T

    mem_sum = placed[:, row_tokens : row_tokens + bank].astype(F32)
    memory_grad = jnp.where(parity == 0, mem_sum, jnp.roll(mem_sum, half, axis=0)).T
    tokens_grad = finish_tokens(blocks, here, placed, exchange(*dtok), row_tokens)

    return (
        layer_output,
        tokens_grad,
        memory_grad,
        first_total[:, :width],
        by_row[:width],
        first_total[:, width : 2 * width],
        first_total[:, 2 * width : 3 * width],
        by_row[width : 2 * width],
        first_total[:, 3 * width : 4 * width].T,
        by_col[0],
        by_col[1],
        by_col[2],
        up_total,
        by_row[2 * width :],
        down_total,
        by_col[3],
        by_col[4],
        by_col[5],
    )


def solution(mesh):
    return jax.shard_map(
        on_device,
        mesh=mesh,
        in_specs=(
            P("col", ("leaf", "row")),
            P("leaf", "col"),
            P("leaf"),
            P("leaf", None),
            P("col", "row"),
            P("row"),
            P("col", "row"),
            P("col", "row"),
            P("row"),
            P("row", "col"),
            P("col"),
            P("col"),
            P("col"),
            P("col", "row"),
            P("row"),
            P("col", "row"),
            P("col"),
            P("col"),
            P("col"),
            P("col", ("leaf", "row")),
        ),
        out_specs=(
            P("col", ("leaf", "row")),
            P("col", ("leaf", "row")),
            P("leaf", "col"),
            P("col", "row"),
            P("row"),
            P("col", "row"),
            P("col", "row"),
            P("row"),
            P("row", "col"),
            P("col"),
            P("col"),
            P("col"),
            P("col", "row"),
            P("row"),
            P("col", "row"),
            P("col"),
            P("col"),
            P("col"),
        ),
        check_vma=False,
    )
```

time: 684 us -> 458 us (0.67)
  waiting for transfers between devices: 375 us -> 167 us
  Pallas kernels: 43 us -> 130 us
  matrix products: 83.2 us -> 0 us
  blocking collectives: 46.3 us -> 0 us
  starting transfers between devices: 20.1 us -> 48.8 us
  other arithmetic: 50.1 us -> 36.7 us
  local copies, waits for them, and re-layouts: 41 us -> 53.9 us
    reduce_scatter x4 -> x1, waiting for transfers between devices: 204 us -> 0.01 us  [on_device(): placed = lax.psum_scatter(placed, 'row', scatter_dimension=0, tiled=False)]
    ppermute x0 -> x45, waiting for transfers between devices: none -> 167 us  [swap(): return lax.ppermute(array, axis, [(i, i ^ mask) for i in range(count)])]
    all_gather x4 -> x1, waiting for transfers between devices: 154 us -> 0.01 us  [on_device(): everything = lax.all_gather(after(tokens, along), 'row', axis=0)]
    pallas_call x4 -> x17, Pallas kernels: 43 us -> 130 us  [the longest x1 24.7 us: mlp_forward(): pl.pallas_call(functools.partial(mlp_forward_kernel, at), grid=(groups,),...]
    dot_general x15 -> x0, matrix products: 83.2 us -> none  [the longest x4 25.6 us: project(): return jnp.einsum('rdf,dt->rft', block, toks, preferred_element_type=F32)]
    ppermute x0 -> x45, starting transfers between devices: none -> 48.7 us  [swap(): return lax.ppermute(array, axis, [(i, i ^ mask) for i in range(count)])]
    psum x1 -> x0, blocking collectives: 46.3 us -> none  [on_device(): lax.psum(jnp.concatenate([query_bias_grad, value_bias_grad, out_bias_grad...]
    all_to_all x5 -> x0, starting transfers between devices: 19.5 us -> none  [exchange(): return lax.all_to_all(blocks, 'col', 0, 0, tiled=True)]
  transfers between devices with their start and end apart: 14 -> 47, of which waited for: 8 -> 18; matrix products, arithmetic and copies ran while one was open for 17% -> 11% of each run, Pallas kernels for 6% -> 21%
where the time goes in v2:
time: 458 us; the launch traced here: 452 us
  waiting for transfers between devices  167 us (36%)
  Pallas kernels  130 us (28%)
  local copies, waits for them, and re-layouts  53.9 us (12%)
  starting transfers between devices  48.8 us (11%)
  other arithmetic  36.7 us (8%)
  between operations  15.5 us (3%)
    ppermute x45, waiting for transfers between devices, swap(): return lax.ppermute(array, axis, [(i, i ^ mask) for i in range(count)])  167 us
    ppermute x45, starting transfers between devices, swap(): return lax.ppermute(array, axis, [(i, i ^ mask) for i in range(count)])  48.7 us
    unnamed x135, local copies, waits for them, and re-layouts  33.4 us
    pallas_call x1, Pallas kernels, mlp_forward(): pl.pallas_call(functools.partial(mlp_forward_kernel, at), grid=(groups,),...  24.7 us
    pallas_call x1, Pallas kernels, mlp_backward(): pl.pallas_call(functools.partial(mlp_backward_kernel, at), grid=(groups,)...  23.9 us
    pallas_call x1, Pallas kernels, attend_back(): pl.pallas_call(functools.partial(attention_backward, rows // 3 // HEAD, l...  20 us
    pallas_call x1, Pallas kernels, attend(): pl.pallas_call(functools.partial(attention_forward, heads, lengths, segme...  13.6 us
    pallas_call x1, Pallas kernels, first_grads(): pl.pallas_call(functools.partial(first_grad_kernel, width), grid=(groups,...  12.4 us
  transfers between devices with their start and end apart: 47, of which 18 were waited for; matrix products, arithmetic and copies ran while one was open for 11% of the time, Pallas kernels for 21%

profile of v2, /device:TPU:0, one launch (start us, length us, event | category | flops | bytes accessed | tf_op | source)
XLA Modules:
  0.0 451.8 jit_solution(4107526292910429170)
XLA Ops:
  20.7 3.0 collective-permute-start.3
  23.8 3.6 collective-permute-start.2
  29.0 10.3 %collective-permute-done.2 = bf16[304,768]{1,0:T(8,128)(2,1)S(1)} collective-permute-done((bf16[304,768]{1,0:T(8,128)(2,1)S(1)}, bf16[304,768]{1,0:T(8,128)(2,1)S(1)}, u32[]{:S(2)}, u32[]{:S(2)}) %collective-permute-start.2) | collective-permute-done | bytes 466976 | tf_op jit(solution)/shard_map/ppermute | solution.py:641
  39.3 27.7 %collective-permute-done.1 = bf16[304,768]{1,0:T(8,128)(2,1)S(1)} collective-permute-done((bf16[304,768]{1,0:T(8,128)(2,1)S(1)}, bf16[304,768]{1,0:T(8,128)(2,1)S(1)}, u32[]{:S(2)}, u32[]{:S(2)}) %collective-permute-start.1) | collective-permute-done | bytes 466976 | tf_op jit(solution)/shard_map/ppermute | solution.py:641
  72.1 12.3 %collective-permute-done.5 = bf16[1,4,96,768]{3,2,1,0:T(8,128)(2,1)S(1)} collective-permute-done((bf16[1,4,96,768]{3,2,1,0:T(8,128)(2,1)S(1)}, bf16[1,4,96,768]{3,2,1,0:T(8,128)(2,1)S(1)}, u32[]{:S(2)}, u32[]{:S(2)}) %collective-permute-start.5) | collective-permute-done | bytes 589856 | tf_op jit(solution)/shard_map/ppermute | solution.py:641
  86.0 12.0 %collective-permute-done.6 = bf16[1,4,96,768]{3,2,1,0:T(8,128)(2,1)S(1)} collective-permute-done((bf16[1,4,96,768]{3,2,1,0:T(8,128)(2,1)S(1)}, bf16[1,4,96,768]{3,2,1,0:T(8,128)(2,1)S(1)}, u32[]{:S(2)}, u32[]{:S(2)}) %collective-permute-start.6) | collective-permute-done | bytes 589856 | tf_op jit(solution)/shard_map/ppermute | solution.py:641
  103.5 25.1 %collective-permute-done.9 = bf16[2,4,96,768]{3,2,1,0:T(8,128)(2,1)} collective-permute-done((bf16[2,4,96,768]{3,2,1,0:T(8,128)(2,1)}, bf16[2,4,96,768]{3,2,1,0:T(8,128)(2,1)}, u32[]{:S(2)}, u32[]{:S(2)}) %collective-permute-start.9) | collective-permute-done | bytes 1179680 | tf_op jit(solution)/shard_map/ppermute | solution.py:641
  140.6 5.9 %project.2.win_ref = bf16[4,576,896]{2,1,0:T(8,128)(2,1)S(1)} custom-call(bf16[4,384,768]{2,1,0:T(8,128)(2,1)S(1)} %bitcast.231, bf16[4,384,768]{2,1,0:T(8,128)(2,1)S(1)} %bitcast.236, bf16[768,896]{1,0:T(8,128)(2,1)S(1)} %bitcast.242, bf16[4,16,768]{2,1,0:T(8,128)(2,1)S(1)} %pad_maximum_fusion.15.bias_ref), custom_call_target="tpu_custom_call" | custom-call | flops 100000000 | tf_op jit(solution)/shard_map/project/pallas_call | solution.py:214
  152.2 3.7 collective-permute-done.12
  155.9 4.1 pad_maximum_fusion
  159.9 4.9 %collective-permute-done.10 = bf16[2,192,768]{2,1,0:T(8,128)(2,1)S(1)} collective-permute-done((bf16[2,192,768]{2,1,0:T(8,128)(2,1)S(1)}, bf16[2,192,768]{2,1,0:T(8,128)(2,1)S(1)}, u32[]{:S(2)}, u32[]{:S(2)}) %collective-permute-start.10) | collective-permute-done | bytes 589856 | tf_op jit(solution)/shard_map/ppermute | solution.py:641
  170.1 5.0 %project.3.par_ref = bf16[4,384,768]{2,1,0:T(8,128)(2,1)S(1)} custom-call(bf16[4,384,768]{2,1,0:T(8,128)(2,1)S(1)} %bitcast.232, bf16[4,384,768]{2,1,0:T(8,128)(2,1)S(1)} %bitcast.237, bf16[768,768]{1,0:T(8,128)(2,1)S(1)} %bitcast.244, bf16[4,16,768]{2,1,0:T(8,128)(2,1)S(1)} %pad_maximum_fusion.15.bias_ref), custom_call_target="tpu_custom_call" | custom-call | flops 100000000 | tf_op jit(solution)/shard_map/project/pallas_call | solution.py:214
  176.2 13.6 %attention_forward.1 = (bf16[4,192,640]{2,1,0:T(8,128)(2,1)S(1)}, f32[4,3,640]{2,1,0:T(4,128)S(1)}) custom-call(s32[4]{0:T(128)S(1)} %pad_add_fusion.here_ref, s32[40]{0:T(128)S(1)} %copy-done.32, s32[40,20]{1,0:T(8,128)S(1)} %copy.157.slots_ref, bf16[4,576,896]{2,1,0:T(8,128)(2,1)S(1)} %copy-done.10, bf16[4,384,768]{2,1,0:T(8,128)(2,1)S(1)} %project.3.par_ref), custom_call_target="tpu_custom_call" | custom-call | flops 130000003072 | tf_op jit(solution)/shard_map/attention_forward/pallas_call | solution.py:612
  193.4 24.7 %mlp_forward.1 = (bf16[1,192,640]{2,1,0:T(8,128)(2,1)}, bf16[2,192,640]{2,1,0:T(8,128)(2,1)}, bf16[1,192,640]{2,1,0:T(8,128)(2,1)}, bf16[4,768,640]{2,1,0:T(8,12...) custom-call(bf16[768,640]{1,0:T(8,128)(2,1)} %bitcast.256, ...), custom_call_target="tpu_custom_call" | custom-call | flops 240000008192 | tf_op jit(solution)/shard_map/mlp_forward/pallas_call | solution.py:353
  221.4 5.5 %down_grads.1 = (bf16[4,384,768]{2,1,0:T(8,128)(2,1)S(1)}, bf16[4,384,768]{2,1,0:T(8,128)(2,1)}) custom-call(bf16[768,640]{1,0:T(8,128)(2,1)S(1)} %copy-done.48, bf16[4,768,640]{2,1,0:T(8,128)(2,1)S(1)} %copy-done.44), custom_call_target="tpu_custom_call" | custom-call | flops 49999998976 | tf_op jit(solution)/shard_map/down_grads/pallas_call | solution.py:390
  227.3 23.9 %mlp_backward.1 = (bf16[4,384,768]{2,1,0:T(8,128)(2,1)}, bf16[4,384,768]{2,1,0:T(8,128)(2,1)}, f32[768,640]{1,0:T(8,128)}, bf16[768,640]{1,0:T(8,128)(2,1)}, bf1...) custom-call(bf16[768,640]{1,0:T(8,128)(2,1)} %get-tuple-element.128.low_ref, ...), custom_call_target="tpu_custom_call" | custom-call | flops 240000008192 | tf_op jit(solution)/shard_map/mlp_backward/pallas_call | solution.py:479
  251.7 2.8 fusion.2
  256.1 3.6 fusion.3
  260.9 20.0 %attention_backward.1 = (bf16[4,576,896]{2,1,0:T(8,128)(2,1)S(1)}, bf16[4,384,768]{2,1,0:T(8,128)(2,1)S(1)}) custom-call(s32[4]{0:T(128)S(1)} %pad_add_fusion.here_ref, s32[40]{0:T(128)S(1)} %copy-done.32, s32[40,20]{1,0:T(8,128)S(1)} %copy.157.slots_ref, bf16[4,576,896]{2,1,0:T(8,128)(2,1)S(1)} %copy-done.11, bf16[4,384,768]{2,1,0:T(8,128)(2,1)S(1)} %copy-done.19, ...), custom_call_target="tpu_custom_call" | custom-call | flops 199999995904 | tf_op jit(solution)/shard_map/attention_backward/pallas_call | solution.py:627
  281.0 4.4 token_grads.2
  288.1 12.4 %first_grads.1 = (bf16[4,384,896]{2,1,0:T(8,128)(2,1)S(1)}, bf16[4,384,896]{2,1,0:T(8,128)(2,1)}) custom-call(bf16[768,896]{1,0:T(8,128)(2,1)S(1)} %bitcast.243, bf16[768,768]{1,0:T(8,128)(2,1)S(1)} %bitcast.245, bf16[4,576,896]{2,1,0:T(8,128)(2,1)} %copy-done.42, bf16[4,384,768]{2,1,0:T(8,128)(2,1)S(1)} %copy-done.46, bf16[768,640]{1,0:T(8,128)(2,1)S(1)} %copy-done.50, ...), custom_call_target="tpu_custom_call" | custom-call | flops 120000004096 | tf_op jit(solution)/shard_map/first_grads/pallas_call | solution.py:534
  315.6 2.7 copy-done.43
  319.8 5.7 %token_grads.3 = (bf16[1,192,768]{2,1,0:T(8,128)(2,1)S(1)}, bf16[2,192,768]{2,1,0:T(8,128)(2,1)}, bf16[1,192,768]{2,1,0:T(8,128)(2,1)S(1)}) custom-call(bf16[4,384,768]{2,1,0:T(8,128)(2,1)S(1)} %bitcast.234, bf16[4,384,768]{2,1,0:T(8,128)(2,1)S(1)} %bitcast.239, bf16[4,576,896]{2,1,0:T(8,128)(2,1)S(1)} %copy-done.43, f32[768,640]{1,0:T(8,128)S(1)} %copy-done.47), custom_call_target="tpu_custom_call" | custom-call | flops 49999998976 | tf_op jit(solution)/shard_map/token_grads/pallas_call | solution.py:586
  330.2 9.1 %collective-permute-done.24 = bf16[2,96,896]{2,1,0:T(8,128)(2,1)S(1)} collective-permute-done((bf16[2,96,896]{2,1,0:T(8,128)(2,1)S(1)}, bf16[2,96,896]{2,1,0:T(8,128)(2,1)S(1)}, u32[]{:S(2)}, u32[]{:S(2)}) %collective-permute-start.24) | collective-permute-done | bytes 344096 | tf_op jit(solution)/shard_map/ppermute | solution.py:641
  349.3 7.5 %collective-permute-done.36 = bf16[96,768]{1,0:T(8,128)(2,1)S(1)} collective-permute-done((bf16[96,768]{1,0:T(8,128)(2,1)S(1)}, bf16[96,768]{1,0:T(8,128)(2,1)S(1)}, u32[]{:S(2)}, u32[]{:S(2)}) %collective-permute-start.36) | collective-permute-done | bytes 147488 | tf_op jit(solution)/shard_map/ppermute | solution.py:641
  357.9 18.9 %collective-permute-done.35 = bf16[96,768]{1,0:T(8,128)(2,1)} collective-permute-done((bf16[96,768]{1,0:T(8,128)(2,1)S(1)}, bf16[96,768]{1,0:T(8,128)(2,1)}, u32[]{:S(2)}, u32[]{:S(2)}) %collective-permute-start.35) | collective-permute-done | bytes 147488 | tf_op jit(solution)/shard_map/ppermute | solution.py:641
  381.3 3.9 collective-permute-start.37
  385.2 4.9 %collective-permute-done.28 = bf16[4,96,896]{2,1,0:T(8,128)(2,1)S(1)} collective-permute-done((bf16[4,96,896]{2,1,0:T(8,128)(2,1)S(1)}, bf16[4,96,896]{2,1,0:T(8,128)(2,1)S(1)}, u32[]{:S(2)}, u32[]{:S(2)}) %collective-permute-start.28) | collective-permute-done | bytes 688160 | tf_op jit(solution)/shard_map/ppermute | solution.py:641
  391.8 3.0 collective-permute-start.42
  394.8 5.0 %collective-permute-start.41 = (bf16[96,896]{1,0:T(8,128)(2,1)S(1)}, bf16[96,896]{1,0:T(8,128)(2,1)S(1)}, u32[]{:S(2)}, u32[]{:S(2)}) collective-permute-start(bf16[96,896]{1,0:T(8,128)(2,1)S(1)} %get-tuple-element.259), channel_id=1, source_target_pairs={{0,8},{4,12},{8,0},{12,4},{1,9},{5,13},{9,1},{13,5},{2,10},{6,14},... | collective-permute-start | bytes 516104 | tf_op jit(solution)/shard_map/ppermute | solution.py:641
  399.8 14.6 %collective-permute-done.38 = bf16[96,768]{1,0:T(8,128)(2,1)S(1)} collective-permute-done((bf16[96,768]{1,0:T(8,128)(2,1)S(1)}, bf16[96,768]{1,0:T(8,128)(2,1)S(1)}, u32[]{:S(2)}, u32[]{:S(2)}) %collective-permute-start.38) | collective-permute-done | bytes 147488 | tf_op jit(solution)/shard_map/ppermute | solution.py:641
  417.5 7.9 %collective-permute-done.41 = bf16[96,896]{1,0:T(8,128)(2,1)S(1)} collective-permute-done((bf16[96,896]{1,0:T(8,128)(2,1)S(1)}, bf16[96,896]{1,0:T(8,128)(2,1)S(1)}, u32[]{:S(2)}, u32[]{:S(2)}) %collective-permute-start.41) | collective-permute-done | bytes 172064 | tf_op jit(solution)/shard_map/ppermute | solution.py:641
  (305 shorter events, 124.8 us)
Async XLA Ops:
  7.2 141.3 %all-gather.3.cloned.1.call-start = ((), (), s32[]{:S(2)}) async-start(), calls=%async_computation.2 | async-start | bytes 4915200 | tf_op jit(solution)/shard_map/all_gather | solution.py:1033
  20.7 46.2 %collective-permute-start.3 = (bf16[2,192,896]{2,1,0:T(8,128)(2,1)S(1)}, bf16[2,192,896]{2,1,0:T(8,128)(2,1)S(1)}, u32[]{:S(2)}, u32[]{:S(2)}) collective-permute-start(bf16[2,192,896]{2,1,0:T(8,128)(2,1)S(1)} %get-tuple-element.97), channel_id=1, source_target_pairs={{0,2},{1,3},{2,0},{3,1},{4,6},{5,7},{6,4},{7,5},{8,10},{9,11},{10,... | collective-permute-start | bytes 2064392 | tf_op jit(solution)/shard_map/ppermute | solution.py:641
  23.8 15.5 %collective-permute-start.2 = (bf16[304,768]{1,0:T(8,128)(2,1)S(1)}, bf16[304,768]{1,0:T(8,128)(2,1)S(1)}, u32[]{:S(2)}, u32[]{:S(2)}) collective-permute-start(bf16[304,768]{1,0:T(8,128)(2,1)S(1)} %pack_weights.1), channel_id=1, source_target_pairs={{0,12},{4,8},{8,4},{12,0},{1,13},{5,9},{9,5},{13,1},{2,14},{6,10},... | collective-permute-start | bytes 1400840 | tf_op jit(solution)/shard_map/ppermute | solution.py:641
  27.4 39.6 %collective-permute-start.1 = (bf16[304,768]{1,0:T(8,128)(2,1)S(1)}, bf16[304,768]{1,0:T(8,128)(2,1)S(1)}, u32[]{:S(2)}, u32[]{:S(2)}) collective-permute-start(bf16[304,768]{1,0:T(8,128)(2,1)S(1)} %pack_weights.1), channel_id=1, source_target_pairs={{0,8},{4,12},{8,0},{12,4},{1,9},{5,13},{9,1},{13,5},{2,10},{6,14},... | collective-permute-start | bytes 1400840 | tf_op jit(solution)/shard_map/ppermute | solution.py:641
  27.4 39.6 %collective-permute-start = (bf16[304,768]{1,0:T(8,128)(2,1)S(1)}, bf16[304,768]{1,0:T(8,128)(2,1)S(1)}, u32[]{:S(2)}, u32[]{:S(2)}) collective-permute-start(bf16[304,768]{1,0:T(8,128)(2,1)S(1)} %pack_weights.1), channel_id=1, source_target_pairs={{0,4},{4,0},{8,12},{12,8},{1,5},{5,1},{9,13},{13,9},{2,6},{6,2},{1... | collective-permute-start | bytes 1400840 | tf_op jit(solution)/shard_map/ppermute | solution.py:641
  68.6 369.9 %reduce-scatter.2.cloned.1.call-start = ((), (), s32[]{:S(2)}) async-start(), calls=%async_computation.1 | async-start | bytes 5160960 | tf_op jit(solution)/shard_map/reduce_scatter | solution.py:1086
  70.7 15.3 %collective-permute-start.4 = (bf16[1,4,96,768]{3,2,1,0:T(8,128)(2,1)S(1)}, bf16[1,4,96,768]{3,2,1,0:T(8,128)(2,1)S(1)}, u32[]{:S(2)}, u32[]{:S(2)}) collective-permute-start(bf16[1,4,96,768]{3,2,1,0:T(8,128)(2,1)S(1)} %get-tuple-element.275), channel_id=1, source_target_pairs={{0,16},{16,0},{1,17},{17,1},{2,18},{18,2},{3,19},{19,3},{4,20},{20... | collective-permute-start | bytes 1769480 | tf_op jit(solution)/shard_map/ppermute | solution.py:641
  98.5 33.2 %collective-permute-start.7 = (bf16[1,4,384,768]{3,2,1,0:T(8,128)(2,1)S(1)}, bf16[1,4,384,768]{3,2,1,0:T(8,128)(2,1)S(1)}, u32[]{:S(2)}, u32[]{:S(2)}) collective-permute-start(bf16[1,4,384,768]{3,2,1,0:T(8,128)(2,1)S(1)} %bitcast.229), channel_id=1, source_target_pairs={{0,1},{1,0},{2,3},{3,2},{4,5},{5,4},{6,7},{7,6},{8,9},{9,8},{10,11... | collective-permute-start | bytes 7077896 | tf_op jit(solution)/shard_map/ppermute | solution.py:641
  100.8 27.7 %collective-permute-start.9 = (bf16[2,4,96,768]{3,2,1,0:T(8,128)(2,1)}, bf16[2,4,96,768]{3,2,1,0:T(8,128)(2,1)}, u32[]{:S(2)}, u32[]{:S(2)}) collective-permute-start(bf16[2,4,96,768]{3,2,1,0:T(8,128)(2,1)} %pad_maximum_fusion.3), channel_id=1, source_target_pairs={{0,2},{1,3},{2,0},{3,1},{4,6},{5,7},{6,4},{7,5},{8,10},{9,11},{10,... | collective-permute-start | bytes 3538952 | tf_op jit(solution)/shard_map/ppermute | solution.py:641
  101.8 28.3 %collective-permute-start.8 = (bf16[2,192,896]{2,1,0:T(8,128)(2,1)S(1)}, bf16[2,192,896]{2,1,0:T(8,128)(2,1)S(1)}, u32[]{:S(2)}, u32[]{:S(2)}) collective-permute-start(bf16[2,192,896]{2,1,0:T(8,128)(2,1)S(1)} %pad_maximum_fusion.5), channel_id=1, source_target_pairs={{0,1},{1,0},{2,3},{3,2},{4,5},{5,4},{6,7},{7,6},{8,9},{9,8},{10,11... | collective-permute-start | bytes 2064392 | tf_op jit(solution)/shard_map/ppermute | solution.py:641
  101.9 50.3 %collective-permute-start.11 = (bf16[2,4,96,768]{3,2,1,0:T(8,128)(2,1)}, bf16[2,4,96,768]{3,2,1,0:T(8,128)(2,1)}, u32[]{:S(2)}, u32[]{:S(2)}) collective-permute-start(bf16[2,4,96,768]{3,2,1,0:T(8,128)(2,1)} %pad_maximum_fusion.3), channel_id=1, source_target_pairs={{0,16},{16,0},{1,17},{17,1},{2,18},{18,2},{3,19},{19,3},{4,20},{20... | collective-permute-start | bytes 3538952 | tf_op jit(solution)/shard_map/ppermute | solution.py:641
  128.5 27.3 %collective-permute-start.12 = (bf16[2,4,96,768]{3,2,1,0:T(8,128)(2,1)}, bf16[2,4,96,768]{3,2,1,0:T(8,128)(2,1)}, u32[]{:S(2)}, u32[]{:S(2)}) collective-permute-start(bf16[2,4,96,768]{3,2,1,0:T(8,128)(2,1)} %collective-permute-done.9), channel_id=1, source_target_pairs={{0,16},{16,0},{1,17},{17,1},{2,18},{18,2},{3,19},{19,3},{4,20},{20... | collective-permute-start | bytes 3538952 | tf_op jit(solution)/shard_map/ppermute | solution.py:641
  166.6 26.8 %collective-permute-start.16 = (bf16[2,4,384,768]{3,2,1,0:T(8,128)(2,1)}, bf16[2,4,384,768]{3,2,1,0:T(8,128)(2,1)}, u32[]{:S(2)}, u32[]{:S(2)}) collective-permute-start(bf16[2,4,384,768]{3,2,1,0:T(8,128)(2,1)} %bitcast.258), channel_id=1, source_target_pairs={{0,1},{1,0},{2,3},{3,2},{4,5},{5,4},{6,7},{7,6},{8,9},{9,8},{10,11... | collective-permute-start | bytes 14155784 | tf_op jit(solution)/shard_map/ppermute | solution.py:641
  167.1 22.7 %collective-permute-start.14 = (bf16[2,192,640]{2,1,0:T(8,128)(2,1)S(1)}, bf16[2,192,640]{2,1,0:T(8,128)(2,1)S(1)}, u32[]{:S(2)}, u32[]{:S(2)}) collective-permute-start(bf16[2,192,640]{2,1,0:T(8,128)(2,1)S(1)} %copy-done.34), channel_id=1, source_target_pairs={{0,2},{1,3},{2,0},{3,1},{4,6},{5,7},{6,4},{7,5},{8,10},{9,11},{10,... | collective-permute-start | bytes 1474568 | tf_op jit(solution)/shard_map/ppermute | solution.py:641
  226.9 24.8 %collective-permute-start.17 = (bf16[4,384,768]{2,1,0:T(8,128)(2,1)}, bf16[4,384,768]{2,1,0:T(8,128)(2,1)}, u32[]{:S(2)}, u32[]{:S(2)}) collective-permute-start(bf16[4,384,768]{2,1,0:T(8,128)(2,1)} %get-tuple-element.127), channel_id=1, source_target_pairs={{0,1},{1,0},{2,3},{3,2},{4,5},{5,4},{6,7},{7,6},{8,9},{9,8},{10,11... | collective-permute-start | bytes 7077896 | tf_op jit(solution)/shard_map/ppermute | solution.py:641
  254.5 49.4 %collective-permute-start.21 = (bf16[4,2,96,768]{3,2,0,1:T(8,128)(2,1)}, bf16[4,2,96,768]{3,2,0,1:T(8,128)(2,1)}, u32[]{:S(2)}, u32[]{:S(2)}) collective-permute-start(bf16[4,2,96,768]{3,2,0,1:T(8,128)(2,1)} %fusion.2), channel_id=1, source_target_pairs={{0,16},{16,0},{1,17},{17,1},{2,18},{18,2},{3,19},{19,3},{4,20},{20... | collective-permute-start | bytes 3538952 | tf_op jit(solution)/shard_map/ppermute | solution.py:641
  285.4 17.8 %collective-permute-start.19 = (bf16[2,192,896]{2,1,0:T(8,128)(2,1)S(1)}, bf16[2,192,896]{2,1,0:T(8,128)(2,1)S(1)}, u32[]{:S(2)}, u32[]{:S(2)}) collective-permute-start(bf16[2,192,896]{2,1,0:T(8,128)(2,1)S(1)} %get-tuple-element.145), channel_id=1, source_target_pairs={{0,2},{1,3},{2,0},{3,1},{4,6},{5,7},{6,4},{7,5},{8,10},{9,11},{10,... | collective-permute-start | bytes 2064392 | tf_op jit(solution)/shard_map/ppermute | solution.py:641
  303.4 36.2 %collective-permute-start.25 = (bf16[4,2,96,768]{3,2,0,1:T(8,128)(2,1)}, bf16[4,2,96,768]{3,2,0,1:T(8,128)(2,1)}, u32[]{:S(2)}, u32[]{:S(2)}) collective-permute-start(bf16[4,2,96,768]{3,2,0,1:T(8,128)(2,1)} %fusion.3), channel_id=1, source_target_pairs={{0,16},{16,0},{1,17},{17,1},{2,18},{18,2},{3,19},{19,3},{4,20},{20... | collective-permute-start | bytes 3538952 | tf_op jit(solution)/shard_map/ppermute | solution.py:641
  306.4 36.5 %collective-permute-start.26 = (bf16[4,96,768]{2,1,0:T(8,128)(2,1)}, bf16[4,96,768]{2,1,0:T(8,128)(2,1)}, u32[]{:S(2)}, u32[]{:S(2)}) collective-permute-start(bf16[4,96,768]{2,1,0:T(8,128)(2,1)} %fusion.9), channel_id=1, source_target_pairs={{0,2},{1,3},{2,0},{3,1},{4,6},{5,7},{6,4},{7,5},{8,10},{9,11},{10,... | collective-permute-start | bytes 1769480 | tf_op jit(solution)/shard_map/ppermute | solution.py:641
  312.8 17.4 %collective-permute-start.23 = (bf16[2,96,896]{2,1,0:T(8,128)(2,1)S(1)}, bf16[2,96,896]{2,1,0:T(8,128)(2,1)S(1)}, u32[]{:S(2)}, u32[]{:S(2)}) collective-permute-start(bf16[2,96,896]{2,1,0:T(8,128)(2,1)S(1)} %get-tuple-element.262), channel_id=1, source_target_pairs={{0,2},{1,3},{2,0},{3,1},{4,6},{5,7},{6,4},{7,5},{8,10},{9,11},{10,... | collective-permute-start | bytes 1032200 | tf_op jit(solution)/shard_map/ppermute | solution.py:641
  314.1 25.3 %collective-permute-start.24 = (bf16[2,96,896]{2,1,0:T(8,128)(2,1)S(1)}, bf16[2,96,896]{2,1,0:T(8,128)(2,1)S(1)}, u32[]{:S(2)}, u32[]{:S(2)}) collective-permute-start(bf16[2,96,896]{2,1,0:T(8,128)(2,1)S(1)} %get-tuple-element.263), channel_id=1, source_target_pairs={{0,16},{16,0},{1,17},{17,1},{2,18},{18,2},{3,19},{19,3},{4,20},{20... | collective-permute-start | bytes 1032200 | tf_op jit(solution)/shard_map/ppermute | solution.py:641
  325.5 52.3 %collective-permute-start.32 = (bf16[2,192,768]{2,1,0:T(8,128)(2,1)}, bf16[2,192,768]{2,1,0:T(8,128)(2,1)S(1)}, u32[]{:S(2)}, u32[]{:S(2)}) collective-permute-start(bf16[2,192,768]{2,1,0:T(8,128)(2,1)} %get-tuple-element.161), channel_id=1, source_target_pairs={{0,2},{1,3},{2,0},{3,1},{4,6},{5,7},{6,4},{7,5},{8,10},{9,11},{10,... | collective-permute-start | bytes 1769480 | tf_op jit(solution)/shard_map/ppermute | solution.py:641
  342.0 36.7 %collective-permute-start.27 = (bf16[4,96,768]{2,1,0:T(8,128)(2,1)}, bf16[4,96,768]{2,1,0:T(8,128)(2,1)}, u32[]{:S(2)}, u32[]{:S(2)}) collective-permute-start(bf16[4,96,768]{2,1,0:T(8,128)(2,1)} %fusion.8), channel_id=1, source_target_pairs={{0,2},{1,3},{2,0},{3,1},{4,6},{5,7},{6,4},{7,5},{8,10},{9,11},{10,... | collective-permute-start | bytes 1769480 | tf_op jit(solution)/shard_map/ppermute | solution.py:641
  346.9 29.9 %collective-permute-start.35 = (bf16[96,768]{1,0:T(8,128)(2,1)S(1)}, bf16[96,768]{1,0:T(8,128)(2,1)}, u32[]{:S(2)}, u32[]{:S(2)}) collective-permute-start(bf16[96,768]{1,0:T(8,128)(2,1)S(1)} %get-tuple-element.270), channel_id=1, source_target_pairs={{0,8},{4,12},{8,0},{12,4},{1,9},{5,13},{9,1},{13,5},{2,10},{6,14},... | collective-permute-start | bytes 442376 | tf_op jit(solution)/shard_map/ppermute | solution.py:641
  346.9 29.9 %collective-permute-start.34 = (bf16[96,768]{1,0:T(8,128)(2,1)S(1)}, bf16[96,768]{1,0:T(8,128)(2,1)}, u32[]{:S(2)}, u32[]{:S(2)}) collective-permute-start(bf16[96,768]{1,0:T(8,128)(2,1)S(1)} %get-tuple-element.271), channel_id=1, source_target_pairs={{0,4},{4,0},{8,12},{12,8},{1,5},{5,1},{9,13},{13,9},{2,6},{6,2},{1... | collective-permute-start | bytes 442376 | tf_op jit(solution)/shard_map/ppermute | solution.py:641
  356.8 24.5 %collective-permute-start.29 = (bf16[4,96,896]{2,1,0:T(8,128)(2,1)S(1)}, bf16[4,96,896]{2,1,0:T(8,128)(2,1)S(1)}, u32[]{:S(2)}, u32[]{:S(2)}) collective-permute-start(bf16[4,96,896]{2,1,0:T(8,128)(2,1)S(1)} %pad_maximum_fusion.8), channel_id=1, source_target_pairs={{0,2},{1,3},{2,0},{3,1},{4,6},{5,7},{6,4},{7,5},{8,10},{9,11},{10,... | collective-permute-start | bytes 2064392 | tf_op jit(solution)/shard_map/ppermute | solution.py:641
  378.8 62.1 %collective-permute-start.33 = (bf16[2,192,768]{2,1,0:T(8,128)(2,1)}, bf16[2,192,768]{2,1,0:T(8,128)(2,1)S(1)}, u32[]{:S(2)}, u32[]{:S(2)}) collective-permute-start(bf16[2,192,768]{2,1,0:T(8,128)(2,1)} %pad_maximum_fusion.11), channel_id=1, source_target_pairs={{0,1},{1,0},{2,3},{3,2},{4,5},{5,4},{6,7},{7,6},{8,9},{9,8},{10,11... | collective-permute-start | bytes 1769480 | tf_op jit(solution)/shard_map/ppermute | solution.py:641
  381.3 33.1 %collective-permute-start.38 = (bf16[96,768]{1,0:T(8,128)(2,1)S(1)}, bf16[96,768]{1,0:T(8,128)(2,1)S(1)}, u32[]{:S(2)}, u32[]{:S(2)}) collective-permute-start(bf16[96,768]{1,0:T(8,128)(2,1)S(1)} %get-tuple-element.267), channel_id=1, source_target_pairs={{0,8},{4,12},{8,0},{12,4},{1,9},{5,13},{9,1},{13,5},{2,10},{6,14},... | collective-permute-start | bytes 442376 | tf_op jit(solution)/shard_map/ppermute | solution.py:641
  381.3 33.1 %collective-permute-start.37 = (bf16[96,768]{1,0:T(8,128)(2,1)S(1)}, bf16[96,768]{1,0:T(8,128)(2,1)S(1)}, u32[]{:S(2)}, u32[]{:S(2)}) collective-permute-start(bf16[96,768]{1,0:T(8,128)(2,1)S(1)} %get-tuple-element.268), channel_id=1, source_target_pairs={{0,4},{4,0},{8,12},{12,8},{1,5},{5,1},{9,13},{13,9},{2,6},{6,2},{1... | collective-permute-start | bytes 442376 | tf_op jit(solution)/shard_map/ppermute | solution.py:641
  391.8 24.2 %collective-permute-start.42 = (bf16[96,896]{1,0:T(8,128)(2,1)S(1)}, bf16[96,896]{1,0:T(8,128)(2,1)S(1)}, u32[]{:S(2)}, u32[]{:S(2)}) collective-permute-start(bf16[96,896]{1,0:T(8,128)(2,1)S(1)} %get-tuple-element.258), channel_id=1, source_target_pairs={{0,12},{4,8},{8,4},{12,0},{1,13},{5,9},{9,5},{13,1},{2,14},{6,10},... | collective-permute-start | bytes 516104 | tf_op jit(solution)/shard_map/ppermute | solution.py:641
  394.8 30.6 %collective-permute-start.41 = (bf16[96,896]{1,0:T(8,128)(2,1)S(1)}, bf16[96,896]{1,0:T(8,128)(2,1)S(1)}, u32[]{:S(2)}, u32[]{:S(2)}) collective-permute-start(bf16[96,896]{1,0:T(8,128)(2,1)S(1)} %get-tuple-element.259), channel_id=1, source_target_pairs={{0,8},{4,12},{8,0},{12,4},{1,9},{5,13},{9,1},{13,5},{2,10},{6,14},... | collective-permute-start | bytes 516104 | tf_op jit(solution)/shard_map/ppermute | solution.py:641
  414.4 18.7 %collective-permute-start.30 = (bf16[2,192,640]{2,1,0:T(8,128)(2,1)}, bf16[2,192,640]{2,1,0:T(8,128)(2,1)S(1)}, u32[]{:S(2)}, u32[]{:S(2)}) collective-permute-start(bf16[2,192,640]{2,1,0:T(8,128)(2,1)} %get-tuple-element.169), channel_id=1, source_target_pairs={{0,2},{1,3},{2,0},{3,1},{4,6},{5,7},{6,4},{7,5},{8,10},{9,11},{10,... | collective-permute-start | bytes 1474568 | tf_op jit(solution)/shard_map/ppermute | solution.py:641
  (84 other events, 678.9 us)
Sparse Core Ops, SparseCore 0:
  68.7 75.6 all-gather.2
  311.2 92.2 reduce-scatter.1

commit v3 on v2

--- a/solution.py
+++ b/solution.py
@@ -187,6 +187,10 @@
     return pl.CostEstimate(flops=int(microseconds * 1.0e9), bytes_accessed=0, transcendentals=0)
 
 
+def held(*arrays):
+    return tuple(pltpu.with_memory_space_constraint(array, pltpu.HBM) for array in arrays)
+
+
 def params(mib):
     return pltpu.CompilerParams(vmem_limit_bytes=mib << 20)
 
@@ -197,8 +201,21 @@
     return jnp.concatenate([column] * (columns // 128), axis=1)
 
 
-def project_kernel(low, high, scaled, near_ref, far_ref, toks_ref, bias_ref, out_ref):
+def join_pieces(refs, toks_ref):
+    @pl.when(pl.program_id(0) == 0)
+    def join():
+        feat = refs[0].shape[1]
+        for i, (piece, place) in enumerate(PIECES):
+            toks_ref[i * feat : (i + 1) * feat] = refs[piece][place]
+
+
+def project_kernel(low, high, scaled, near_ref, far_ref, *refs):
     depth = near_ref.shape[1]
+    if len(refs) > 3:
+        toks_ref, bias_ref, out_ref = refs[5], refs[3], refs[4]
+        join_pieces(refs[:3], toks_ref)
+    else:
+        toks_ref, bias_ref, out_ref = refs
     out = tn(near_ref[0, :, low:high], toks_ref[:depth]) + tn(far_ref[0, :, low:high], toks_ref[depth:])
     out = (out + across_lanes(bias_ref[0], 1, low, high, out.shape[1])).astype(BF16)
     if scaled:
@@ -209,302 +226,311 @@
 
 
 def project(near, far, toks, bias, low, high, scaled):
-    groups = near.shape[0]
-    out = jax.ShapeDtypeStruct((groups, high - low, toks.shape[1]), BF16)
+    groups, depth = near.shape[:2]
+    pieces = toks if isinstance(toks, tuple) else (toks,)
+    out = jax.ShapeDtypeStruct((groups, high - low, pieces[0].shape[-1]), BF16)
     return pl.pallas_call(
         functools.partial(project_kernel, low, high, scaled),
         grid=(groups,),
-        in_specs=[step_block(near), step_block(far), whole_block(toks), step_block(bias)],
+        in_specs=[step_block(near), step_block(far), *[whole_block(piece) for piece in pieces], step_block(bias)],
+        scratch_shapes=[pltpu.VMEM((2 * depth, pieces[0].shape[-1]), BF16)] if len(pieces) > 1 else [],
         out_specs=step_block(out),
         out_shape=out,
         compiler_params=params(40),
         cost_estimate=cost(0.1),
         name="project",
-    )(near, far, toks, bias)
+    )(near, far, *pieces, bias)
 
 
 def chunks(columns):
     return columns // 128
 
 
-def mlp_forward_kernel(
+def mlp_kernel(
     at,
     ctx_ref,
     win_ref,
     cot_keep,
     cot_got,
     cot_last,
-    out_ref,
-    near_up,
-    far_up,
-    near_down,
-    far_down,
+    near_first,
+    far_first,
+    near_ref,
+    far_ref,
     bias_ref,
     keep_ref,
     along_ref,
     close_ref,
     active_ref,
-    slope_ref,
-    grad_ref,
+    upper_ref,
+    hidden_ref,
     low_ref,
-    hidden_ref,
-    normed_ref,
-    scale_ref,
+    first_low_ref,
+    dctx_ref,
+    up_sum_ref,
     sums_ref,
     total_ref,
     wide_ref,
     parts_ref,
+    normed_ref,
+    scale_ref,
+    slope_ref,
+    columns_ref,
+    out_ref,
+    weights_ref,
+    sem,
 ):
-    step, last = pl.program_id(0), pl.num_programs(0) - 1
-    depth = near_up.shape[2]
+    step, groups = pl.program_id(0), slope_ref.shape[0]
+    depth, width = near_ref.shape[2:]
     model, own = total_ref.shape
     feat = keep_ref.shape[1]
-
-    def column(i):
-        return win_ref[:, at + i : at + i + 1].astype(F32)
+    heads = ctx_ref.shape[1]
+    skip = out_ref.shape[3] - heads
+
+    def weight_copies(block):
+        return [
+            pltpu.make_async_copy(
+                source.at[which, block], weights_ref.at[which, side, block], sem.at[2 + 4 * block + 2 * which + side]
+            )
+            for which in range(2)
+            for side, source in enumerate((near_ref, far_ref))
+        ]
+
+    first_copies = [
+        pltpu.make_async_copy(
+            source.at[:, :, pl.ds(width - out_ref.shape[3], out_ref.shape[3])], out_ref.at[side], sem.at[side]
+        )
+        for side, source in enumerate((near_first, far_first))
+    ]
+
+    def over_columns(body):
+        def run(i, carry):
+            body(pl.ds(pl.multiple_of(i * 128, 128), 128))
+            return carry
+
+        lax.fori_loop(0, own // 128, run, 0)
+
+    def sum_parts(first):
+        for i in range(3):
+            sums_ref[:, first + i : first + i + 1] = jnp.sum(parts_ref[i], axis=1, keepdims=True)
+        parts_ref[...] = jnp.zeros(parts_ref.shape, F32)
 
     @pl.when(step == 0)
     def start():
-        total_ref[...] = nn(out_ref[...], ctx_ref[...])
-        bias, gain, shift = column(0), column(1), column(2)
-
-        def body(i, carry):
-            cols = pl.ds(pl.multiple_of(i * 128, 128), 128)
-            values = total_ref[:, cols] + bias + win_ref[:, cols].astype(F32)
+        for copy in first_copies:
+            copy.start()
+        for block in range(groups):
+            for copy in weight_copies(block):
+                copy.start()
+        for i in range(6):
+            columns_ref[i] = jnp.broadcast_to(win_ref[:, at + i : at + i + 1].astype(F32), (model, 128))
+        parts_ref[...] = jnp.zeros(parts_ref.shape, F32)
+        for copy in first_copies:
+            copy.wait()
+        for n in range(groups):
+            near, far = nn(out_ref[0, n, :, skip:], ctx_ref[n]), nn(out_ref[1, n, :, skip:], ctx_ref[n])
+            if n == 0:
+                total_ref[:depth], total_ref[depth:] = near, far
+            else:
+                total_ref[:depth] += near
+                total_ref[depth:] += far
+
+        def body(cols):
+            values = total_ref[:, cols] + columns_ref[0] + win_ref[:, cols].astype(F32)
             center, scale = norm_stats(values)
             normed = (values - center) * scale
-            hidden = normed * gain + shift
+            hidden = normed * columns_ref[1] + columns_ref[2]
             normed_ref[:, cols] = normed
             scale_ref[:, cols] = scale
             wide_ref[:, cols] = hidden
             hidden_ref[:, cols] = hidden.astype(BF16)
-            return carry
-
-        lax.fori_loop(0, chunks(own), body, 0)
+
+        over_columns(body)
         total_ref[...] = jnp.zeros(total_ref.shape, F32)
 
-    width = near_up.shape[3]
-    piece = width // 3
-    for low in range(0, width, piece):
-        rows = slice(low, low + piece)
-        upper = tn(near_up[0, 0, :, rows], hidden_ref[:depth]) + tn(far_up[0, 0, :, rows], hidden_ref[depth:])
-        upper = upper + across_lanes(bias_ref[0], 0, low, low + piece, own)
-        phi = 0.5 * (1.0 + lax.erf(upper * np.float32(0.5**0.5)))
-        active_ref[0, rows] = (upper * phi).astype(BF16)
-        slope_ref[0, rows] = (
-            phi + upper * jnp.exp(-0.5 * upper * upper) * np.float32(1.0 / np.sqrt(2.0 * np.pi))
-        ).astype(BF16)
-    total_ref[:depth] += nn(near_down[0, 0], active_ref[0])
-    total_ref[depth:] += nn(far_down[0, 0], active_ref[0])
-
-    @pl.when(step == last)
-    def finish():
-        bias, gain, shift = column(3), column(4), column(5)
-        parts_ref[...] = jnp.zeros(parts_ref.shape, F32)
-
-        def body(i, carry):
-            cols = pl.ds(pl.multiple_of(i * 128, 128), 128)
-            values = total_ref[:, cols] + bias + wide_ref[:, cols]
+    @pl.when(step < groups)
+    def forward():
+        for block in range(groups):
+
+            @pl.when(step == block)
+            def arrive(block=block):
+                for copy in weight_copies(block):
+                    copy.wait()
+
+        piece = width // 3
+        for low in range(0, width, piece):
+            rows = slice(low, low + piece)
+            upper = tn(weights_ref[0, 0, step, :, rows], hidden_ref[:depth])
+            upper = upper + tn(weights_ref[0, 1, step, :, rows], hidden_ref[depth:])
+            upper = upper + across_lanes(bias_ref[0], 0, low, low + piece, own)
+            phi = 0.5 * (1.0 + lax.erf(upper * np.float32(0.5**0.5)))
+            active_ref[0, rows] = (upper * phi).astype(BF16)
+            slope_ref[step, rows] = (
+                phi + upper * jnp.exp(-0.5 * upper * upper) * np.float32(1.0 / np.sqrt(2.0 * np.pi))
+            ).astype(BF16)
+        active = active_ref[0]
+        total_ref[:depth] += nn(weights_ref[1, 0, step], active)
+        total_ref[depth:] += nn(weights_ref[1, 1, step], active)
+
+    @pl.when(step == groups - 1)
+    def turn():
+        pieces = (cot_keep, cot_got, cot_last)
+
+        def body(cols):
+            values = total_ref[:, cols] + columns_ref[3] + wide_ref[:, cols]
             center, scale = norm_stats(values)
             normed = (values - center) * scale
-            result = (normed * gain + shift).astype(BF16)
+            result = (normed * columns_ref[4] + columns_ref[5]).astype(BF16)
             keep_ref[0, :, cols] = result[:feat]
             along_ref[0, :, cols] = result[feat : 2 * feat]
             close_ref[0, :, cols] = result[2 * feat : 3 * feat]
             along_ref[1, :, cols] = result[3 * feat :]
-            pieces = (cot_keep, cot_got, cot_last)
             cot = jnp.concatenate([pieces[i][j, :, cols] for i, j in PIECES], axis=0).astype(F32)
-            grad = norm_back(cot, normed, scale, gain)
-            grad_ref[:, cols] = grad
+            grad = norm_back(cot, normed, scale, columns_ref[4])
+            total_ref[:, cols] = grad
             grad_low = grad.astype(BF16)
             low_ref[:, cols] = grad_low
             parts_ref[0] += grad_low.astype(F32)
             parts_ref[1] += cot * normed
             parts_ref[2] += cot
-            return carry
-
-        lax.fori_loop(0, chunks(own), body, 0)
-        for i in range(3):
-            sums_ref[:, i : i + 1] = jnp.sum(parts_ref[i], axis=1, keepdims=True)
-
-
-def weight_block(array, which):
-    return pl.BlockSpec((1, 1) + array.shape[2:], lambda step, *_: (which, step, 0, 0))
-
-
-def mlp_forward(at, ctx, win, cot, out_t, near, far, bias):
+
+        over_columns(body)
+        sum_parts(3)
+
+    @pl.when(step >= groups)
+    def backward():
+        block = step - groups
+        upper = tn(weights_ref[1, 0, block], low_ref[:depth]) + tn(weights_ref[1, 1, block], low_ref[depth:])
+        upper = (upper * slope_ref[block].astype(F32)).astype(BF16)
+        upper_ref[0] = upper
+        up_sum_ref[0] = jnp.sum(upper.astype(F32), axis=1, keepdims=True)
+        total_ref[:depth] += nn(weights_ref[0, 0, block], upper)
+        total_ref[depth:] += nn(weights_ref[0, 1, block], upper)
+
+    @pl.when(step == 2 * groups - 1)
+    def finish():
+        def body(cols):
+            hidden_grad = total_ref[:, cols]
+            normed = normed_ref[:, cols]
+            first_low = norm_back(hidden_grad, normed, scale_ref[:, cols], columns_ref[1]).astype(BF16)
+            first_low_ref[:, cols] = first_low
+            parts_ref[0] += first_low.astype(F32)
+            parts_ref[1] += hidden_grad * normed
+            parts_ref[2] += hidden_grad
+
+        over_columns(body)
+        sum_parts(0)
+        for n in range(groups):
+            grads = tn(out_ref[0, n, :, skip:], first_low_ref[:depth]) + tn(out_ref[1, n, :, skip:], first_low_ref[depth:])
+            dctx_ref[n] = grads.astype(BF16)
+
+
+def once(array):
+    return pl.BlockSpec(
+        array.shape, lambda step, *_: (0,) * len(array.shape), pipeline_mode=pl.Buffered(1)
+    )
+
+
+def mlp(at, ctx, win, cot, near_first, far_first, near, far, bias):
     groups, depth, width = near.shape[1:]
     feat, own = cot[0].shape[1:]
     model = feat * 4
+    out_columns = -(-ctx.shape[1] // 128) * 128
+
+    def early(array):
+        return pl.BlockSpec((1,) + array.shape[1:], lambda step, *_: (jnp.minimum(step, groups - 1), 0, 0))
+
+    def late(array):
+        return pl.BlockSpec((1,) + array.shape[1:], lambda step, *_: (jnp.maximum(step - groups, 0), 0, 0))
+
     outs = [
         jax.ShapeDtypeStruct((1, feat, own), BF16),
         jax.ShapeDtypeStruct((2, feat, own), BF16),
         jax.ShapeDtypeStruct((1, feat, own), BF16),
         jax.ShapeDtypeStruct((groups, width, own), BF16),
         jax.ShapeDtypeStruct((groups, width, own), BF16),
-        jax.ShapeDtypeStruct((model, own), F32),
         jax.ShapeDtypeStruct((model, own), BF16),
         jax.ShapeDtypeStruct((model, own), BF16),
-        jax.ShapeDtypeStruct((model, own), F32),
-        jax.ShapeDtypeStruct((1, own), F32),
-        jax.ShapeDtypeStruct((model, 3), F32),
+        jax.ShapeDtypeStruct((model, own), BF16),
+        jax.ShapeDtypeStruct(ctx.shape, BF16),
+        jax.ShapeDtypeStruct((groups, width, 1), F32),
+        jax.ShapeDtypeStruct((model, 6), F32),
     ]
-    specs = [step_block(o) if i in (3, 4) else whole_block(o) for i, o in enumerate(outs)]
-    return pl.pallas_call(
-        functools.partial(mlp_forward_kernel, at),
-        grid=(groups,),
+    return pl.pallas_call(
+        functools.partial(mlp_kernel, at),
+        grid=(2 * groups,),
         in_specs=[
-            whole_block(ctx),
-            whole_block(win),
-            *[whole_block(piece) for piece in cot],
-            whole_block(out_t),
-            weight_block(near, 0),
-            weight_block(far, 0),
-            weight_block(near, 1),
-            weight_block(far, 1),
-            step_block(bias),
+            once(ctx),
+            once(win),
+            *[once(piece) for piece in cot],
+            HBM,
+            HBM,
+            HBM,
+            HBM,
+            pl.BlockSpec((1,) + bias.shape[1:], lambda step, *_: (jnp.minimum(step, groups - 1), 0, 0)),
         ],
-        out_specs=specs,
+        out_specs=[early(o) if i == 3 else late(o) if i in (4, 9) else once(o) for i, o in enumerate(outs)],
         out_shape=outs,
         scratch_shapes=[
             pltpu.VMEM((model, own), F32),
             pltpu.VMEM((model, own), F32),
             pltpu.VMEM((3, model, 128), F32),
+            pltpu.VMEM((model, own), F32),
+            pltpu.VMEM((1, own), F32),
+            pltpu.VMEM((groups, width, own), BF16),
+            pltpu.VMEM((6, model, 128), F32),
+            pltpu.VMEM((2, groups, depth, out_columns), BF16),
+            pltpu.VMEM((2, 2, groups, depth, width), BF16),
+            pltpu.SemaphoreType.DMA((2 + 4 * groups,)),
         ],
-        compiler_params=params(56),
-        cost_estimate=cost(240),
-        name="mlp_forward",
-    )(ctx, win, *cot, out_t, near, far, near, far, bias)
-
-
-def down_grad_kernel(low_ref, active_ref, keep_ref, send_ref):
-    grads = nt(low_ref[...], active_ref[0]).astype(BF16)
-    depth = keep_ref.shape[1]
-    keep_ref[0] = grads[:depth]
-    send_ref[0] = grads[depth:]
-
-
-def down_grads(low, active):
+        compiler_params=params(44),
+        cost_estimate=cost(400),
+        name="mlp",
+    )(ctx, win, *cot, *held(near_first, far_first, near, far), bias)
+
+
+def hidden_grad_kernel(low_ref, hidden_ref, active_ref, upper_ref, down_keep, down_send, up_keep, up_send):
+    depth = down_keep.shape[1]
+    for keep, send, left, right in (
+        (down_keep, down_send, low_ref, active_ref),
+        (up_keep, up_send, hidden_ref, upper_ref),
+    ):
+        keep[0] = nt(left[:depth], right[0]).astype(BF16)
+        send[0] = nt(left[depth:], right[0]).astype(BF16)
+
+
+def hidden_grads(low, hidden, active, upper):
     groups, width, own = active.shape
     out = jax.ShapeDtypeStruct((groups, low.shape[0] // 2, width), BF16)
     return pl.pallas_call(
-        down_grad_kernel,
+        hidden_grad_kernel,
         grid=(groups,),
-        in_specs=[whole_block(low), step_block(active)],
-        out_specs=[step_block(out)] * 2,
-        out_shape=[out] * 2,
+        in_specs=[whole_block(low), whole_block(hidden), step_block(active), step_block(upper)],
+        out_specs=[step_block(out)] * 4,
+        out_shape=[out] * 4,
         compiler_params=params(32),
-        cost_estimate=cost(50),
-        name="down_grads",
-    )(low, active)
-
-
-def mlp_backward_kernel(
-    at,
+        cost_estimate=cost(100),
+        name="hidden_grads",
+    )(low, hidden, active, upper)
+
+
+def first_grad_kernel(
+    width,
+    win_ref,
+    par_keep,
+    par_got,
+    par_last,
+    dwin_ref,
+    dpar_ref,
     low_ref,
-    slope_ref,
-    hidden_ref,
-    near_up,
-    far_up,
-    near_down,
-    far_down,
-    grad_ref,
-    normed_ref,
-    scale_ref,
-    win_ref,
-    out_ref,
+    ctx_ref,
+    up_ref,
+    sums_ref,
     keep_ref,
     send_ref,
-    first_ref,
-    first_low_ref,
-    dctx_ref,
-    bias_ref,
-    sums_ref,
-    total_ref,
-    parts_ref,
+    par_ref,
 ):
-    step, last = pl.program_id(0), pl.num_programs(0) - 1
-    depth = near_up.shape[2]
-    model, own = low_ref.shape
-
-    @pl.when(step == 0)
-    def start():
-        total_ref[...] = grad_ref[...]
-
-    upper = tn(near_down[0, 0], low_ref[:depth]) + tn(far_down[0, 0], low_ref[depth:])
-    upper = (upper * slope_ref[0].astype(F32)).astype(BF16)
-    bias_ref[0] = jnp.sum(upper.astype(F32), axis=1, keepdims=True)
-    total_ref[:depth] += nn(near_up[0, 0], upper)
-    total_ref[depth:] += nn(far_up[0, 0], upper)
-    keep_ref[0] = nt(hidden_ref[:depth], upper).astype(BF16)
-    send_ref[0] = nt(hidden_ref[depth:], upper).astype(BF16)
-
-    @pl.when(step == last)
-    def finish():
-        gain = win_ref[:, at + 1 : at + 2].astype(F32)
-        parts_ref[...] = jnp.zeros(parts_ref.shape, F32)
-
-        def body(i, carry):
-            cols = pl.ds(pl.multiple_of(i * 128, 128), 128)
-            hidden_grad = total_ref[:, cols]
-            normed = normed_ref[:, cols]
-            first = norm_back(hidden_grad, normed, scale_ref[:, cols], gain)
-            first_ref[:, cols] = first
-            first_low = first.astype(BF16)
-            first_low_ref[:, cols] = first_low
-            parts_ref[0] += first_low.astype(F32)
-            parts_ref[1] += hidden_grad * normed
-            parts_ref[2] += hidden_grad
-            return carry
-
-        lax.fori_loop(0, chunks(own), body, 0)
-        for i in range(3):
-            sums_ref[:, i : i + 1] = jnp.sum(parts_ref[i], axis=1, keepdims=True)
-        dctx_ref[...] = tn(out_ref[...], first_low_ref[...]).astype(BF16)
-
-
-def mlp_backward(at, low, slope, hidden, near, far, grad, normed, scale, win, out_t):
-    groups, depth, width = near.shape[1:]
-    model, own = low.shape
-    outs = [
-        jax.ShapeDtypeStruct((groups, depth, width), BF16),
-        jax.ShapeDtypeStruct((groups, depth, width), BF16),
-        jax.ShapeDtypeStruct((model, own), F32),
-        jax.ShapeDtypeStruct((model, own), BF16),
-        jax.ShapeDtypeStruct((out_t.shape[1], own), BF16),
-        jax.ShapeDtypeStruct((groups, width, 1), F32),
-        jax.ShapeDtypeStruct((model, 3), F32),
-    ]
-    specs = [step_block(o) if i in (0, 1, 5) else whole_block(o) for i, o in enumerate(outs)]
-    return pl.pallas_call(
-        functools.partial(mlp_backward_kernel, at),
-        grid=(groups,),
-        in_specs=[
-            whole_block(low),
-            step_block(slope),
-            whole_block(hidden),
-            weight_block(near, 0),
-            weight_block(far, 0),
-            weight_block(near, 1),
-            weight_block(far, 1),
-            whole_block(grad),
-            whole_block(normed),
-            whole_block(scale),
-            whole_block(win),
-            whole_block(out_t),
-        ],
-        out_specs=specs,
-        out_shape=outs,
-        scratch_shapes=[pltpu.VMEM((model, own), F32), pltpu.VMEM((3, model, 128), F32)],
-        compiler_params=params(56),
-        cost_estimate=cost(240),
-        name="mlp_backward",
-    )(low, slope, hidden, near, far, near, far, grad, normed, scale, win, out_t)
-
-
-def first_grad_kernel(
-    width, win_ref, par_ref, dwin_ref, dpar_ref, low_ref, ctx_ref, up_ref, first_ref, last_ref, keep_ref, send_ref
-):
+    join_pieces((par_keep, par_got, par_last), par_ref)
     depth = keep_ref.shape[1]
     half = depth // 4
     query = jnp.sum(dwin_ref[0, :width].astype(F32), axis=1, keepdims=True)
@@ -524,11 +550,11 @@
             grads = grads + nt(par, dpar_ref[0, (i - 1) * width : i * width])
             out_ref[0, :, i * width : (i + 1) * width] = grads.astype(BF16)
         out_ref[0, :, 3 * width : 4 * width] = nt(low_ref[rows], ctx_ref[0]).astype(BF16)
-        extra = jnp.concatenate([by_row, first_ref[rows], last_ref[rows], pad], axis=1)
+        extra = jnp.concatenate([by_row, sums_ref[rows], pad], axis=1)
         out_ref[0, :, 4 * width :] = extra.astype(BF16)
 
 
-def first_grads(win, par, dwin, dpar, low, ctx, up_bias, first_sums, last_sums):
+def first_grads(win, par, dwin, dpar, low, ctx, up_bias, sums):
     groups, width, own = ctx.shape
     out = jax.ShapeDtypeStruct((groups, low.shape[0] // 2, 4 * width + 128), BF16)
     return pl.pallas_call(
@@ -536,21 +562,21 @@
         grid=(groups,),
         in_specs=[
             whole_block(win),
-            whole_block(par),
+            *[whole_block(piece) for piece in par],
             step_block(dwin),
             step_block(dpar),
             whole_block(low),
             step_block(ctx),
             step_block(up_bias),
-            whole_block(first_sums),
-            whole_block(last_sums),
+            whole_block(sums),
         ],
         out_specs=[step_block(out)] * 2,
         out_shape=[out] * 2,
+        scratch_shapes=[pltpu.VMEM((low.shape[0], par[0].shape[2]), BF16)],
         compiler_params=params(40),
-        cost_estimate=cost(120),
+        cost_estimate=cost(15),
         name="first_grads",
-    )(win, par, dwin, dpar, low, ctx, up_bias, first_sums, last_sums)
+    )(win, *par, dwin, dpar, low, ctx, up_bias, sums)
 
 
 def token_grad_kernel(low, high, parent, near_ref, far_ref, dwin_ref, more_ref, keep_ref, along_ref, close_ref, total_ref):
@@ -563,7 +589,7 @@
     def start():
         total_ref[...] = jnp.zeros(total_ref.shape, F32)
         if not parent:
-            total_ref[:, :own] = more_ref[...]
+            total_ref[:, :own] = more_ref[...].astype(F32)
 
     if parent:
         grads = jnp.concatenate([more_ref[0], dwin_ref[0, low:high, more_ref.shape[2] :]], axis=1)
@@ -596,7 +622,7 @@
         out_shape=outs,
         scratch_shapes=[pltpu.VMEM((2 * depth, columns), F32)],
         compiler_params=params(40),
-        cost_estimate=cost(50),
+        cost_estimate=cost(50 if parent else 30),
         name="token_grads",
     )(near, far, dwin, more)
 
@@ -627,7 +653,7 @@
     return pl.pallas_call(
         functools.partial(attention_backward, rows // 3 // HEAD, lengths, segments, bank),
         grid=(groups,),
-        in_specs=[SMEM] * 3 + [step_block(window), step_block(parent), step_block(dctx), step_block(lse)],
+        in_specs=[SMEM] * 3 + [step_block(array) for array in (window, parent, dctx, lse)],
         out_specs=[step_block(out) for out in outs],
         out_shape=outs,
         compiler_params=params(40),
@@ -643,6 +669,7 @@
 
 SMEM = pl.BlockSpec(memory_space=pltpu.SMEM)
 VMEM = pl.BlockSpec(memory_space=pltpu.VMEM)
+HBM = pl.BlockSpec(memory_space=pltpu.HBM)
 ORDER = (0, 2, 1, 3)
 SENDS = ((0, 0), (1, 0), (2, 0), (1, 1))
 
@@ -663,33 +690,40 @@
     ).astype(BF16)
 
 
-def pack_weights_kernel(
-    here_ref,
-    query_ref,
-    key_ref,
-    value_ref,
-    out_ref,
-    up_ref,
-    down_ref,
-    up_b_ref,
-    query_b_ref,
-    value_b_ref,
-    half_ref,
-    turned_ref,
-):
-    feat, width = query_ref.shape
+def as_row(ref):
+    return ref[...].astype(F32).reshape(1, ref.shape[0])
+
+
+def fetch(pairs, sem):
+    copies = [pltpu.make_async_copy(source, target, sem.at[i]) for i, (source, target) in enumerate(pairs)]
+    for copy in copies:
+        copy.start()
+    for copy in copies:
+        copy.wait()
+
+
+def pack_weights_kernel(here_ref, *refs):
+    count = 9
+    inputs, half_ref = refs[:count], refs[count]
+    held, turned_ref, sem = refs[count + 1 : -2], refs[-2], refs[-1]
+    feat, width = inputs[0].shape
     half = feat // 2
     rows = pl.ds(flipped(here_ref, 0, half), half)
+    small = [inputs[i] for i in (0, 1, 2, 3, 6, 7, 8)]
+    fetch(
+        [*zip(small, held)]
+        + [(inputs[4 + i].at[rows, :], half_ref.at[pl.ds((1 + i) * half, half), :]) for i in range(2)],
+        sem,
+    )
+    query_ref, key_ref, value_ref, out_ref, up_b_ref, query_b_ref, value_b_ref = held
     turned_ref[...] = tn(out_ref[...], spots(width, width, 0)).astype(BF16)
     for i, ref in enumerate((query_ref, key_ref, value_ref, turned_ref)):
         half_ref[:half, i * width : (i + 1) * width] = ref[rows, :]
-    half_ref[half : 2 * half] = up_ref[rows, :]
-    half_ref[2 * half : 3 * half] = down_ref[rows, :]
     zero = jnp.zeros((1, width), F32)
-    joint = [query_b_ref[...].astype(F32), zero, value_b_ref[...].astype(F32), zero]
+    joint = [as_row(query_b_ref), zero, as_row(value_b_ref), zero]
     wide = (half_ref.shape[0] - 3 * half, half_ref.shape[1])
     index = lax.broadcasted_iota(jnp.int32, wide, 0)
-    up_row = jnp.broadcast_to(up_b_ref[...].astype(F32), wide)
+    up_row = jnp.broadcast_to(as_row(up_b_ref), wide)
     joint_row = jnp.broadcast_to(jnp.concatenate(joint, axis=1), wide)
     half_ref[3 * half :] = jnp.where(index == 0, up_row, jnp.where(index == 1, joint_row, 0.0)).astype(BF16)
 
@@ -697,26 +731,34 @@
 def pack_weights(here, query, key, value, out, up, down, *biases):
     feat, width = query.shape
     hidden = up.shape[1]
+    inputs = (query, key, value, out, up, down, *biases)
+    small = [query, key, value, out, *biases]
     return pl.pallas_call(
         pack_weights_kernel,
-        in_specs=[SMEM] + [VMEM] * 9,
+        in_specs=[SMEM] + [HBM] * len(inputs),
         out_specs=VMEM,
         out_shape=jax.ShapeDtypeStruct((3 * feat // 2 + 16, hidden), BF16),
-        scratch_shapes=[pltpu.VMEM((feat, width), BF16)],
+        scratch_shapes=[pltpu.VMEM(array.shape, array.dtype) for array in small]
+        + [pltpu.VMEM((feat, width), BF16), pltpu.SemaphoreType.DMA((len(inputs),))],
         compiler_params=params(24),
         cost_estimate=cost(0.1),
         name="pack_weights",
-    )(here, query, key, value, out, up, down, *[bias.reshape(1, -1) for bias in biases])
-
-
-def pack_kernel(blocks, sided, here_ref, source_ref, *refs):
+    )(here, *held(*inputs))
+
+
+def pack_kernel(blocks, sided, here_ref, *refs):
+    given = 1 + sided
+    outs, held, sem = refs[given : given + 3], refs[given + 3 : given + 3 + given], refs[-1]
+    fetch([*zip(refs[:given], held)], sem)
+    source_ref = held[0]
     half = source_ref.shape[0] // 2
     count = len(blocks[0])
-    outs = refs[2:5] if sided else refs
     if sided:
-        mem_ref, vec_ref, side_ref = refs[0], refs[1], refs[5]
+        mem_ref, vector_refs, side_ref = held[1], held[2:], refs[-2]
         bank = mem_ref.shape[0]
-        side = tn(mem_ref[...], spots(bank, 128, 0)) + tn(vec_ref[...], spots(vec_ref.shape[0], 128, bank))
+        vectors = jnp.concatenate([as_row(ref) for ref in vector_refs], axis=0)
+        vectors = jnp.concatenate([vectors, jnp.zeros((8 - len(vector_refs), vectors.shape[1]), F32)], axis=0)
+        side = tn(mem_ref[...], spots(bank, 128, 0)) + tn(vectors.astype(BF16), spots(8, 128, bank))
         side_ref[...] = side.astype(BF16)
     for slot, (out, place) in enumerate(SENDS):
         for part in range(2):
@@ -732,16 +774,19 @@
 def pack(blocks, here, source, *side):
     feat = source.shape[0]
     columns = len(blocks[0]) * 128 + (128 if side else 0)
-    return pl.pallas_call(
-        functools.partial(pack_kernel, blocks, bool(side)),
-        in_specs=[SMEM] + [VMEM] * (1 + len(side)),
+    inputs = (source, *side)
+    return pl.pallas_call(
+        functools.partial(pack_kernel, blocks, len(side)),
+        in_specs=[SMEM] + [HBM] * len(inputs),
         out_specs=[VMEM] * 3,
         out_shape=[jax.ShapeDtypeStruct((n, feat, columns), source.dtype) for n in (1, 2, 1)],
-        scratch_shapes=[pltpu.VMEM((feat, 128), BF16)] if side else [],
+        scratch_shapes=[pltpu.VMEM(array.shape, array.dtype) for array in inputs]
+        + ([pltpu.VMEM((feat, 128), BF16)] if side else [])
+        + [pltpu.SemaphoreType.DMA((len(inputs),))],
         compiler_params=params(24),
         cost_estimate=cost(0.1),
         name="pack",
-    )(here, source, *side)
+    )(here, *held(*inputs))
 
 
 def exchange(keep, along, near):
@@ -761,9 +806,11 @@
     return parents_ref[here_ref[0] * here_ref[3] + at_distance(here_ref, segments, slot, j)]
 
 
-def pick_kernel(segments, here_ref, parents_ref, source_ref, *outs):
+def pick_kernel(segments, here_ref, parents_ref, source_ref, *refs):
+    outs, sem = refs[:3], refs[3]
     half = source_ref.shape[1] // 2
     seg_row = here_ref[3]
+    pairs = []
     for slot, (out, place) in enumerate(SENDS):
         for j in range(len(segments[0])):
             seg = jnp.maximum(parent_of(here_ref, parents_ref, segments, slot, j), 0)
@@ -771,9 +818,9 @@
             at = pl.multiple_of((seg - row * seg_row) * SEG, SEG)
             for part in range(2):
                 rows = slice(part * half, (part + 1) * half)
-                outs[out][place, rows, j * SEG : (j + 1) * SEG] = source_ref[
-                    row, pl.ds(flipped(here_ref, part, half), half), pl.ds(at, SEG)
-                ]
+                source = source_ref.at[row, pl.ds(flipped(here_ref, part, half), half), pl.ds(at, SEG)]
+                pairs.append((source, outs[out].at[place, rows, pl.ds(j * SEG, SEG)]))
+    fetch(pairs, sem)
 
 
 def pick_parents(segments, here, parents, gathered):
@@ -781,18 +828,20 @@
     columns = len(segments[0]) * SEG
     return pl.pallas_call(
         functools.partial(pick_kernel, segments),
-        in_specs=[SMEM, SMEM, VMEM],
+        in_specs=[SMEM, SMEM, HBM],
         out_specs=[VMEM] * 3,
         out_shape=[jax.ShapeDtypeStruct((n, feat, columns), gathered.dtype) for n in (1, 2, 1)],
+        scratch_shapes=[pltpu.SemaphoreType.DMA((8 * len(segments[0]),))],
         compiler_params=params(24),
         cost_estimate=cost(1),
         name="pick_parents",
-    )(here, parents, gathered)
+    )(here, parents, *held(gathered))
 
 
 def add_parents_kernel(segments, seg_row, here_ref, parents_ref, *refs):
-    pieces, out_ref, sum_ref = refs[:3], refs[3], refs[4]
+    pieces, given_ref, sum_ref, out_ref, sem = refs[:3], refs[3], refs[4], refs[5], refs[6]
     window = len(segments[0]) * SEG
+    copies = []
     sum_ref[...] = jnp.zeros(sum_ref.shape, F32)
     for slot, (piece, place) in enumerate(PIECES):
         for j in range(len(segments[0])):
@@ -807,6 +856,10 @@
         for s in range(seg_row):
             out_ref[r, :, s * SEG : (s + 1) * SEG] = sum_ref[r * seg_row + s].astype(BF16)
         out_ref[r, :, seg_row * SEG :] = mem.astype(BF16)
+        copies.append(pltpu.make_async_copy(out_ref.at[r], given_ref.at[r], sem.at[r]))
+        copies[-1].start()
+    for copy in copies:
+        copy.wait()
 
 
 def add_parents(segments, here, parents, pieces, rows, seg_row):
@@ -815,11 +868,15 @@
     return pl.pallas_call(
         functools.partial(add_parents_kernel, segments, seg_row),
         in_specs=[SMEM, SMEM, VMEM, VMEM, VMEM],
-        out_specs=VMEM,
-        out_shape=jax.ShapeDtypeStruct((rows, feat, seg_row * SEG + bank), BF16),
-        scratch_shapes=[pltpu.VMEM((rows * seg_row, feat, SEG), F32)],
+        out_specs=HBM,
+        out_shape=pltpu.HBM((rows, feat, seg_row * SEG + bank), BF16),
+        scratch_shapes=[
+            pltpu.VMEM((rows * seg_row, feat, SEG), F32),
+            pltpu.VMEM((rows, feat, seg_row * SEG + bank), BF16),
+            pltpu.SemaphoreType.DMA((rows,)),
+        ],
         compiler_params=params(40),
-        cost_estimate=cost(20),
+        cost_estimate=cost(60),
         name="add_parents",
     )(here, parents, *pieces)
 
@@ -875,14 +932,40 @@
     )(here, *pieces)
 
 
+def unpack_kernel(width, count, here_ref, mine_ref, other_ref, query_ref, key_ref, value_ref, out_ref, more_ref, all_ref):
+    half = mine_ref.shape[0]
+    all_ref[pl.ds(flipped(here_ref, 0, half), half), :] = mine_ref[...].astype(F32)
+    all_ref[pl.ds(flipped(here_ref, 1, half), half), :] = other_ref[...].astype(F32)
+    for i, ref in enumerate((query_ref, key_ref, value_ref)):
+        ref[...] = all_ref[:, i * width : (i + 1) * width]
+    out_ref[...] = all_ref[:, 3 * width : 4 * width].T
+    rows = all_ref[:, 4 * width :].T
+    more_ref[...] = rows[: more_ref.shape[0]]
+
+
+def unpack(here, mine, other, width, count):
+    feat = 2 * mine.shape[0]
+    square = jax.ShapeDtypeStruct((feat, width), F32)
+    return pl.pallas_call(
+        functools.partial(unpack_kernel, width, count),
+        in_specs=[SMEM, VMEM, VMEM],
+        out_specs=[VMEM] * 5,
+        out_shape=[square] * 3 + [jax.ShapeDtypeStruct((width, feat), F32), jax.ShapeDtypeStruct((24, feat), F32)],
+        scratch_shapes=[pltpu.VMEM((feat, mine.shape[1]), F32)],
+        compiler_params=params(24),
+        cost_estimate=cost(2),
+        name="unpack",
+    )(here, mine, other)
+
+
 def gather_weights(half):
     return [half] + [swap(half, "row", n) for n in range(1, lax.axis_size("row"))]
 
 
-def spread_weights(along):
+def spread_weights(along, *gate):
     along = jnp.stack(along, axis=1)
     opposite = swap(along, "leaf", 1)
-    across = swap(along, "col", 2)
+    across = after(swap(along, "col", 2), *gate)
     return along, opposite, across, swap(across, "leaf", 1)
 
 
@@ -908,6 +991,16 @@
 def reduce_across(keep, near):
     shape = reduce_blocks(keep)
     return add_up(keep.reshape(shape)[:, :, 1], near.reshape(shape)[:, :, 1]).astype(BF16)
+
+
+def reduce_y(keep, near):
+    shape = reduce_blocks(keep)
+    return add_up(keep.reshape(shape)[:, 1], near.reshape(shape)[:, 1]).astype(BF16)
+
+
+def reduce_x(keep, near, got):
+    shape = reduce_blocks(keep)
+    return add_up(keep.reshape(shape)[:, 0, 1], near.reshape(shape)[:, 0, 1], got[:, 1]).astype(BF16)
 
 
 def reduce_up(keep, near, across):
@@ -1024,9 +1117,8 @@
     )
     along = gather_weights(weight_half)
 
-    zero = jnp.zeros((feat,), BF16)
-    vectors = jnp.stack([out_bias, norm_gain, norm_shift, down_bias, final_gain, final_shift, zero, zero])
-    token_sends = pack(blocks, here, after(tokens, weight_half), memory, vectors)
+    vectors = (out_bias, norm_gain, norm_shift, down_bias, final_gain, final_shift)
+    token_sends = pack(blocks, here, after(tokens, weight_half), memory, *vectors)
     cot_sends = pack(own_blocks, here, after(cotangent, token_sends))
     token_got = swap(token_sends[1], "col", 2)
     along = after(along, cot_sends, token_got)
@@ -1035,97 +1127,99 @@
     near_first, far_first = (array[0] for array in whole_weights(spread_weights([piece[:half][None] for piece in along])))
     token_last = swap(jnp.concatenate([token_sends[2], token_got[1:]], axis=0), "col", 1)
     tok_window = joined((token_sends[0], token_got, token_last)).reshape(model, window + tail)
-    second_parts = spread_weights([piece[half : 3 * half].reshape(2, half, -1) for piece in along])
     win = project(near_first, far_first, tok_window, row_vectors, 0, 3 * width, width)
-    out_t = jnp.concatenate([near_first[:, :, 3 * width :], far_first[:, :, 3 * width :]], axis=1)
-    out_t = out_t.transpose(1, 0, 2).reshape(model, rows * width)
-    everything = after(everything, win, out_t, second_parts[2])
+    second_parts = spread_weights([piece[half : 3 * half].reshape(2, half, -1) for piece in along], win)
+    cot_keep, cot_along, cot_near = after(cot_sends, second_parts[2])
+    cot_got = swap(cot_along, "col", 2)
+    cot_near = jnp.concatenate([cot_near, cot_got[1:]], axis=0)
+    cot_pieces = cot_keep, cot_got, swap(cot_near, "col", 1)
+    everything = after(everything, second_parts[2], cot_near)
     par_keep, par_along, par_near = pick_parents(segments, here, parents, everything)
     par_got = swap(par_along, "col", 2)
     near, far = whole_weights(after(second_parts, par_along))
     par_got = after(par_got, near)
     par_near = jnp.concatenate([par_near, par_got[1:]], axis=0)
-    tok_parent = joined((par_keep, par_got, swap(par_near, "col", 1))).reshape(model, window)
+    tok_parent = (par_keep, par_got, swap(par_near, "col", 1))
     par = project(near_first, far_first, tok_parent, row_vectors, width, 3 * width, 0)
-    cot_keep, cot_along, cot_near = after(cot_sends, par_near)
-    cot_got = swap(cot_along, "col", 2)
     ctx, lse = attend(lengths, segments, bank, scalars, win, par)
-    cot_got = after(cot_got, ctx)
-    cot_pieces = cot_keep, cot_got, swap(jnp.concatenate([cot_near, cot_got[1:]], axis=0), "col", 1)
     at = window + bank
-    *result, active, slope, second_grad, down_low, hidden_low, normed, scale, last_sums = mlp_forward(
-        at, ctx.reshape(rows * width, own), tok_window, cot_pieces, out_t, near, far, row_vectors
+    *result, active, upper_low, hidden_low, down_low, first_low, dctx, up_bias_grad, sums = mlp(
+        at, ctx, tok_window, cot_pieces, near_first, far_first, near, far, row_vectors
     )
-    down_keep, down_send = down_grads(down_low, active)
-    up_keep, up_send, first_grad, first_low, dctx, up_bias_grad, first_sums = mlp_backward(
-        at, after(down_low, down_send), slope, hidden_low, near, far, second_grad, normed, scale, tok_window, out_t
+    result_keep, result_along, result_near = result
+    dwin, dpar = attend_back(lengths, segments, bank, scalars, win, par, dctx, lse)
+
+    par_keep, par_along, par_near = token_grads(
+        near_first, far_first, dwin, dpar, width, 3 * width, True, window + tail
     )
+    par_got = swap(par_along, "col", 2)
+    down_keep, down_send, up_keep, up_send = hidden_grads(after(down_low, par_along), hidden_low, active, upper_low)
     down_near, up_near = swap(down_send, "col", 1), swap(up_send, "col", 1)
-    down_across = reduce_across(after(down_keep, dctx), down_near)
-    up_across = reduce_across(after(up_keep, down_across), up_near)
-    dctx = after(dctx, down_across, up_across).reshape(rows, width, own)
-    dwin, dpar = attend_back(lengths, segments, bank, scalars, win, par, dctx, lse)
-
-    dtok_par = token_grads(near_first, far_first, dwin, dpar, width, 3 * width, True, window + tail)
-    par_keep, par_along, par_near = dtok_par
-    par_got = swap(par_along, "col", 2)
-    first_low = after(first_low, par_along)
+    par_got = after(par_got, up_send)
+    par_near = jnp.concatenate([par_near, par_got[1:]], axis=0)
+    placed = add_parents(segments, here, parents, (par_keep, par_got, swap(par_near, "col", 1)), rows, seg_row)
+    down_across = reduce_across(after(down_keep, placed), down_near)
+    up_along = reduce_y(after(up_keep, down_across), up_near)
     first_keep, first_send = first_grads(
-        tok_window, tok_parent, dwin, dpar, first_low, ctx, up_bias_grad, first_sums, last_sums
+        tok_window, tok_parent, dwin, dpar, after(first_low, up_along), ctx, up_bias_grad, sums
     )
-    par_got = after(par_got, first_send)
-    par_near = jnp.concatenate([par_near, par_got[1:]], axis=0)
+    placed = lax.psum_scatter(placed, "row", scatter_dimension=0, tiled=False)
     first_near = swap(first_send, "col", 1)
+    dtok = token_grads(near_first, far_first, dwin, after(first_low, first_send), 0, 3 * width, False, window)
+    corner = reduce_corner(after(first_keep, dtok), first_near)
+    by_leaf, by_col = swap(corner[0], "leaf", 1), swap(corner[1], "col", 2)
+    up_got = swap(up_along, "col", 2)
+    up_across = reduce_x(after(up_keep, corner), up_near, up_got)
     down_across = swap(down_across, "leaf", 1)
-    down_up = reduce_up(after(down_keep, par_near), down_near, down_across)
-    par_last = after(swap(par_near, "col", 1), down_up)
-    placed = add_parents(segments, here, parents, (par_keep, par_got, par_last), rows, seg_row)
-    corner = reduce_corner(after(first_keep, placed), first_near)
-    by_leaf, by_col = swap(corner[0], "leaf", 1), swap(corner[1], "col", 2)
-    dtok = token_grads(near_first, far_first, dwin, after(first_grad, corner), 0, 3 * width, False, window)
-    placed = lax.psum_scatter(placed, "row", scatter_dimension=0, tiled=False)
-    edges = reduce_edges(after(first_keep, dtok), first_near, by_leaf, by_col)
+    down_up = reduce_up(after(down_keep, up_across), down_near, down_across)
+    edges = reduce_edges(after(first_keep, down_up), first_near, by_leaf, by_col)
     by_leaf, by_col = swap(edges[0], "leaf", 1), swap(edges[1], "col", 2)
     up_across = swap(up_across, "leaf", 1)
-    up_up = reduce_up(after(up_keep, edges), up_near, up_across)
+    up_rows = reduce_mine(after(up_keep, edges), up_near, up_got[:, 0], up_across)
     down_up = swap(down_up, "col", 2)
-    down_rows = reduce_along(after(down_keep, up_up), down_near, down_across, down_up)
-    up_up = swap(up_up, "col", 2)
-    up_rows = reduce_along(after(up_keep, down_rows), up_near, up_across, up_up)
-    first_rows = reduce_mine(after(first_keep, up_rows), first_near, by_leaf, by_col)
-    result_pieces = exchange(*after(result, first_rows))
+    down_rows = reduce_along(after(down_keep, up_rows), down_near, down_across, down_up)
+    result_got = after(swap(result_along, "col", 2), down_rows)
+    result_near = jnp.concatenate([result_near, result_got[1:]], axis=0)
+    result_pieces = result_keep, result_got, swap(result_near, "col", 1)
+    first_rows = reduce_mine(after(first_keep, down_rows), first_near, by_leaf, by_col)
+    dtok_keep, dtok_along, dtok_near = dtok
+    dtok_got = after(swap(dtok_along, "col", 2), first_rows, result_near)
+    dtok_near = jnp.concatenate([dtok_near, dtok_got[1:]], axis=0)
+    layer_output = place(own_blocks, here, result_pieces, row_tokens)
+    mem_sum = placed[:, row_tokens : row_tokens + bank].astype(F32)
+    memory_grad = jnp.where(parity == 0, mem_sum, jnp.roll(mem_sum, half, axis=0)).T
+    tokens_grad = finish_tokens(
+        blocks, here, placed, (dtok_keep, dtok_got, swap(dtok_near, "col", 1)), row_tokens
+    )
     down_got, up_got, first_got = send_rows(down_rows), send_rows(up_rows), send_rows(first_rows)
+    down_rows, up_rows = after((down_rows, up_rows), first_rows)
     second_mine = jnp.concatenate([reduce_rows(down_rows, down_got), reduce_rows(up_rows, up_got)], axis=1)
     second_other = swap(second_mine, "leaf", 1)
-    first_mine = reduce_rows(after(first_rows, second_mine), first_got)
+    first_mine = reduce_rows(after(first_rows, second_mine, tokens_grad, memory_grad, layer_output), first_got)
     first_other = swap(first_mine, "leaf", 1)
-    layer_output = place(own_blocks, here, result_pieces, row_tokens)
 
     def in_order(mine, other):
         return jnp.where(
             parity == 0, jnp.concatenate([mine, other], axis=0), jnp.concatenate([other, mine], axis=0)
         ).astype(F32)
 
-    second_total, first_total = in_order(second_mine, second_other), in_order(first_mine, first_other)
+    second_total = in_order(second_mine, second_other)
     down_total, up_total = second_total[:, :hidden_width], second_total[:, hidden_width:]
     count = (2 * width + hidden_width) // half
-    by_row = first_mine[:, 4 * width : 4 * width + count].astype(F32).T.reshape(-1)
-    by_col = first_total[:, 4 * width + count : 4 * width + count + 6].T
-
-    mem_sum = placed[:, row_tokens : row_tokens + bank].astype(F32)
-    memory_grad = jnp.where(parity == 0, mem_sum, jnp.roll(mem_sum, half, axis=0)).T
-    tokens_grad = finish_tokens(blocks, here, placed, exchange(*dtok), row_tokens)
+    first_query, first_key, first_value, first_out, vectors = unpack(here, first_mine, first_other, width, count + 6)
+    by_row = vectors[:count, :half].reshape(-1)
+    by_col = vectors[count : count + 6]
 
     return (
         layer_output,
         tokens_grad,
         memory_grad,
-        first_total[:, :width],
+        first_query,
         by_row[:width],
-        first_total[:, width : 2 * width],
-        first_total[:, 2 * width : 3 * width],
+        first_key,
+        first_value,
         by_row[width : 2 * width],
-        first_total[:, 3 * width : 4 * width].T,
+        first_out,
         by_col[0],
         by_col[1],
         by_col[2],

time: 458 us -> 416 us (0.908)
  other arithmetic: 36.7 us -> 21.9 us
  local copies, waits for them, and re-layouts: 53.9 us -> 40.7 us
  waiting for transfers between devices: 167 us -> 154 us
    ppermute x45, waiting for transfers between devices: 167 us -> 151 us  [swap(): return lax.ppermute(array, axis, [(i, i ^ mask) for i in range(count)])]
    convert_element_type x2 -> x1, other arithmetic: 6.41 us -> 1.77 us  [reduce_across(): add_up(keep.reshape(shape)[:, :, 1], near.reshape(shape)[:, :, 1])]
    unnamed x135 -> x128, local copies, waits for them, and re-layouts: 33.4 us -> 30.4 us
  transfers between devices with their start and end apart: 47 -> 47, of which waited for: 18 -> 25; matrix products, arithmetic and copies ran while one was open for 11% -> 6% of each run, Pallas kernels for 21% -> 16%
where the time goes in v3:
time: 416 us; the launch traced here: 408 us
  waiting for transfers between devices  154 us (37%)
  Pallas kernels  132 us (32%)
  starting transfers between devices  44.4 us (11%)
  local copies, waits for them, and re-layouts  40.7 us (10%)
  other arithmetic  21.9 us (5%)
  between operations  15.4 us (4%)
    ppermute x45, waiting for transfers between devices, swap(): return lax.ppermute(array, axis, [(i, i ^ mask) for i in range(count)])  151 us
    ppermute x45, starting transfers between devices, swap(): return lax.ppermute(array, axis, [(i, i ^ mask) for i in range(count)])  44.4 us
    pallas_call x1, Pallas kernels, mlp(): pl.pallas_call(functools.partial(mlp_kernel, at), grid=(2 * groups,), in_...  35.9 us
    unnamed x128, local copies, waits for them, and re-layouts  30.4 us
    pallas_call x1, Pallas kernels, attend_back(): pl.pallas_call(functools.partial(attention_backward, rows // 3 // HEAD, l...  20.1 us
    pallas_call x1, Pallas kernels, attend(): pl.pallas_call(functools.partial(attention_forward, heads, lengths, segme...  13.5 us
    pallas_call x1, Pallas kernels, first_grads(): pl.pallas_call(functools.partial(first_grad_kernel, width), grid=(groups,...  12.7 us
    pallas_call x2, Pallas kernels, project(): pl.pallas_call(functools.partial(project_kernel, low, high, scaled), grid...  12.1 us
  transfers between devices with their start and end apart: 47, of which 25 were waited for; matrix products, arithmetic and copies ran while one was open for 6% of the time, Pallas kernels for 16%

profile of v3, /device:TPU:0, one launch (start us, length us, event | category | flops | bytes accessed | tf_op | source)
XLA Modules:
  0.0 407.6 jit_solution(15122214068186759967)
XLA Ops:
  9.5 2.3 pack.2
  11.7 3.0 collective-permute-start.3
  14.8 3.6 collective-permute-start.2
  23.3 7.0 %collective-permute-done.2 = bf16[304,768]{1,0:T(8,128)(2,1)S(1)} collective-permute-done((bf16[304,768]{1,0:T(8,128)(2,1)S(1)}, bf16[304,768]{1,0:T(8,128)(2,1)S(1)}, u32[]{:S(2)}, u32[]{:S(2)}) %collective-permute-start.2) | collective-permute-done | bytes 466976 | tf_op jit(solution)/shard_map/ppermute | solution.py:667
  30.3 27.7 %collective-permute-done.1 = bf16[304,768]{1,0:T(8,128)(2,1)S(1)} collective-permute-done((bf16[304,768]{1,0:T(8,128)(2,1)S(1)}, bf16[304,768]{1,0:T(8,128)(2,1)S(1)}, u32[]{:S(2)}, u32[]{:S(2)}) %collective-permute-start.1) | collective-permute-done | bytes 466976 | tf_op jit(solution)/shard_map/ppermute | solution.py:667
  62.8 12.3 %collective-permute-done.5 = bf16[1,4,96,768]{3,2,1,0:T(8,128)(2,1)S(1)} collective-permute-done((bf16[1,4,96,768]{3,2,1,0:T(8,128)(2,1)S(1)}, bf16[1,4,96,768]{3,2,1,0:T(8,128)(2,1)S(1)}, u32[]{:S(2)}, u32[]{:S(2)}) %collective-permute-start.5) | collective-permute-done | bytes 589856 | tf_op jit(solution)/shard_map/ppermute | solution.py:667
  76.7 12.0 %collective-permute-done.6 = bf16[1,4,96,768]{3,2,1,0:T(8,128)(2,1)S(1)} collective-permute-done((bf16[1,4,96,768]{3,2,1,0:T(8,128)(2,1)S(1)}, bf16[1,4,96,768]{3,2,1,0:T(8,128)(2,1)S(1)}, u32[]{:S(2)}, u32[]{:S(2)}) %collective-permute-start.6) | collective-permute-done | bytes 589856 | tf_op jit(solution)/shard_map/ppermute | solution.py:667
  95.6 5.9 %project.2.win_ref = bf16[4,576,896]{2,1,0:T(8,128)(2,1)S(1)} custom-call(bf16[4,384,768]{2,1,0:T(8,128)(2,1)S(1)} %bitcast.206, bf16[4,384,768]{2,1,0:T(8,128)(2,1)S(1)} %bitcast.211, bf16[768,896]{1,0:T(8,128)(2,1)S(1)} %bitcast.216, bf16[4,16,768]{2,1,0:T(8,128)(2,1)S(1)} %pad_maximum_fusion.14.refs_1_.refs_3_.bias_ref), custom_call_target="tpu_custom_call" | custom-call | flops 100000000 | tf_op jit(solution)/shard_map/project/pallas_call | solution.py:232
  103.5 15.7 %collective-permute-done.9 = bf16[2,4,96,768]{3,2,0,1:T(8,128)(2,1)} collective-permute-done((bf16[2,4,96,768]{3,2,0,1:T(8,128)(2,1)}, bf16[2,4,96,768]{3,2,0,1:T(8,128)(2,1)}, u32[]{:S(2)}, u32[]{:S(2)}) %collective-permute-start.9) | collective-permute-done | bytes 1179680 | tf_op jit(solution)/shard_map/ppermute | solution.py:667
  121.6 9.9 %collective-permute-done.10.cot_got = bf16[2,192,640]{2,1,0:T(8,128)(2,1)S(1)} collective-permute-done((bf16[2,192,640]{2,1,0:T(8,128)(2,1)S(1)}, bf16[2,192,640]{2,1,0:T(8,128)(2,1)S(1)}, u32[]{:S(2)}, u32[]{:S(2)}) %collective-permute-start.10) | collective-permute-done | bytes 491552 | tf_op jit(solution)/shard_map/ppermute | solution.py:667
  139.0 8.2 %collective-permute-done.13 = bf16[2,4,96,768]{3,2,0,1:T(8,128)(2,1)} collective-permute-done((bf16[2,4,96,768]{3,2,0,1:T(8,128)(2,1)}, bf16[2,4,96,768]{3,2,0,1:T(8,128)(2,1)}, u32[]{:S(2)}, u32[]{:S(2)}) %collective-permute-start.13) | collective-permute-done | bytes 1179680 | tf_op jit(solution)/shard_map/ppermute | solution.py:667
  147.2 2.6 pad_maximum_fusion
  149.8 2.6 copy.58
  157.5 6.3 %project.3.par_ref = bf16[4,384,768]{2,1,0:T(8,128)(2,1)S(1)} custom-call(bf16[4,384,768]{2,1,0:T(8,128)(2,1)S(1)} %bitcast.207, bf16[4,384,768]{2,1,0:T(8,128)(2,1)S(1)} %bitcast.213, bf16[1,192,768]{2,1,0:T(8,128)(2,1)S(1)} %get-tuple-element.111.refs_0_.par_keep, bf16[2,192,768]{2,1,0:T(8,128)(2,1)S(1)} %collective-permute-done.11.refs_1_.par_got, ...), custom_call_target="tpu_custom_call" | custom-call | flops 100000000 | tf_op jit(solution)/shard_map/project/pallas_call | solution.py:232
  163.8 13.5 %attention_forward.1 = (bf16[4,192,640]{2,1,0:T(8,128)(2,1)S(1)}, f32[4,3,640]{2,1,0:T(4,128)S(1)}) custom-call(s32[4]{0:T(128)S(1)} %pad_add_fusion.here_ref, s32[40]{0:T(128)S(1)} %copy-done.25, s32[40,20]{1,0:T(8,128)S(1)} %copy.59.slots_ref, bf16[4,576,896]{2,1,0:T(8,128)(2,1)S(1)} %copy-done.11, bf16[4,384,768]{2,1,0:T(8,128)(2,1)S(1)} %project.3.par_ref), custom_call_target="tpu_custom_call" | custom-call | flops 130000003072 | tf_op jit(solution)/shard_map/attention_forward/pallas_call | solution.py:638
  177.4 2.2 copy-done.62
  179.7 35.9 %mlp.1 = (bf16[1,192,640]{2,1,0:T(8,128)(2,1)S(1)}, bf16[2,192,640]{2,1,0:T(8,128)(2,1)}, bf16[1,192,640]{2,1,0:T(8,128)(2,1)S(1)}, bf16[4,768,640]{2,1,0:T(8,12...) custom-call(bf16[4,192,640]{2,1,0:T(8,128)(2,1)S(1)} %get-tuple-elem, ...), custom_call_target="tpu_custom_call" | custom-call | flops 399999991808 | tf_op jit(solution)/shard_map/mlp/pallas_call | solution.py:459
  221.1 20.1 %attention_backward.1 = (bf16[4,576,896]{2,1,0:T(8,128)(2,1)S(1)}, bf16[4,384,768]{2,1,0:T(8,128)(2,1)S(1)}) custom-call(s32[4]{0:T(128)S(1)} %pad_add_fusion.here_ref, s32[40]{0:T(128)S(1)} %copy-done.25, s32[40,20]{1,0:T(8,128)S(1)} %copy.59.slots_ref, bf16[4,576,896]{2,1,0:T(8,128)(2,1)S(1)} %copy-done.12, bf16[4,384,768]{2,1,0:T(8,128)(2,1)S(1)} %copy-done.17, ...), custom_call_target="tpu_custom_call" | custom-call | flops 199999995904 | tf_op jit(solution)/shard_map/attention_backward/pallas_call | solution.py:653
  241.3 4.4 %token_grads.2 = (bf16[1,192,896]{2,1,0:T(8,128)(2,1)S(1)}, bf16[2,192,896]{2,1,0:T(8,128)(2,1)S(1)}, bf16[1,192,896]{2,1,0:T(8,128)(2,1)S(1)}) custom-call(bf16[4,384,768]{2,1,0:T(8,128)(2,1)S(1)} %bitcast.209, bf16[4,384,768]{2,1,0:T(8,128)(2,1)S(1)} %bitcast.214, bf16[4,576,896]{2,1,0:T(8,128)(2,1)S(1)} %get-tuple-element.126.dwin_ref, ...), custom_call_target="tpu_custom_call" | custom-call | flops 49999998976 | tf_op jit(solution)/shard_map/token_grads/pallas_call | solution.py:612
  251.5 9.0 %hidden_grads.1 = (bf16[4,384,768]{2,1,0:T(8,128)(2,1)S(1)}, bf16[4,384,768]{2,1,0:T(8,128)(2,1)}, bf16[4,384,768]{2,1,0:T(8,128)(2,1)S(1)}, bf16[4,384,768]{2,1,0:T(8,128)(2,1)}) custom-call(bf16[768,640]{1,0:T(8,128)(2,1)S(1)} %copy-done.50, bf16[768,640]{1,0:T(8,128)(2,1)S(1)} %copy-done.48, bf16[4,768,640]{2,1,0:T(8,128)(2,1)S(1)} %copy-done.45, ...), custom_call_target="tpu_custom_call" | custom-call | flops 99999997952 | tf_op jit(solution)/shard_map/hidden_grads/pallas_call | solution.py:505
  265.8 3.6 add_parents.1
  269.4 3.3 collective-permute-done.20
  282.9 12.7 %first_grads.1 = (bf16[4,384,896]{2,1,0:T(8,128)(2,1)S(1)}, bf16[4,384,896]{2,1,0:T(8,128)(2,1)}) custom-call(bf16[768,896]{1,0:T(8,128)(2,1)S(1)} %bitcast.218, bf16[1,192,768]{2,1,0:T(8,128)(2,1)S(1)} %get-tuple-element.111.refs_0_.par_keep, bf16[2,192,768]{2,1,0:T(8,128)(2,1)S(1)} %collective-permute-done.11.refs_1_.par_got, ...), custom_call_target="tpu_custom_call" | custom-call | flops 15000000512 | tf_op jit(solution)/shard_map/first_grads/pallas_call | solution.py:560
  297.7 5.6 %token_grads.3 = (bf16[1,192,768]{2,1,0:T(8,128)(2,1)S(1)}, bf16[2,192,768]{2,1,0:T(8,128)(2,1)}, bf16[1,192,768]{2,1,0:T(8,128)(2,1)S(1)}) custom-call(bf16[4,384,768]{2,1,0:T(8,128)(2,1)S(1)} %bitcast.210, bf16[4,384,768]{2,1,0:T(8,128)(2,1)S(1)} %bitcast.215, bf16[4,576,896]{2,1,0:T(8,128)(2,1)S(1)} %copy-done.35, bf16[768,640]{1,0:T(8,128)(2,1)S(1)} %copy-done.42), custom_call_target="tpu_custom_call" | custom-call | flops 30000001024 | tf_op jit(solution)/shard_map/token_grads/pallas_call | solution.py:612
  311.4 15.6 %collective-permute-done.25 = bf16[2,96,896]{2,1,0:T(8,128)(2,1)S(1)} collective-permute-done((bf16[2,96,896]{2,1,0:T(8,128)(2,1)S(1)}, bf16[2,96,896]{2,1,0:T(8,128)(2,1)S(1)}, u32[]{:S(2)}, u32[]{:S(2)}) %collective-permute-start.25) | collective-permute-done | bytes 344096 | tf_op jit(solution)/shard_map/ppermute | solution.py:667
  329.4 13.9 %collective-permute-done.27 = bf16[4,96,768]{2,1,0:T(8,128)(2,1)S(1)} collective-permute-done((bf16[4,96,768]{2,1,0:T(8,128)(2,1)S(1)}, bf16[4,96,768]{2,1,0:T(8,128)(2,1)S(1)}, u32[]{:S(2)}, u32[]{:S(2)}) %collective-permute-start.27) | collective-permute-done | bytes 589856 | tf_op jit(solution)/shard_map/ppermute | solution.py:667
  350.2 6.2 %collective-permute-done.31 = bf16[4,96,896]{2,1,0:T(8,128)(2,1)S(1)} collective-permute-done((bf16[4,96,896]{2,1,0:T(8,128)(2,1)S(1)}, bf16[4,96,896]{2,1,0:T(8,128)(2,1)S(1)}, u32[]{:S(2)}, u32[]{:S(2)}) %collective-permute-start.31) | collective-permute-done | bytes 688160 | tf_op jit(solution)/shard_map/ppermute | solution.py:667
  363.2 2.3 collective-permute-done.34
  367.0 5.0 %collective-permute-done.38 = bf16[96,768]{1,0:T(8,128)(2,1)S(1)} collective-permute-done((bf16[96,768]{1,0:T(8,128)(2,1)S(1)}, bf16[96,768]{1,0:T(8,128)(2,1)S(1)}, u32[]{:S(2)}, u32[]{:S(2)}) %collective-permute-start.38) | collective-permute-done | bytes 147488 | tf_op jit(solution)/shard_map/ppermute | solution.py:667
  373.5 2.3 collective-permute-start.42
  384.7 2.4 finish_tokens.1
  393.2 3.0 collective-permute-done.43.other_ref
  (275 shorter events, 112.1 us)
Async XLA Ops:
  7.2 128.2 %all-gather.3.cloned.1.call-start = ((), (), s32[]{:S(2)}) async-start(), calls=%async_computation.2 | async-start | bytes 4915200 | tf_op jit(solution)/shard_map/all_gather | solution.py:1125
  11.7 46.2 %collective-permute-start.3 = (bf16[2,192,896]{2,1,0:T(8,128)(2,1)S(1)}, bf16[2,192,896]{2,1,0:T(8,128)(2,1)S(1)}, u32[]{:S(2)}, u32[]{:S(2)}) collective-permute-start(bf16[2,192,896]{2,1,0:T(8,128)(2,1)S(1)} %get-tuple-element.96), channel_id=1, source_target_pairs={{0,2},{1,3},{2,0},{3,1},{4,6},{5,7},{6,4},{7,5},{8,10},{9,11},{10,... | collective-permute-start | bytes 2064392 | tf_op jit(solution)/shard_map/ppermute | solution.py:667
  14.8 15.5 %collective-permute-start.2 = (bf16[304,768]{1,0:T(8,128)(2,1)S(1)}, bf16[304,768]{1,0:T(8,128)(2,1)S(1)}, u32[]{:S(2)}, u32[]{:S(2)}) collective-permute-start(bf16[304,768]{1,0:T(8,128)(2,1)S(1)} %pack_weights.1), channel_id=1, source_target_pairs={{0,12},{4,8},{8,4},{12,0},{1,13},{5,9},{9,5},{13,1},{2,14},{6,10},... | collective-permute-start | bytes 1400840 | tf_op jit(solution)/shard_map/ppermute | solution.py:667
  18.4 39.6 %collective-permute-start.1 = (bf16[304,768]{1,0:T(8,128)(2,1)S(1)}, bf16[304,768]{1,0:T(8,128)(2,1)S(1)}, u32[]{:S(2)}, u32[]{:S(2)}) collective-permute-start(bf16[304,768]{1,0:T(8,128)(2,1)S(1)} %pack_weights.1), channel_id=1, source_target_pairs={{0,8},{4,12},{8,0},{12,4},{1,9},{5,13},{9,1},{13,5},{2,10},{6,14},... | collective-permute-start | bytes 1400840 | tf_op jit(solution)/shard_map/ppermute | solution.py:667
  18.4 39.6 %collective-permute-start = (bf16[304,768]{1,0:T(8,128)(2,1)S(1)}, bf16[304,768]{1,0:T(8,128)(2,1)S(1)}, u32[]{:S(2)}, u32[]{:S(2)}) collective-permute-start(bf16[304,768]{1,0:T(8,128)(2,1)S(1)} %pack_weights.1), channel_id=1, source_target_pairs={{0,4},{4,0},{8,12},{12,8},{1,5},{5,1},{9,13},{13,9},{2,6},{6,2},{1... | collective-permute-start | bytes 1400840 | tf_op jit(solution)/shard_map/ppermute | solution.py:667
  59.6 323.0 %reduce-scatter.2.cloned.1.call-start = ((), (), s32[]{:S(2)}) async-start(), calls=%async_computation.1 | async-start | bytes 5160960 | tf_op jit(solution)/shard_map/reduce_scatter | solution.py:1166
  60.8 14.4 %collective-permute-start.5 = (bf16[1,4,96,768]{3,2,1,0:T(8,128)(2,1)S(1)}, bf16[1,4,96,768]{3,2,1,0:T(8,128)(2,1)S(1)}, u32[]{:S(2)}, u32[]{:S(2)}) collective-permute-start(bf16[1,4,96,768]{3,2,1,0:T(8,128)(2,1)S(1)} %get-tuple-element.227), channel_id=1, source_target_pairs={{0,2},{1,3},{2,0},{3,1},{4,6},{5,7},{6,4},{7,5},{8,10},{9,11},{10,... | collective-permute-start | bytes 1769480 | tf_op jit(solution)/shard_map/ppermute | solution.py:667
  61.3 15.3 %collective-permute-start.4 = (bf16[1,4,96,768]{3,2,1,0:T(8,128)(2,1)S(1)}, bf16[1,4,96,768]{3,2,1,0:T(8,128)(2,1)S(1)}, u32[]{:S(2)}, u32[]{:S(2)}) collective-permute-start(bf16[1,4,96,768]{3,2,1,0:T(8,128)(2,1)S(1)} %get-tuple-element.227), channel_id=1, source_target_pairs={{0,16},{16,0},{1,17},{17,1},{2,18},{18,2},{3,19},{19,3},{4,20},{20... | collective-permute-start | bytes 1769480 | tf_op jit(solution)/shard_map/ppermute | solution.py:667
  75.2 13.5 %collective-permute-start.6 = (bf16[1,4,96,768]{3,2,1,0:T(8,128)(2,1)S(1)}, bf16[1,4,96,768]{3,2,1,0:T(8,128)(2,1)S(1)}, u32[]{:S(2)}, u32[]{:S(2)}) collective-permute-start(bf16[1,4,96,768]{3,2,1,0:T(8,128)(2,1)S(1)} %collective-permute-done.5), channel_id=1, source_target_pairs={{0,16},{16,0},{1,17},{17,1},{2,18},{18,2},{3,19},{19,3},{4,20},{20... | collective-permute-start | bytes 1769480 | tf_op jit(solution)/shard_map/ppermute | solution.py:667
  92.2 27.0 %collective-permute-start.9 = (bf16[2,4,96,768]{3,2,0,1:T(8,128)(2,1)}, bf16[2,4,96,768]{3,2,0,1:T(8,128)(2,1)}, u32[]{:S(2)}, u32[]{:S(2)}) collective-permute-start(bf16[2,4,96,768]{3,2,0,1:T(8,128)(2,1)} %pad_maximum_fusion.3), channel_id=1, source_target_pairs={{0,2},{1,3},{2,0},{3,1},{4,6},{5,7},{6,4},{7,5},{8,10},{9,11},{10,... | collective-permute-start | bytes 3538952 | tf_op jit(solution)/shard_map/ppermute | solution.py:667
  93.2 45.8 %collective-permute-start.12 = (bf16[2,4,96,768]{3,2,0,1:T(8,128)(2,1)}, bf16[2,4,96,768]{3,2,0,1:T(8,128)(2,1)}, u32[]{:S(2)}, u32[]{:S(2)}) collective-permute-start(bf16[2,4,96,768]{3,2,0,1:T(8,128)(2,1)} %pad_maximum_fusion.3), channel_id=1, source_target_pairs={{0,16},{16,0},{1,17},{17,1},{2,18},{18,2},{3,19},{19,3},{4,20},{20... | collective-permute-start | bytes 3538952 | tf_op jit(solution)/shard_map/ppermute | solution.py:667
  119.2 28.0 %collective-permute-start.13 = (bf16[2,4,96,768]{3,2,0,1:T(8,128)(2,1)}, bf16[2,4,96,768]{3,2,0,1:T(8,128)(2,1)}, u32[]{:S(2)}, u32[]{:S(2)}) collective-permute-start(bf16[2,4,96,768]{3,2,0,1:T(8,128)(2,1)} %collective-permute-done.9), channel_id=1, source_target_pairs={{0,16},{16,0},{1,17},{17,1},{2,18},{18,2},{3,19},{19,3},{4,20},{20... | collective-permute-start | bytes 3538952 | tf_op jit(solution)/shard_map/ppermute | solution.py:667
  137.4 15.1 %collective-permute-start.11 = (bf16[2,192,768]{2,1,0:T(8,128)(2,1)S(1)}, bf16[2,192,768]{2,1,0:T(8,128)(2,1)S(1)}, u32[]{:S(2)}, u32[]{:S(2)}) collective-permute-start(bf16[2,192,768]{2,1,0:T(8,128)(2,1)S(1)} %get-tuple-element.112), channel_id=1, source_target_pairs={{0,2},{1,3},{2,0},{3,1},{4,6},{5,7},{6,4},{7,5},{8,10},{9,11},{10,... | collective-permute-start | bytes 1769480 | tf_op jit(solution)/shard_map/ppermute | solution.py:667
  153.6 23.8 %collective-permute-start.15 = (bf16[2,192,640]{2,1,0:T(8,128)(2,1)}, bf16[2,192,640]{2,1,0:T(8,128)(2,1)S(1)}, u32[]{:S(2)}, u32[]{:S(2)}) collective-permute-start(bf16[2,192,640]{2,1,0:T(8,128)(2,1)} %pad_maximum_fusion.11), channel_id=1, source_target_pairs={{0,1},{1,0},{2,3},{3,2},{4,5},{5,4},{6,7},{7,6},{8,9},{9,8},{10,11... | collective-permute-start | bytes 1474568 | tf_op jit(solution)/shard_map/ppermute | solution.py:667
  154.1 23.3 %collective-permute-start.16 = (bf16[2,4,384,768]{3,2,1,0:T(8,128)(2,1)}, bf16[2,4,384,768]{3,2,1,0:T(8,128)(2,1)S(1)}, u32[]{:S(2)}, u32[]{:S(2)}) collective-permute-start(bf16[2,4,384,768]{3,2,1,0:T(8,128)(2,1)} %bitcast.231), channel_id=1, source_target_pairs={{0,1},{1,0},{2,3},{3,2},{4,5},{5,4},{6,7},{7,6},{8,9},{9,8},{10,11... | collective-permute-start | bytes 14155784 | tf_op jit(solution)/shard_map/ppermute | solution.py:667
  245.7 17.5 %collective-permute-start.18 = (bf16[2,192,896]{2,1,0:T(8,128)(2,1)S(1)}, bf16[2,192,896]{2,1,0:T(8,128)(2,1)S(1)}, u32[]{:S(2)}, u32[]{:S(2)}) collective-permute-start(bf16[2,192,896]{2,1,0:T(8,128)(2,1)S(1)} %get-tuple-element.128), channel_id=1, source_target_pairs={{0,2},{1,3},{2,0},{3,1},{4,6},{5,7},{6,4},{7,5},{8,10},{9,11},{10,... | collective-permute-start | bytes 2064392 | tf_op jit(solution)/shard_map/ppermute | solution.py:667
  263.5 12.5 %collective-permute-start.21 = (bf16[4,384,768]{2,1,0:T(8,128)(2,1)}, bf16[4,384,768]{2,1,0:T(8,128)(2,1)}, u32[]{:S(2)}, u32[]{:S(2)}) collective-permute-start(bf16[4,384,768]{2,1,0:T(8,128)(2,1)} %get-tuple-element.137), channel_id=1, source_target_pairs={{0,1},{1,0},{2,3},{3,2},{4,5},{5,4},{6,7},{7,6},{8,9},{9,8},{10,11... | collective-permute-start | bytes 7077896 | tf_op jit(solution)/shard_map/ppermute | solution.py:667
  264.0 85.2 %collective-permute-start.17 = (bf16[2,192,640]{2,1,0:T(8,128)(2,1)}, bf16[2,192,640]{2,1,0:T(8,128)(2,1)}, u32[]{:S(2)}, u32[]{:S(2)}) collective-permute-start(bf16[2,192,640]{2,1,0:T(8,128)(2,1)} %get-tuple-element.122), channel_id=1, source_target_pairs={{0,2},{1,3},{2,0},{3,1},{4,6},{5,7},{6,4},{7,5},{8,10},{9,11},{10,... | collective-permute-start | bytes 1474568 | tf_op jit(solution)/shard_map/ppermute | solution.py:667
  274.5 33.5 %collective-permute-start.24 = (bf16[4,2,96,768]{3,2,0,1:T(8,128)(2,1)S(1)}, bf16[4,2,96,768]{3,2,0,1:T(8,128)(2,1)}, u32[]{:S(2)}, u32[]{:S(2)}) collective-permute-start(bf16[4,2,96,768]{3,2,0,1:T(8,128)(2,1)S(1)} %fusion.2), channel_id=1, source_target_pairs={{0,16},{16,0},{1,17},{17,1},{2,18},{18,2},{3,19},{19,3},{4,20},{20... | collective-permute-start | bytes 3538952 | tf_op jit(solution)/shard_map/ppermute | solution.py:667
  277.7 28.0 %collective-permute-start.23 = (bf16[4,2,96,768]{3,2,0,1:T(8,128)(2,1)S(1)}, bf16[4,2,96,768]{3,2,0,1:T(8,128)(2,1)}, u32[]{:S(2)}, u32[]{:S(2)}) collective-permute-start(bf16[4,2,96,768]{3,2,0,1:T(8,128)(2,1)S(1)} %fusion.3), channel_id=1, source_target_pairs={{0,2},{1,3},{2,0},{3,1},{4,6},{5,7},{6,4},{7,5},{8,10},{9,11},{10,... | collective-permute-start | bytes 3538952 | tf_op jit(solution)/shard_map/ppermute | solution.py:667
  303.3 72.5 %collective-permute-start.30 = (bf16[2,192,768]{2,1,0:T(8,128)(2,1)}, bf16[2,192,768]{2,1,0:T(8,128)(2,1)S(1)}, u32[]{:S(2)}, u32[]{:S(2)}) collective-permute-start(bf16[2,192,768]{2,1,0:T(8,128)(2,1)} %get-tuple-element.150), channel_id=1, source_target_pairs={{0,2},{1,3},{2,0},{3,1},{4,6},{5,7},{6,4},{7,5},{8,10},{9,11},{10,... | collective-permute-start | bytes 1769480 | tf_op jit(solution)/shard_map/ppermute | solution.py:667
  304.1 22.9 %collective-permute-start.25 = (bf16[2,96,896]{2,1,0:T(8,128)(2,1)S(1)}, bf16[2,96,896]{2,1,0:T(8,128)(2,1)S(1)}, u32[]{:S(2)}, u32[]{:S(2)}) collective-permute-start(bf16[2,96,896]{2,1,0:T(8,128)(2,1)S(1)} %get-tuple-element.214), channel_id=1, source_target_pairs={{0,2},{1,3},{2,0},{3,1},{4,6},{5,7},{6,4},{7,5},{8,10},{9,11},{10,... | collective-permute-start | bytes 1032200 | tf_op jit(solution)/shard_map/ppermute | solution.py:667
  305.7 22.1 %collective-permute-start.26 = (bf16[2,96,896]{2,1,0:T(8,128)(2,1)S(1)}, bf16[2,96,896]{2,1,0:T(8,128)(2,1)S(1)}, u32[]{:S(2)}, u32[]{:S(2)}) collective-permute-start(bf16[2,96,896]{2,1,0:T(8,128)(2,1)S(1)} %get-tuple-element.215), channel_id=1, source_target_pairs={{0,16},{16,0},{1,17},{17,1},{2,18},{18,2},{3,19},{19,3},{4,20},{20... | collective-permute-start | bytes 1032200 | tf_op jit(solution)/shard_map/ppermute | solution.py:667
  309.5 36.0 %collective-permute-start.28 = (bf16[4,96,768]{2,1,0:T(8,128)(2,1)S(1)}, bf16[4,96,768]{2,1,0:T(8,128)(2,1)S(1)}, u32[]{:S(2)}, u32[]{:S(2)}) collective-permute-start(bf16[4,96,768]{2,1,0:T(8,128)(2,1)S(1)} %fusion.8), channel_id=1, source_target_pairs={{0,2},{1,3},{2,0},{3,1},{4,6},{5,7},{6,4},{7,5},{8,10},{9,11},{10,... | collective-permute-start | bytes 1769480 | tf_op jit(solution)/shard_map/ppermute | solution.py:667
  327.0 16.3 %collective-permute-start.27 = (bf16[4,96,768]{2,1,0:T(8,128)(2,1)S(1)}, bf16[4,96,768]{2,1,0:T(8,128)(2,1)S(1)}, u32[]{:S(2)}, u32[]{:S(2)}) collective-permute-start(bf16[4,96,768]{2,1,0:T(8,128)(2,1)S(1)} %fusion.9), channel_id=1, source_target_pairs={{0,16},{16,0},{1,17},{17,1},{2,18},{18,2},{3,19},{19,3},{4,20},{20... | collective-permute-start | bytes 1769480 | tf_op jit(solution)/shard_map/ppermute | solution.py:667
  327.8 28.6 %collective-permute-start.31 = (bf16[4,96,896]{2,1,0:T(8,128)(2,1)S(1)}, bf16[4,96,896]{2,1,0:T(8,128)(2,1)S(1)}, u32[]{:S(2)}, u32[]{:S(2)}) collective-permute-start(bf16[4,96,896]{2,1,0:T(8,128)(2,1)S(1)} %pad_maximum_fusion.6), channel_id=1, source_target_pairs={{0,16},{16,0},{1,17},{17,1},{2,18},{18,2},{3,19},{19,3},{4,20},{20... | collective-permute-start | bytes 2064392 | tf_op jit(solution)/shard_map/ppermute | solution.py:667
  343.3 14.4 %collective-permute-start.32 = (bf16[4,96,896]{2,1,0:T(8,128)(2,1)S(1)}, bf16[4,96,896]{2,1,0:T(8,128)(2,1)S(1)}, u32[]{:S(2)}, u32[]{:S(2)}) collective-permute-start(bf16[4,96,896]{2,1,0:T(8,128)(2,1)S(1)} %pad_maximum_fusion.7), channel_id=1, source_target_pairs={{0,2},{1,3},{2,0},{3,1},{4,6},{5,7},{6,4},{7,5},{8,10},{9,11},{10,... | collective-permute-start | bytes 2064392 | tf_op jit(solution)/shard_map/ppermute | solution.py:667
  347.1 13.2 %collective-permute-start.36 = (bf16[96,768]{1,0:T(8,128)(2,1)S(1)}, bf16[96,768]{1,0:T(8,128)(2,1)S(1)}, u32[]{:S(2)}, u32[]{:S(2)}) collective-permute-start(bf16[96,768]{1,0:T(8,128)(2,1)S(1)} %get-tuple-element.218), channel_id=1, source_target_pairs={{0,12},{4,8},{8,4},{12,0},{1,13},{5,9},{9,5},{13,1},{2,14},{6,10},... | collective-permute-start | bytes 442376 | tf_op jit(solution)/shard_map/ppermute | solution.py:667
  365.5 13.3 %collective-permute-start.29 = (bf16[2,192,640]{2,1,0:T(8,128)(2,1)S(1)}, bf16[2,192,640]{2,1,0:T(8,128)(2,1)S(1)}, u32[]{:S(2)}, u32[]{:S(2)}) collective-permute-start(bf16[2,192,640]{2,1,0:T(8,128)(2,1)S(1)} %pad_maximum_fusion.12), channel_id=1, source_target_pairs={{0,1},{1,0},{2,3},{3,2},{4,5},{5,4},{6,7},{7,6},{8,9},{9,8},{10,11... | collective-permute-start | bytes 1474568 | tf_op jit(solution)/shard_map/ppermute | solution.py:667
  373.5 13.6 %collective-permute-start.42 = (bf16[96,896]{1,0:T(8,128)(2,1)}, bf16[96,896]{1,0:T(8,128)(2,1)}, u32[]{:S(2)}, u32[]{:S(2)}) collective-permute-start(bf16[96,896]{1,0:T(8,128)(2,1)} %get-tuple-element.210), channel_id=1, source_target_pairs={{0,12},{4,8},{8,4},{12,0},{1,13},{5,9},{9,5},{13,1},{2,14},{6,10},... | collective-permute-start | bytes 516104 | tf_op jit(solution)/shard_map/ppermute | solution.py:667
  375.8 13.4 %collective-permute-start.41 = (bf16[96,896]{1,0:T(8,128)(2,1)}, bf16[96,896]{1,0:T(8,128)(2,1)}, u32[]{:S(2)}, u32[]{:S(2)}) collective-permute-start(bf16[96,896]{1,0:T(8,128)(2,1)} %get-tuple-element.211), channel_id=1, source_target_pairs={{0,8},{4,12},{8,0},{12,4},{1,9},{5,13},{9,1},{13,5},{2,10},{6,14},... | collective-permute-start | bytes 516104 | tf_op jit(solution)/shard_map/ppermute | solution.py:667
  375.8 13.4 %collective-permute-start.40 = (bf16[96,896]{1,0:T(8,128)(2,1)}, bf16[96,896]{1,0:T(8,128)(2,1)}, u32[]{:S(2)}, u32[]{:S(2)}) collective-permute-start(bf16[96,896]{1,0:T(8,128)(2,1)} %get-tuple-element.212), channel_id=1, source_target_pairs={{0,4},{4,0},{8,12},{12,8},{1,5},{5,1},{9,13},{13,9},{2,6},{6,2},{1... | collective-permute-start | bytes 516104 | tf_op jit(solution)/shard_map/ppermute | solution.py:667
  (81 other events, 678.2 us)
Sparse Core Ops, SparseCore 0:
  59.7 75.6 all-gather.2
  269.5 74.3 reduce-scatter.1
